TPU v7x, 1024 devices: a whole 4x8x16 slice. The times are simulated.
1024 devices in a mesh: grp: 16 (over y, core), shard: 16 (over z), side: 4 (over x).
Axes of the slice: x: 4, y: 8, z: 16, core: 2. Of those that a mesh axis runs over, the one named last changes fastest.
Arguments:
- tokens: bfloat16 [4096, 4096], P(('grp', 'side')), may hold values from -6 to 6
- routes: int32 [4096, 8], P(('grp', 'side')), may hold values from 0 to 63, all different within a row; in each aligned block of 64 rows (0 to 63, 64 to 127, ...) at most 16 rows name the same one
- probs: float32 [4096, 8], P(('grp', 'side')), may hold values from 0.02 to 1
- w_gate: bfloat16 [256, 4096, 256], P(('grp', 'shard')), may hold values from -0.09375 to 0.09375
- w_up: bfloat16 [256, 4096, 256], P(('grp', 'shard')), may hold values from -0.09375 to 0.09375
- w_down: bfloat16 [256, 256, 4096], P(('grp', 'shard')), may hold values from -0.1875 to 0.1875
Outputs:
- mixed: bfloat16 [4096, 4096], P(('grp', 'side'), 'shard')
Inputs may be any that keep to these rules, and one draw needn't show every extreme that they name: `routes`: each token names 8 different experts. Within each aligned block of 64 tokens no expert is named by more than 16 tokens, a bound that some block reaches.
All inputs are finite; a program needn't handle non-finite values.
Results may differ from a plain program's by a relative error of at most 0.0057.
Values may be sent and summed in bfloat16 or wider, within the bound.
No kernel may reach another device: no remote copies, remote signals or barrier semaphores. Data moves between devices by JAX's collectives and lax.ppermute only.
A program may use at most 32 MiB of HBM per device.

v0:
```python
import jax
import jax.numpy as jnp
from jax import lax
from jax.sharding import PartitionSpec as P

TPE = 4


def tile_pass(rows, w_gate, w_up, w_down):
    flat = rows.reshape(-1, rows.shape[2])
    gate = jnp.dot(flat, w_gate[0], preferred_element_type=jnp.float32)
    upper = jnp.dot(flat, w_up[0], preferred_element_type=jnp.float32)
    hidden = (jax.nn.silu(gate) * upper).astype(jnp.bfloat16)
    result = jnp.dot(hidden, w_down[0], preferred_element_type=jnp.float32).astype(jnp.bfloat16)
    return result.reshape(rows.shape[0], rows.shape[1], -1)


def on_device(tokens, routes, probs, w_gate, w_up, w_down):
    groups = lax.axis_size("grp")
    shards = lax.axis_size("shard")
    per_group = shards // TPE
    experts_all = groups * per_group
    tok_count = tokens.shape[0]
    top_count = routes.shape[1]
    capacity = 2 * tok_count * top_count // experts_all
    local = lax.axis_index("shard") // TPE
    targets = jnp.arange(groups, dtype=jnp.int32) * per_group + local
    gates = probs / jnp.sum(probs, axis=-1, keepdims=True)
    match = routes[:, :, None] == targets[None, None, :]
    hits = jnp.sum(match.astype(jnp.int32), axis=1)
    gate_hits = jnp.sum(jnp.where(match, gates[:, :, None], jnp.float32(0.0)), axis=1)
    ranks = jnp.cumsum(hits, axis=0) - 1
    slots = jnp.arange(capacity, dtype=jnp.int32)
    select = ((hits.T[:, None, :] > 0) & (ranks.T[:, None, :] == slots[None, :, None])).astype(
        jnp.bfloat16
    )
    outgoing = jnp.einsum("gct,td->gcd", select, tokens, preferred_element_type=jnp.float32).astype(
        jnp.bfloat16
    )
    arrived = lax.all_to_all(outgoing, "grp", split_axis=0, concat_axis=0, tiled=True)
    results = tile_pass(arrived, w_gate, w_up, w_down)
    returned = lax.all_to_all(results, "grp", split_axis=0, concat_axis=0, tiled=True)

    def add_group(total, items):
        picks, rows_back, weight = items
        picked = jnp.einsum("ct,cd->td", picks, rows_back, preferred_element_type=jnp.float32)
        return (total + weight[:, None] * picked, None)

    start = jnp.zeros((tok_count, tokens.shape[1]), jnp.float32)
    combined, unused = lax.scan(add_group, start, (select, returned, gate_hits.T))
    return lax.psum_scatter(combined, "shard", scatter_dimension=1, tiled=True).astype(jnp.bfloat16)


def solution(mesh):
    return jax.shard_map(
        on_device,
        mesh=mesh,
        in_specs=(
            P(("grp", "side"), None),
            P(("grp", "side"), None),
            P(("grp", "side"), None),
            P(("grp", "shard"), None, None),
            P(("grp", "shard"), None, None),
            P(("grp", "shard"), None, None),
        ),
        out_specs=P(("grp", "side"), "shard"),
        check_vma=False,
    )
```

profile of v0, /device:TPU:6, one launch (start us, length us, event | category | flops | bytes accessed | tf_op | source)
XLA Modules:
  0.0 240.1 jit_solution(7993060290146220080)
XLA Ops:
  6.5 0.9 fusion.31
  7.5 0.1 copy.11
  7.6 0.1 reduce_window_sum.11
  7.7 0.1 copy.12
  7.7 1.7 convolution_convert_fusion.1
  9.5 56.8 %all_to_all.10 = bf16[16,16,4096]{2,1,0:T(8,128)(2,1)S(1)} all-to-all(bf16[16,16,4096]{2,1,0:T(8,128)(2,1)S(1)} %convolution_convert_fusion.1), channel_id=1, replica_groups=mesh['grp'=16,'shard'=16,'side'=4] {'grp'}, dimensions={0} | all-to-all | bytes 4194304 | tf_op jit(solution)/shard_map/all_to_all | solution.py:40
  66.3 1.3 copy-done.2
  67.6 0.7 fusion.10
  68.3 5.9 %convolution_convert_fusion = bf16[256,4096]{1,0:T(8,128)(2,1)} fusion(bf16[1,256,4096]{2,1,0:T(8,128)(2,1)S(1)} %copy-done, bf16[256,4096]{1,0:T(8,128)(2,1)} %bitcast.42, bf16[1,4096,256]{2,1,0:T(8,128)(2,1)} %param.12, f32[256,256]{1,0:T(8,128)S(1)} %fusion.10), kind=kOutput, calls=%fused_computation.9 | convolution fusion | flops 1075183616 | bytes 8650752 | tf_op jit(solution)/shard_map/dot_general | solution.py:14
  74.2 4.6 %all-to-all-start.1 = ((bf16[16,16,4096]{2,1,0:T(8,128)(2,1)}), bf16[16,16,4096]{2,1,0:T(8,128)(2,1)}, u32[]{:S(2)}, u32[]{:S(2)}) async-start(bf16[16,16,4096]{2,1,0:T(8,128)(2,1)} %bitcast.43), calls=%async_computation.1 | async-start | bytes 4194304 | tf_op jit(solution)/shard_map/all_to_all | solution.py:42
  78.9 0.1 fusion.30
  79.0 49.0 %all-to-all-done.1 = bf16[16,16,4096]{2,1,0:T(8,128)(2,1)} async-done(((bf16[16,16,4096]{2,1,0:T(8,128)(2,1)}), bf16[16,16,4096]{2,1,0:T(8,128)(2,1)}, u32[]{:S(2)}, u32[]{:S(2)}) %all-to-all-start.1) | async-done | bytes 2097184 | tf_op jit(solution)/shard_map/all_to_all | solution.py:42
  128.0 22.0 %while.11 = (s32[]{:T(128)}, f32[64,4096]{1,0:T(8,128)S(1)}, f32[16,64]{1,0:T(8,128)S(1)}, bf16[16,16,64]{2,1,0:T(8,128)(2,1)S(1)}, bf16[16,16,4096]{2,1,0:T(8,128)(2,1)}, /*index=5*/s32[]{:T(128)}, s32[]{:T(128)}) while((s32[]{:T(128)}, f32[64,4096]{1,0:T(8,128)S(1)}, f32[16,64]{1,0:T(8,128)S(1)}, ...), condition=%wide.region_5.6_spmd.clone, body=%wide.region_4.5_spmd.clone.sunk | while | flops 9175043 | bytes 2234459 | solution.py:50
  128.0 1.3 fusion.44
  129.4 1.3 fusion.44
  130.8 1.3 fusion.44
  132.2 1.3 fusion.44
  133.5 1.3 fusion.44
  134.9 1.3 fusion.44
  136.3 1.3 fusion.44
  137.7 1.3 fusion.44
  139.0 1.3 fusion.44
  140.4 1.3 fusion.44
  141.8 1.3 fusion.44
  143.2 1.3 fusion.44
  144.5 1.3 fusion.44
  145.9 1.3 fusion.44
  147.3 1.3 fusion.44
  148.7 1.3 fusion.44
  150.0 1.0 copy-done.1
  151.0 80.8 %reduce-scatter.2.cloned.1.call-done = f32[64,256]{1,0:T(8,128)} async-done(((f32[64,4096]{1,0:T(8,128)}), f32[64,256]{1,0:T(8,128)}) %reduce-scatter.2.cloned.1.call-update) | async-done | bytes 65552 | tf_op jit(solution)/shard_map/reduce_scatter | solution.py:51
  231.8 1.5 convert_element_type.23
  (35 shorter events, 0.3 us)
Async XLA Ops:
  6.5 61.8 %copy-start = (bf16[1,256,4096]{2,1,0:T(8,128)(2,1)S(1)}, bf16[1,256,4096]{2,1,0:T(8,128)(2,1)}, u32[]{:S(2)}) copy-start(bf16[1,256,4096]{2,1,0:T(8,128)(2,1)} %param.13) | copy-start | bytes 6291460
  9.5 58.1 %copy-start.3 = (bf16[1,4096,256]{2,1,0:T(8,128)(2,1)S(1)}, bf16[1,4096,256]{2,1,0:T(8,128)(2,1)}, u32[]{:S(2)}) copy-start(bf16[1,4096,256]{2,1,0:T(8,128)(2,1)} %param.11) | copy-start | bytes 6291460
  66.2 1.4 copy-start.2
  74.2 4.6 %copy-start.4 = (f32[64,8]{0,1:T(8,128)S(1)}, f32[64,8]{0,1:T(8,128)}, u32[]{:S(2)}) copy-start(f32[64,8]{0,1:T(8,128)} %param.10) | copy-start | bytes 6148
  74.2 4.7 %copy-start.5 = (s32[64,8]{0,1:T(8,128)S(1)}, s32[64,8]{0,1:T(8,128)}, u32[]{:S(2)}) copy-start(s32[64,8]{0,1:T(8,128)} %param.9) | copy-start | bytes 6148
  74.2 53.8 %all-to-all-start.1 = ((bf16[16,16,4096]{2,1,0:T(8,128)(2,1)}), bf16[16,16,4096]{2,1,0:T(8,128)(2,1)}, u32[]{:S(2)}, u32[]{:S(2)}) async-start(bf16[16,16,4096]{2,1,0:T(8,128)(2,1)} %bitcast.43), calls=%async_computation.1 | async-start | bytes 4194304 | tf_op jit(solution)/shard_map/all_to_all | solution.py:42
  78.8 153.0 %reduce-scatter.2.cloned.1.call-start = ((), (), s32[]{:S(2)}) async-start(), calls=%async_computation.3 | async-start | bytes 1114112 | tf_op jit(solution)/shard_map/reduce_scatter | solution.py:51
  150.0 1.0 copy-start.1
Sparse Core Ops, SparseCore 0:
  151.2 80.6 reduce-scatter.1
where the time goes:
time: 241 us; the launch traced here: 240 us
  waiting for transfers between devices  130 us (54%)
  blocking collectives  56.8 us (24%)
  matrix products  29.6 us (12%)
  between operations  13.5 us (6%)
  starting transfers between devices  4.6 us (2%)
  local copies, waits for them, and re-layouts  2.65 us (1%)
  other arithmetic  2.63 us (1%)
    reduce_scatter x1, waiting for transfers between devices, on_device(): lax.psum_scatter(combined, 'shard', scatter_dimension=1, tiled=True)  80.8 us
    all_to_all x1, blocking collectives, on_device(): lax.all_to_all(outgoing, 'grp', split_axis=0, concat_axis=0, tiled=True)  56.8 us
    all_to_all x1, waiting for transfers between devices, on_device(): lax.all_to_all(results, 'grp', split_axis=0, concat_axis=0, tiled=True)  49 us
    dot_general x16, matrix products, add_group(): jnp.einsum('ct,cd->td', picks, rows_back, preferred_element_type=jnp.floa...  21.3 us
    dot_general x1, matrix products, tile_pass(): jnp.dot(hidden, w_down[0], preferred_element_type=jnp.float32)  5.89 us
  transfers between devices with their start and end apart: 2, of which 2 were waited for; matrix products, arithmetic and copies ran while one was open for 0% of the time, Pallas kernels for 0%

commit v1 on v0

v1 whole, which is shorter than its diff:
```python
import jax
import jax.numpy as jnp
from jax import lax
from jax.sharding import PartitionSpec as P

TPE = 4


def tile_pass(rows, w_gate, w_up, w_down):
    gate = jnp.dot(rows, w_gate[0], preferred_element_type=jnp.float32)
    upper = jnp.dot(rows, w_up[0], preferred_element_type=jnp.float32)
    hidden = (jax.nn.silu(gate) * upper).astype(jnp.bfloat16)
    return jnp.dot(hidden, w_down[0], preferred_element_type=jnp.float32).astype(jnp.bfloat16)


def on_device(tokens, routes, probs, w_gate, w_up, w_down):
    groups = lax.axis_size("grp")
    shards = lax.axis_size("shard")
    per_group = shards // TPE
    experts_all = groups * per_group
    tok_count, width = tokens.shape
    top_count = routes.shape[1]
    capacity = 2 * tok_count * top_count // experts_all
    local = lax.axis_index("shard") // TPE
    targets = jnp.arange(groups, dtype=jnp.int32) * per_group + local
    gates = probs / jnp.sum(probs, axis=-1, keepdims=True)
    match = routes[:, :, None] == targets[None, None, :]
    hits = jnp.any(match, axis=1)
    gate_hits = jnp.sum(jnp.where(match, gates[:, :, None], jnp.float32(0.0)), axis=1)
    before = jnp.tril(jnp.ones((tok_count, tok_count), jnp.bfloat16), -1)
    ranks = jnp.dot(before, hits.astype(jnp.bfloat16), preferred_element_type=jnp.float32)
    slots = jnp.arange(capacity, dtype=jnp.int32)
    ranks = ranks.astype(jnp.int32)
    chosen = hits[:, :, None] & (ranks[:, :, None] == slots[None, None, :])
    select = chosen.astype(jnp.bfloat16).reshape(tok_count, groups * capacity)
    weight = jnp.where(chosen, gate_hits[:, :, None], jnp.float32(0.0))
    weight = weight.reshape(tok_count, groups * capacity)
    high = weight.astype(jnp.bfloat16)
    low = (weight - high.astype(jnp.float32)).astype(jnp.bfloat16)
    outgoing = lax.dot_general(
        select, tokens, (((0,), (0,)), ((), ())), preferred_element_type=jnp.float32
    ).astype(jnp.bfloat16)
    arrived = lax.all_to_all(outgoing, "grp", split_axis=0, concat_axis=0, tiled=True)
    results = tile_pass(arrived, w_gate, w_up, w_down)
    returned = lax.all_to_all(results, "grp", split_axis=0, concat_axis=0, tiled=True)
    both = jnp.concatenate([high, low], axis=0)
    mixed = jnp.dot(both, returned, preferred_element_type=jnp.float32)
    combined = (mixed[:tok_count] + mixed[tok_count:]).astype(jnp.bfloat16)
    pieces = combined.reshape(tok_count, shards, width // shards).transpose(1, 0, 2)
    pieces = lax.all_to_all(pieces, "shard", split_axis=0, concat_axis=0, tiled=True)
    return jnp.sum(pieces.astype(jnp.float32), axis=0).astype(jnp.bfloat16)


def solution(mesh):
    return jax.shard_map(
        on_device,
        mesh=mesh,
        in_specs=(
            P(("grp", "side"), None),
            P(("grp", "side"), None),
            P(("grp", "side"), None),
            P(("grp", "shard"), None, None),
            P(("grp", "shard"), None, None),
            P(("grp", "shard"), None, None),
        ),
        out_specs=P(("grp", "side"), "shard"),
        check_vma=False,
    )
```

time: 241 us -> 173 us (0.72)
  waiting for transfers between devices: 130 us -> 48.9 us
  blocking collectives: 56.8 us -> 105 us
  matrix products: 29.6 us -> 10.7 us
  between operations: 13.5 us -> 0.12 us
    reduce_scatter x1 -> x0, waiting for transfers between devices: 80.8 us -> none  [on_device(): lax.psum_scatter(combined, 'shard', scatter_dimension=1, tiled=True)]
    all_to_all x0 -> x1, blocking collectives: none -> 47.8 us  [on_device(): lax.all_to_all(pieces, 'shard', split_axis=0, concat_axis=0, tiled=True)]
    dot_general x18 -> x4, matrix products: 23.7 us -> 4.76 us  [the longest x1 2.14 us: on_device(): mixed = jnp.dot(both, returned, preferred_element_type=jnp.float32)]
  transfers between devices with their start and end apart: 2 -> 1, of which waited for: 2 -> 1; matrix products, arithmetic and copies ran while one was open for 0% -> 0% of each run, Pallas kernels for 0% -> 0%
where the time goes in v1:
time: 173 us; the launch traced here: 172 us
  blocking collectives  105 us (61%)
  waiting for transfers between devices  48.9 us (28%)
  matrix products  10.7 us (6%)
  starting transfers between devices  4.57 us (3%)
  other arithmetic  2.13 us (1%)
    all_to_all x1, blocking collectives, on_device(): lax.all_to_all(outgoing, 'grp', split_axis=0, concat_axis=0, tiled=True)  56.8 us
    all_to_all x1, waiting for transfers between devices, on_device(): lax.all_to_all(results, 'grp', split_axis=0, concat_axis=0, tiled=True)  48.9 us
    all_to_all x1, blocking collectives, on_device(): lax.all_to_all(pieces, 'shard', split_axis=0, concat_axis=0, tiled=True)  47.8 us
    dot_general x1, matrix products, tile_pass(): jnp.dot(hidden, w_down[0], preferred_element_type=jnp.float32)  5.95 us
    all_to_all x1, starting transfers between devices, on_device(): lax.all_to_all(results, 'grp', split_axis=0, concat_axis=0, tiled=True)  4.57 us
  transfers between devices with their start and end apart: 1, of which 1 were waited for; matrix products, arithmetic and copies ran while one was open for 0% of the time, Pallas kernels for 0%

profile of v1, /device:TPU:6, one launch (start us, length us, event | category | flops | bytes accessed | tf_op | source)
XLA Modules:
  0.0 172.4 jit_solution(17324062609258718513)
XLA Ops:
  0.0 0.0 copy-start
  0.0 0.1 eq.40
  0.1 0.9 compare_reduce_fusion
  1.0 0.2 convolution_convert_fusion.2
  1.2 0.1 fusion.23
  1.3 1.7 %convolution_convert_fusion.1 = bf16[256,4096]{1,0:T(8,128)(2,1)S(1)} fusion(pred[64,256]{0,1:T(32,128)(4,1)S(1)} %fusion.23, bf16[64,4096]{1,0:T(8,128)(2,1)} %param.6), kind=kOutput, calls=%fused_computation.1 | convolution fusion | flops 135266304 | bytes 2637824 | tf_op jit(solution)/shard_map/dot_general | solution.py:40
  3.1 0.0 copy-start.2
  3.1 56.8 %all_to_all.29 = bf16[16,16,4096]{2,1,0:T(8,128)(2,1)S(1)} all-to-all(bf16[16,16,4096]{2,1,0:T(8,128)(2,1)S(1)} %bitcast.58), channel_id=1, replica_groups=mesh['grp'=16,'shard'=16,'side'=4] {'grp'}, dimensions={0} | all-to-all | bytes 4194304 | tf_op jit(solution)/shard_map/all_to_all | solution.py:43
  59.9 0.0 copy-start.1
  59.9 1.3 copy-done.1
  61.1 0.0 copy-done.2
  61.2 0.7 fusion.3
  61.9 0.0 copy-done
  61.9 5.9 %convolution_convert_fusion = bf16[256,4096]{1,0:T(8,128)(2,1)} fusion(bf16[1,256,4096]{2,1,0:T(8,128)(2,1)S(1)} %copy-done, bf16[256,4096]{1,0:T(8,128)(2,1)} %bitcast.57, bf16[1,4096,256]{2,1,0:T(8,128)(2,1)} %param.10, f32[256,256]{1,0:T(8,128)S(1)} %fusion.3), kind=kOutput, calls=%fused_computation | convolution fusion | flops 1075183616 | bytes 8650752 | tf_op jit(solution)/shard_map/dot_general | solution.py:13
  67.8 0.0 copy-start.3
  67.8 0.0 copy-start.4
  67.8 4.6 %all-to-all-start.1 = ((bf16[16,16,4096]{2,1,0:T(8,128)(2,1)}), bf16[16,16,4096]{2,1,0:T(8,128)(2,1)}, u32[]{:S(2)}, u32[]{:S(2)}) async-start(bf16[16,16,4096]{2,1,0:T(8,128)(2,1)} %bitcast.59), calls=%async_computation.1 | async-start | bytes 4194304 | tf_op jit(solution)/shard_map/all_to_all | solution.py:45
  72.4 0.0 copy-done.3
  72.4 0.0 copy-done.4
  72.5 0.1 fusion.24
  72.5 0.1 fusion.20
  72.7 0.1 fusion.21
  72.8 48.9 %all-to-all-done.1 = bf16[16,16,4096]{2,1,0:T(8,128)(2,1)} async-done(((bf16[16,16,4096]{2,1,0:T(8,128)(2,1)}), bf16[16,16,4096]{2,1,0:T(8,128)(2,1)}, u32[]{:S(2)}, u32[]{:S(2)}) %all-to-all-start.1) | async-done | bytes 2097184 | tf_op jit(solution)/shard_map/all_to_all | solution.py:45
  121.6 2.1 %fusion.25 = f32[128,4096]{1,0:T(8,128)S(1)} fusion(bf16[256,4096]{1,0:T(8,128)(2,1)} %bitcast.9, bf16[64,256]{0,1:T(8,128)(2,1)S(1)} %fusion.21, bf16[64,256]{0,1:T(8,128)(2,1)S(1)} %fusion.20), kind=kOutput, calls=%fused_computation.28 | convolution fusion | flops 268566528 | bytes 4259840 | tf_op jit(solution)/shard_map/dot_general | solution.py:47
  123.8 0.1 fusion.13
  123.9 47.8 %all_to_all.30 = bf16[16,64,256]{2,1,0:T(8,128)(2,1)S(1)} all-to-all(bf16[16,64,256]{2,1,0:T(8,128)(2,1)S(1)} %bitcast.61), channel_id=1, replica_groups=mesh['grp'=16,'shard'=16,'side'=4] {'shard'}, dimensions={0} | all-to-all | bytes 1048576 | tf_op jit(solution)/shard_map/all_to_all | solution.py:50
  171.7 0.7 reduce_sum.32
  (6 shorter events, 0.1 us)
Async XLA Ops:
  0.0 61.9 %copy-start = (bf16[1,256,4096]{2,1,0:T(8,128)(2,1)S(1)}, bf16[1,256,4096]{2,1,0:T(8,128)(2,1)}, u32[]{:S(2)}) copy-start(bf16[1,256,4096]{2,1,0:T(8,128)(2,1)} %param.11) | copy-start | bytes 6291460
  3.1 58.1 %copy-start.2 = (bf16[1,4096,256]{2,1,0:T(8,128)(2,1)S(1)}, bf16[1,4096,256]{2,1,0:T(8,128)(2,1)}, u32[]{:S(2)}) copy-start(bf16[1,4096,256]{2,1,0:T(8,128)(2,1)} %param.9) | copy-start | bytes 6291460
  59.9 1.3 copy-start.1
  67.8 4.6 %copy-start.3 = (f32[64,8]{0,1:T(8,128)S(1)}, f32[64,8]{0,1:T(8,128)}, u32[]{:S(2)}) copy-start(f32[64,8]{0,1:T(8,128)} %param.8) | copy-start | bytes 6148
  67.8 4.6 %copy-start.4 = (s32[64,8]{0,1:T(8,128)S(1)}, s32[64,8]{0,1:T(8,128)}, u32[]{:S(2)}) copy-start(s32[64,8]{0,1:T(8,128)} %param.7) | copy-start | bytes 6148
  67.8 53.8 %all-to-all-start.1 = ((bf16[16,16,4096]{2,1,0:T(8,128)(2,1)}), bf16[16,16,4096]{2,1,0:T(8,128)(2,1)}, u32[]{:S(2)}, u32[]{:S(2)}) async-start(bf16[16,16,4096]{2,1,0:T(8,128)(2,1)} %bitcast.59), calls=%async_computation.1 | async-start | bytes 4194304 | tf_op jit(solution)/shard_map/all_to_all | solution.py:45

commit v2 on v0

v2 whole, which is shorter than its diff:
```python
import functools

import jax
import jax.numpy as jnp
from jax import lax
from jax.experimental import pallas as pl
from jax.experimental.pallas import tpu as pltpu
from jax.sharding import PartitionSpec as P


TPE = 4
BF16 = jnp.bfloat16
F32 = jnp.float32


def dot(a, b, dims=((1,), (0,))):
    return lax.dot_general(a, b, (dims, ((), ())), preferred_element_type=F32)


def dispatch_kernel(cap, per_group, place, routes, probs, tokens, sent, high, low):
    rows, tok = high.shape
    row = lax.broadcasted_iota(jnp.int32, (rows, tok), 0)
    target = lax.shift_right_logical(row, cap.bit_length() - 1) * per_group + place[0]
    slot = lax.bitwise_and(row, cap - 1).astype(F32)
    gates = probs[...] / jnp.sum(probs[...], axis=0, keepdims=True)
    hits = jnp.zeros((rows, tok), F32)
    weight = jnp.zeros((rows, tok), F32)
    for k in range(routes.shape[0]):
        match = routes[k : k + 1, :] == target
        hits = jnp.where(match, F32(1.0), hits)
        weight = jnp.where(match, gates[k : k + 1, :], weight)
    before = lax.broadcasted_iota(jnp.int32, (tok, tok), 0)
    before = before < lax.broadcasted_iota(jnp.int32, (tok, tok), 1)
    ranks = dot(hits.astype(BF16), jnp.where(before, F32(1.0), F32(0.0)).astype(BF16))
    chosen = (hits > 0.5) & (ranks == slot)
    select = jnp.where(chosen, F32(1.0), F32(0.0)).astype(BF16)
    weight = jnp.where(chosen, weight, F32(0.0))
    top = weight.astype(BF16)
    high[...] = top
    low[...] = (weight - top.astype(F32)).astype(BF16)
    step = min(512, sent.shape[1])
    for at in range(0, sent.shape[1], step):
        sent[:, at : at + step] = dot(select, tokens[:, at : at + step]).astype(BF16)


def shuffle_kernel(block, place, weights, *outs):
    for k, out in enumerate(outs):
        owner = lax.bitwise_xor(place[1], k)
        for m in range(out.shape[1] // block):
            at = pl.multiple_of((m * TPE + owner) * block, block)
            out[:, m * block : (m + 1) * block] = weights[:, pl.ds(at, block)]


def hidden_kernel(rows, w_gate, w_up, out):
    gate = dot(rows[...], w_gate[...])
    upper = dot(rows[...], w_up[...])
    out[...] = (gate / (1.0 + jnp.exp(-gate)) * upper).astype(BF16)


def down_kernel(*refs):
    hidden, weights, out = refs[:TPE], refs[TPE : 2 * TPE], refs[-1]
    step = min(256, out.shape[1])
    for at in range(0, out.shape[1], step):
        total = dot(hidden[0][...], weights[0][:, at : at + step])
        for k in range(1, TPE):
            total = total + dot(hidden[k][...], weights[k][:, at : at + step])
        out[:, at : at + step] = total.astype(BF16)


def combine_kernel(place, high, low, rows, kept, *sent):
    block = kept.shape[1]
    for k in range(TPE):
        at = pl.multiple_of(lax.bitwise_xor(place[0], k) * block, block)
        piece = rows[:, pl.ds(at, block)]
        total = dot(high[...], piece, ((0,), (0,))) + dot(low[...], piece, ((0,), (0,)))
        if k == 0:
            kept[...] = total
        else:
            sent[k - 1][...] = total.astype(BF16)


def finish_kernel(kept, *refs):
    total = kept[...]
    for part in refs[:-1]:
        total = total + part[...].astype(F32)
    refs[-1][...] = total.astype(BF16)


def call(kernel, shapes, *args, flops=0):
    specs = [pl.BlockSpec(memory_space=pltpu.VMEM)] * len(args)
    if args[0].ndim == 1:
        specs[0] = pl.BlockSpec(memory_space=pltpu.SMEM)
    outs = [jax.ShapeDtypeStruct(s, d) for s, d in shapes]
    moved = sum(a.size * a.dtype.itemsize for a in (*args, *outs))
    return pl.pallas_call(
        kernel,
        out_shape=outs,
        in_specs=specs,
        out_specs=[pl.BlockSpec(memory_space=pltpu.VMEM)] * len(outs),
        compiler_params=pltpu.CompilerParams(vmem_limit_bytes=16 << 20),
        cost_estimate=pl.CostEstimate(flops=flops, bytes_accessed=moved, transcendentals=0),
    )(*args)


def on_device(tokens, routes, probs, w_gate, w_up, w_down):
    groups, shards = lax.axis_size("grp"), lax.axis_size("shard")
    per_group = shards // TPE
    tok, width = tokens.shape
    units = w_down.shape[1]
    block, quarter = width // shards, width // TPE
    cap = 2 * tok * routes.shape[1] // (groups * per_group)
    rows = groups * cap
    z = lax.axis_index("shard")
    place = jnp.stack([z // TPE, lax.rem(z, TPE)]).astype(jnp.int32)

    def over_y(x):
        x = lax.all_to_all(x.reshape(groups, cap, -1), "grp", 0, 0, tiled=True)
        return x.reshape(rows, -1)

    def swap(x, bits):
        return lax.ppermute(x, "shard", [(i, i ^ bits) for i in range(shards)])

    sent, high, low = call(
        functools.partial(dispatch_kernel, cap, per_group),
        [((rows, width), BF16), ((rows, tok), BF16), ((rows, tok), BF16)],
        place, routes.T, probs.T, tokens, flops=2 * rows * tok * width,
    )
    arrived = over_y(sent)
    parts = call(
        functools.partial(shuffle_kernel, block),
        [((units, quarter), BF16)] * TPE, place, w_down[0],
    )
    weights = [parts[0]] + [swap(parts[k], k) for k in range(1, TPE)]
    (hidden,) = call(
        hidden_kernel, [((rows, units), BF16)], arrived, w_gate[0], w_up[0],
        flops=4 * rows * width * units,
    )
    hiddens = [hidden] + [swap(hidden, k) for k in range(1, TPE)]
    (result,) = call(
        down_kernel, [((rows, quarter), BF16)], *hiddens, *weights,
        flops=2 * rows * width * units,
    )
    returned = over_y(result)
    kept, *halves = call(
        combine_kernel,
        [((tok, block), F32)] + [((tok, block), BF16)] * (TPE - 1),
        place, high, low, returned,
    )
    halves = [swap(h, TPE * (k + 1)) for k, h in enumerate(halves)]
    (mixed,) = call(finish_kernel, [((tok, block), BF16)], kept, *halves)
    return mixed


def solution(mesh):
    return jax.shard_map(
        on_device,
        mesh=mesh,
        in_specs=(
            P(("grp", "side"), None),
            P(("grp", "side"), None),
            P(("grp", "side"), None),
            P(("grp", "shard"), None, None),
            P(("grp", "shard"), None, None),
            P(("grp", "shard"), None, None),
        ),
        out_specs=P(("grp", "side"), "shard"),
        check_vma=False,
    )
```

time: 241 us -> 145 us (0.60)
  waiting for transfers between devices: 130 us -> 49.8 us
  starting transfers between devices: 4.6 us -> 56.9 us
  blocking collectives: 56.8 us -> 20.3 us
  matrix products: 29.6 us -> 0 us
  between operations: 13.5 us -> 0.17 us
  Pallas kernels: 0 us -> 7.94 us
  local copies, waits for them, and re-layouts: 2.65 us -> 8.51 us
  other arithmetic: 2.63 us -> 0.07 us
    reduce_scatter x1 -> x0, waiting for transfers between devices: 80.8 us -> none  [on_device(): lax.psum_scatter(combined, 'shard', scatter_dimension=1, tiled=True)]
    ppermute x0 -> x9, starting transfers between devices: none -> 49.7 us  [swap(): return lax.ppermute(x, 'shard', [(i, i ^ bits) for i in range(shards)])]
    all_to_all x1, blocking collectives: 56.8 us -> 20.3 us  [over_y(): x = lax.all_to_all(x.reshape(groups, cap, -1), 'grp', 0, 0, tiled=True)]
    dot_general x19 -> x0, matrix products: 29.6 us -> none  [the longest x16 21.3 us: add_group(): jnp.einsum('ct,cd->td', picks, rows_back, preferred_element_type=jnp.floa...]
    ppermute x0 -> x9, waiting for transfers between devices: none -> 16.4 us  [swap(): return lax.ppermute(x, 'shard', [(i, i ^ bits) for i in range(shards)])]
    all_to_all x1, waiting for transfers between devices: 49 us -> 33.4 us  [over_y(): x = lax.all_to_all(x.reshape(groups, cap, -1), 'grp', 0, 0, tiled=True)]
    pallas_call x0 -> x6, Pallas kernels: none -> 7.94 us  [call(): pl.pallas_call(kernel, out_shape=outs, in_specs=specs, out_specs=[pl.Bloc...]
    unnamed x12 -> x14, local copies, waits for them, and re-layouts: 2.35 us -> 8.51 us
  transfers between devices with their start and end apart: 2 -> 10, of which waited for: 2 -> 4; matrix products, arithmetic and copies ran while one was open for 0% -> 0% of each run, Pallas kernels for 0% -> 2%
where the time goes in v2:
time: 145 us; the launch traced here: 144 us
  starting transfers between devices  56.9 us (39%)
  waiting for transfers between devices  49.8 us (34%)
  blocking collectives  20.3 us (14%)
  local copies, waits for them, and re-layouts  8.51 us (6%)
  Pallas kernels  7.94 us (5%)
    ppermute x9, starting transfers between devices, swap(): return lax.ppermute(x, 'shard', [(i, i ^ bits) for i in range(shards)])  49.7 us
    all_to_all x1, waiting for transfers between devices, over_y(): x = lax.all_to_all(x.reshape(groups, cap, -1), 'grp', 0, 0, tiled=True)  33.4 us
    all_to_all x1, blocking collectives, over_y(): x = lax.all_to_all(x.reshape(groups, cap, -1), 'grp', 0, 0, tiled=True)  20.3 us
    ppermute x9, waiting for transfers between devices, swap(): return lax.ppermute(x, 'shard', [(i, i ^ bits) for i in range(shards)])  16.4 us
    unnamed x14, local copies, waits for them, and re-layouts  8.51 us
    pallas_call x6, Pallas kernels, call(): pl.pallas_call(kernel, out_shape=outs, in_specs=specs, out_specs=[pl.Bloc...  7.94 us
    all_to_all x1, starting transfers between devices, over_y(): x = lax.all_to_all(x.reshape(groups, cap, -1), 'grp', 0, 0, tiled=True)  7.2 us
  transfers between devices with their start and end apart: 10, of which 4 were waited for; matrix products, arithmetic and copies ran while one was open for 0% of the time, Pallas kernels for 2%

profile of v2, /device:TPU:6, one launch (start us, length us, event | category | flops | bytes accessed | tf_op | source)
XLA Modules:
  0.0 143.7 jit_solution(5659368352492400391)
XLA Ops:
  0.0 0.1 pad_add_fusion.place
  0.1 1.0 copy-done.4
  1.1 0.7 copy-done.5
  1.8 0.7 copy-done.6
  2.5 1.4 shard_map.64
  3.9 1.3 copy-done.3
  5.2 7.2 %all-to-all-start = ((bf16[16,16,4096]{2,1,0:T(8,128)(2,1)}), bf16[16,16,4096]{2,1,0:T(8,128)(2,1)S(1)}, u32[]{:S(2)}, u32[]{:S(2)}) async-start(bf16[16,16,4096]{2,1,0:T(8,128)(2,1)} %bitcast.15), calls=%async_computation | async-start | bytes 4194304 | tf_op jit(solution)/shard_map/all_to_all | solution.py:117
  12.4 0.0 copy-start.2
  12.4 1.6 %copy-done.2 = bf16[1,256,4096]{2,1,0:T(8,128)(2,1)S(1)} copy-done((bf16[1,256,4096]{2,1,0:T(8,128)(2,1)S(1)}, bf16[1,256,4096]{2,1,0:T(8,128)(2,1)}, u32[]{:S(2)}) %copy-start.2) | copy-done | bytes 2097176
  14.0 1.9 %shard_map.66 = (bf16[256,1024]{1,0:T(8,128)(2,1)S(1)}, bf16[256,1024]{1,0:T(8,128)(2,1)}, bf16[256,1024]{1,0:T(8,128)(2,1)}, bf16[256,1024]{1,0:T(8,128)(2,1)}) custom-call(s32[2]{0:T(128)S(1)} %pad_add_fusion.place, bf16[256,4096]{1,0:T(8,128)(2,1)S(1)} %bitcast.14), custom_call_target="tpu_custom_call" | custom-call | bytes 4194312 | tf_op jit(solution)/shard_map/pallas_call | solution.py:95
  15.9 4.3 %collective-permute-start.3 = (bf16[256,1024]{1,0:T(8,128)(2,1)}, bf16[256,1024]{1,0:T(8,128)(2,1)S(1)}, u32[]{:S(2)}, u32[]{:S(2)}) collective-permute-start(bf16[256,1024]{1,0:T(8,128)(2,1)} %get-tuple-element.20), channel_id=1, source_target_pairs={{0,4},{4,0},{8,12},{12,8},{16,20},{20,16},{24,28},{28,24},{32,36},... | collective-permute-start | bytes 1572872 | tf_op jit(solution)/shard_map/ppermute | solution.py:121
  20.2 6.1 %collective-permute-start.4 = (bf16[256,1024]{1,0:T(8,128)(2,1)}, bf16[256,1024]{1,0:T(8,128)(2,1)}, u32[]{:S(2)}, u32[]{:S(2)}) collective-permute-start(bf16[256,1024]{1,0:T(8,128)(2,1)} %get-tuple-element.21), channel_id=1, source_target_pairs={{0,8},{4,12},{8,0},{12,4},{16,24},{20,28},{24,16},{28,20},{32,40},... | collective-permute-start | bytes 1572872 | tf_op jit(solution)/shard_map/ppermute | solution.py:121
  26.3 1.9 %collective-permute-start.5 = (bf16[256,1024]{1,0:T(8,128)(2,1)}, bf16[256,1024]{1,0:T(8,128)(2,1)}, u32[]{:S(2)}, u32[]{:S(2)}) collective-permute-start(bf16[256,1024]{1,0:T(8,128)(2,1)} %get-tuple-element.22), channel_id=1, source_target_pairs={{0,12},{4,8},{8,4},{12,0},{16,28},{20,24},{24,20},{28,16},{32,44},... | collective-permute-start | bytes 1572872 | tf_op jit(solution)/shard_map/ppermute | solution.py:121
  28.2 33.4 %all-to-all-done = bf16[16,16,4096]{2,1,0:T(8,128)(2,1)S(1)} async-done(((bf16[16,16,4096]{2,1,0:T(8,128)(2,1)}), bf16[16,16,4096]{2,1,0:T(8,128)(2,1)S(1)}, u32[]{:S(2)}, u32[]{:S(2)}) %all-to-all-start) | async-done | bytes 2097184 | tf_op jit(solution)/shard_map/all_to_all | solution.py:117
  61.7 1.6 %copy-done = bf16[1,4096,256]{2,1,0:T(8,128)(2,1)S(1)} copy-done((bf16[1,4096,256]{2,1,0:T(8,128)(2,1)S(1)}, bf16[1,4096,256]{2,1,0:T(8,128)(2,1)}, u32[]{:S(2)}) %copy-start) | copy-done | bytes 2097176
  63.2 1.6 %copy-done.1 = bf16[1,4096,256]{2,1,0:T(8,128)(2,1)S(1)} copy-done((bf16[1,4096,256]{2,1,0:T(8,128)(2,1)S(1)}, bf16[1,4096,256]{2,1,0:T(8,128)(2,1)}, u32[]{:S(2)}) %copy-start.1) | copy-done | bytes 2097176
  64.8 1.3 shard_map.65.refs_0_
  66.1 4.3 %collective-permute-start = (bf16[256,256]{1,0:T(8,128)(2,1)S(1)}, bf16[256,256]{1,0:T(8,128)(2,1)S(1)}, u32[]{:S(2)}, u32[]{:S(2)}) collective-permute-start(bf16[256,256]{1,0:T(8,128)(2,1)S(1)} %shard_map.65.refs_0_), channel_id=1, source_target_pairs={{0,4},{4,0},{8,12},{12,8},{16,20},{20,16},{24,28},{28,24},{32,36},... | collective-permute-start | bytes 393224 | tf_op jit(solution)/shard_map/ppermute | solution.py:121
  70.4 6.1 %collective-permute-start.1 = (bf16[256,256]{1,0:T(8,128)(2,1)S(1)}, bf16[256,256]{1,0:T(8,128)(2,1)S(1)}, u32[]{:S(2)}, u32[]{:S(2)}) collective-permute-start(bf16[256,256]{1,0:T(8,128)(2,1)S(1)} %shard_map.65.refs_0_), channel_id=1, source_target_pairs={{0,8},{4,12},{8,0},{12,4},{16,24},{20,28},{24,16},{28,20},{32,40},... | collective-permute-start | bytes 393224 | tf_op jit(solution)/shard_map/ppermute | solution.py:121
  76.5 0.0 collective-permute-done.3.refs_5_
  76.5 1.9 %collective-permute-start.2 = (bf16[256,256]{1,0:T(8,128)(2,1)S(1)}, bf16[256,256]{1,0:T(8,128)(2,1)S(1)}, u32[]{:S(2)}, u32[]{:S(2)}) collective-permute-start(bf16[256,256]{1,0:T(8,128)(2,1)S(1)} %shard_map.65.refs_0_), channel_id=1, source_target_pairs={{0,12},{4,8},{8,4},{12,0},{16,28},{20,24},{24,20},{28,16},{32,44},... | collective-permute-start | bytes 393224 | tf_op jit(solution)/shard_map/ppermute | solution.py:121
  78.5 0.0 collective-permute-done.refs_1_
  78.5 7.7 %collective-permute-done.1.refs_2_ = bf16[256,256]{1,0:T(8,128)(2,1)S(1)} collective-permute-done((bf16[256,256]{1,0:T(8,128)(2,1)S(1)}, bf16[256,256]{1,0:T(8,128)(2,1)S(1)}, u32[]{:S(2)}, u32[]{:S(2)}) %collective-permute-start.1) | collective-permute-done | bytes 131104 | tf_op jit(solution)/shard_map/ppermute | solution.py:121
  86.1 1.9 %shard_map.67 = bf16[256,1024]{1,0:T(8,128)(2,1)S(1)} custom-call(bf16[256,256]{1,0:T(8,128)(2,1)S(1)} %shard_map.65.refs_0_, bf16[256,256]{1,0:T(8,128)(2,1)S(1)} %collective-permute-done.refs_1_, bf16[256,256]{1,0:T(8,128)(2,1)S(1)} %collective-permute-done.1.refs_2_, bf16[256,256]{1,0:T(8,128)(2,1)S(1)} %collective-permute-done.2.refs_3_, ...), custom_call_target="tpu_custom_call" | custom-call | flops 536870912 | bytes 3145728 | tf_op jit(solution)/shard_map/pallas_call | solution.py:95
  88.1 20.3 %all_to_all.10 = bf16[16,16,1024]{2,1,0:T(8,128)(2,1)S(1)} all-to-all(bf16[16,16,1024]{2,1,0:T(8,128)(2,1)S(1)} %bitcast.17), channel_id=1, replica_groups=mesh['grp'=16,'shard'=16,'side'=4] {'grp'}, dimensions={0} | all-to-all | bytes 1048576 | tf_op jit(solution)/shard_map/all_to_all | solution.py:117
  108.3 0.9 shard_map.68
  109.2 10.9 %collective-permute-start.6 = (bf16[64,256]{1,0:T(8,128)(2,1)S(1)}, bf16[64,256]{1,0:T(8,128)(2,1)S(1)}, u32[]{:S(2)}, u32[]{:S(2)}) collective-permute-start(bf16[64,256]{1,0:T(8,128)(2,1)S(1)} %get-tuple-element.24), channel_id=1, source_target_pairs={{0,16},{4,20},{8,24},{12,28},{16,0},{20,4},{24,8},{28,12},{32,48},... | collective-permute-start | bytes 98312 | tf_op jit(solution)/shard_map/ppermute | solution.py:121
  120.1 12.3 %collective-permute-start.7 = (bf16[64,256]{1,0:T(8,128)(2,1)S(1)}, bf16[64,256]{1,0:T(8,128)(2,1)S(1)}, u32[]{:S(2)}, u32[]{:S(2)}) collective-permute-start(bf16[64,256]{1,0:T(8,128)(2,1)S(1)} %get-tuple-element.25), channel_id=1, source_target_pairs={{0,32},{4,36},{8,40},{12,44},{16,48},{20,52},{24,56},{28,60},{32,0... | collective-permute-start | bytes 98312 | tf_op jit(solution)/shard_map/ppermute | solution.py:121
  132.5 1.9 %collective-permute-start.8 = (bf16[64,256]{1,0:T(8,128)(2,1)S(1)}, bf16[64,256]{1,0:T(8,128)(2,1)S(1)}, u32[]{:S(2)}, u32[]{:S(2)}) collective-permute-start(bf16[64,256]{1,0:T(8,128)(2,1)S(1)} %get-tuple-element.26), channel_id=1, source_target_pairs={{0,48},{4,52},{8,56},{12,60},{16,32},{20,36},{24,40},{28,44},{32,1... | collective-permute-start | bytes 98312 | tf_op jit(solution)/shard_map/ppermute | solution.py:121
  134.4 0.4 collective-permute-done.7.refs_1_
  134.8 8.3 %collective-permute-done.8.refs_2_ = bf16[64,256]{1,0:T(8,128)(2,1)S(1)} collective-permute-done((bf16[64,256]{1,0:T(8,128)(2,1)S(1)}, bf16[64,256]{1,0:T(8,128)(2,1)S(1)}, u32[]{:S(2)}, u32[]{:S(2)}) %collective-permute-start.8) | collective-permute-done | bytes 32800 | tf_op jit(solution)/shard_map/ppermute | solution.py:121
  143.1 0.6 shard_map.69
  (10 shorter events, 0.0 us)
Async XLA Ops:
  0.1 1.0 copy-start.4
  1.1 0.7 copy-start.5
  1.8 0.7 copy-start.6
  3.9 1.3 copy-start.3
  5.2 56.4 %all-to-all-start = ((bf16[16,16,4096]{2,1,0:T(8,128)(2,1)}), bf16[16,16,4096]{2,1,0:T(8,128)(2,1)S(1)}, u32[]{:S(2)}, u32[]{:S(2)}) async-start(bf16[16,16,4096]{2,1,0:T(8,128)(2,1)} %bitcast.15), calls=%async_computation | async-start | bytes 4194304 | tf_op jit(solution)/shard_map/all_to_all | solution.py:117
  12.4 1.6 %copy-start.2 = (bf16[1,256,4096]{2,1,0:T(8,128)(2,1)S(1)}, bf16[1,256,4096]{2,1,0:T(8,128)(2,1)}, u32[]{:S(2)}) copy-start(bf16[1,256,4096]{2,1,0:T(8,128)(2,1)} %param.11) | copy-start | bytes 6291460
  15.9 60.6 %collective-permute-start.3 = (bf16[256,1024]{1,0:T(8,128)(2,1)}, bf16[256,1024]{1,0:T(8,128)(2,1)S(1)}, u32[]{:S(2)}, u32[]{:S(2)}) collective-permute-start(bf16[256,1024]{1,0:T(8,128)(2,1)} %get-tuple-element.20), channel_id=1, source_target_pairs={{0,4},{4,0},{8,12},{12,8},{16,20},{20,16},{24,28},{28,24},{32,36},... | collective-permute-start | bytes 1572872 | tf_op jit(solution)/shard_map/ppermute | solution.py:121
  20.2 58.2 %collective-permute-start.4 = (bf16[256,1024]{1,0:T(8,128)(2,1)}, bf16[256,1024]{1,0:T(8,128)(2,1)}, u32[]{:S(2)}, u32[]{:S(2)}) collective-permute-start(bf16[256,1024]{1,0:T(8,128)(2,1)} %get-tuple-element.21), channel_id=1, source_target_pairs={{0,8},{4,12},{8,0},{12,4},{16,24},{20,28},{24,16},{28,20},{32,40},... | collective-permute-start | bytes 1572872 | tf_op jit(solution)/shard_map/ppermute | solution.py:121
  26.3 52.2 %collective-permute-start.5 = (bf16[256,1024]{1,0:T(8,128)(2,1)}, bf16[256,1024]{1,0:T(8,128)(2,1)}, u32[]{:S(2)}, u32[]{:S(2)}) collective-permute-start(bf16[256,1024]{1,0:T(8,128)(2,1)} %get-tuple-element.22), channel_id=1, source_target_pairs={{0,12},{4,8},{8,4},{12,0},{16,28},{20,24},{24,20},{28,16},{32,44},... | collective-permute-start | bytes 1572872 | tf_op jit(solution)/shard_map/ppermute | solution.py:121
  61.7 1.6 %copy-start = (bf16[1,4096,256]{2,1,0:T(8,128)(2,1)S(1)}, bf16[1,4096,256]{2,1,0:T(8,128)(2,1)}, u32[]{:S(2)}) copy-start(bf16[1,4096,256]{2,1,0:T(8,128)(2,1)} %param.9) | copy-start | bytes 6291460
  63.2 1.6 %copy-start.1 = (bf16[1,4096,256]{2,1,0:T(8,128)(2,1)S(1)}, bf16[1,4096,256]{2,1,0:T(8,128)(2,1)}, u32[]{:S(2)}) copy-start(bf16[1,4096,256]{2,1,0:T(8,128)(2,1)} %param.10) | copy-start | bytes 6291460
  66.1 12.3 %collective-permute-start = (bf16[256,256]{1,0:T(8,128)(2,1)S(1)}, bf16[256,256]{1,0:T(8,128)(2,1)S(1)}, u32[]{:S(2)}, u32[]{:S(2)}) collective-permute-start(bf16[256,256]{1,0:T(8,128)(2,1)S(1)} %shard_map.65.refs_0_), channel_id=1, source_target_pairs={{0,4},{4,0},{8,12},{12,8},{16,20},{20,16},{24,28},{28,24},{32,36},... | collective-permute-start | bytes 393224 | tf_op jit(solution)/shard_map/ppermute | solution.py:121
  70.4 15.7 %collective-permute-start.1 = (bf16[256,256]{1,0:T(8,128)(2,1)S(1)}, bf16[256,256]{1,0:T(8,128)(2,1)S(1)}, u32[]{:S(2)}, u32[]{:S(2)}) collective-permute-start(bf16[256,256]{1,0:T(8,128)(2,1)S(1)} %shard_map.65.refs_0_), channel_id=1, source_target_pairs={{0,8},{4,12},{8,0},{12,4},{16,24},{20,28},{24,16},{28,20},{32,40},... | collective-permute-start | bytes 393224 | tf_op jit(solution)/shard_map/ppermute | solution.py:121
  76.5 9.6 %collective-permute-start.2 = (bf16[256,256]{1,0:T(8,128)(2,1)S(1)}, bf16[256,256]{1,0:T(8,128)(2,1)S(1)}, u32[]{:S(2)}, u32[]{:S(2)}) collective-permute-start(bf16[256,256]{1,0:T(8,128)(2,1)S(1)} %shard_map.65.refs_0_), channel_id=1, source_target_pairs={{0,12},{4,8},{8,4},{12,0},{16,28},{20,24},{24,20},{28,16},{32,44},... | collective-permute-start | bytes 393224 | tf_op jit(solution)/shard_map/ppermute | solution.py:121
  109.2 25.2 %collective-permute-start.6 = (bf16[64,256]{1,0:T(8,128)(2,1)S(1)}, bf16[64,256]{1,0:T(8,128)(2,1)S(1)}, u32[]{:S(2)}, u32[]{:S(2)}) collective-permute-start(bf16[64,256]{1,0:T(8,128)(2,1)S(1)} %get-tuple-element.24), channel_id=1, source_target_pairs={{0,16},{4,20},{8,24},{12,28},{16,0},{20,4},{24,8},{28,12},{32,48},... | collective-permute-start | bytes 98312 | tf_op jit(solution)/shard_map/ppermute | solution.py:121
  120.1 14.6 %collective-permute-start.7 = (bf16[64,256]{1,0:T(8,128)(2,1)S(1)}, bf16[64,256]{1,0:T(8,128)(2,1)S(1)}, u32[]{:S(2)}, u32[]{:S(2)}) collective-permute-start(bf16[64,256]{1,0:T(8,128)(2,1)S(1)} %get-tuple-element.25), channel_id=1, source_target_pairs={{0,32},{4,36},{8,40},{12,44},{16,48},{20,52},{24,56},{28,60},{32,0... | collective-permute-start | bytes 98312 | tf_op jit(solution)/shard_map/ppermute | solution.py:121
  132.5 10.6 %collective-permute-start.8 = (bf16[64,256]{1,0:T(8,128)(2,1)S(1)}, bf16[64,256]{1,0:T(8,128)(2,1)S(1)}, u32[]{:S(2)}, u32[]{:S(2)}) collective-permute-start(bf16[64,256]{1,0:T(8,128)(2,1)S(1)} %get-tuple-element.26), channel_id=1, source_target_pairs={{0,48},{4,52},{8,56},{12,60},{16,32},{20,36},{24,40},{28,44},{32,1... | collective-permute-start | bytes 98312 | tf_op jit(solution)/shard_map/ppermute | solution.py:121

commit v3 on v2

v3 whole, which is shorter than its diff:
```python
import functools

import jax
import jax.numpy as jnp
from jax import lax
from jax.experimental import pallas as pl
from jax.experimental.pallas import tpu as pltpu
from jax.sharding import PartitionSpec as P


TPE = 4
BF16 = jnp.bfloat16
F32 = jnp.float32


def dot(a, b, dims=((1,), (0,))):
    return lax.dot_general(a, b, (dims, ((), ())), preferred_element_type=F32)


def dispatch_kernel(cap, per_group, place, routes, probs, tokens, *outs):
    tok = tokens.shape[0]
    rows = outs[0].shape[0]
    half = cap // 2
    gates = probs[...] / jnp.sum(probs[...], axis=0, keepdims=True)
    before = lax.broadcasted_iota(jnp.int32, (tok, tok), 0)
    before = before < lax.broadcasted_iota(jnp.int32, (tok, tok), 1)
    before = jnp.where(before, F32(1.0), F32(0.0)).astype(BF16)
    row = lax.broadcasted_iota(jnp.int32, (rows, tok), 0)
    target = lax.shift_right_logical(row, half.bit_length() - 1) * per_group + place[0]
    slot = lax.bitwise_and(row, half - 1).astype(F32)
    hits = jnp.zeros((rows, tok), F32)
    weight = jnp.zeros((rows, tok), F32)
    for k in range(routes.shape[0]):
        match = routes[k : k + 1, :] == target
        hits = jnp.where(match, F32(1.0), hits)
        weight = jnp.where(match, gates[k : k + 1, :], weight)
    ranks = dot(hits.astype(BF16), before)
    for part in range(2):
        sent, high, low = outs[3 * part : 3 * part + 3]
        chosen = (hits > 0.5) & (ranks == slot + F32(part * half))
        select = jnp.where(chosen, F32(1.0), F32(0.0)).astype(BF16)
        mine = jnp.where(chosen, weight, F32(0.0))
        top = mine.astype(BF16)
        high[...] = top
        low[...] = (mine - top.astype(F32)).astype(BF16)
        width = sent.shape[1]
        step = min(512, width)
        for at in range(0, width, step):
            start = place[2] * width + at if part == 0 else at
            piece = tokens[:, pl.ds(pl.multiple_of(start, step), step)]
            sent[:, at : at + step] = dot(select, piece).astype(BF16)


def shuffle_kernel(block, place, weights, *outs):
    for k, out in enumerate(outs):
        owner = lax.bitwise_xor(place[1], k)
        for m in range(out.shape[1] // block):
            at = pl.multiple_of((m * TPE + owner) * block, block)
            out[:, m * block : (m + 1) * block] = weights[:, pl.ds(at, block)]


def activate(gate, upper):
    return (gate / (1.0 + jnp.exp(-gate)) * upper).astype(BF16)


def hidden_pair_kernel(place, mine, other, w_gate, w_up, out):
    width = mine.shape[1]
    own = pl.ds(pl.multiple_of(place[2] * width, width), width)
    far = pl.ds(pl.multiple_of((1 - place[2]) * width, width), width)
    gate = dot(mine[...], w_gate[own, :]) + dot(other[...], w_gate[far, :])
    upper = dot(mine[...], w_up[own, :]) + dot(other[...], w_up[far, :])
    out[...] = activate(gate, upper)


def hidden_kernel(rows, w_gate, w_up, out):
    out[...] = activate(dot(rows[...], w_gate[...]), dot(rows[...], w_up[...]))


def down_kernel(*refs):
    weights, out = refs[2 * TPE : 3 * TPE], refs[-1]
    groups, cap, width = out.shape
    step = min(256, width)
    for part in range(2):
        hidden = refs[part * TPE : (part + 1) * TPE]
        slots = slice(part * cap // 2, (part + 1) * cap // 2)
        for at in range(0, width, step):
            total = dot(hidden[0][...], weights[0][:, at : at + step])
            for k in range(1, TPE):
                total = total + dot(hidden[k][...], weights[k][:, at : at + step])
            total = total.reshape(groups, cap // 2, step)
            out[:, slots, at : at + step] = total.astype(BF16)


def combine_kernel(place, high_a, low_a, high_b, low_b, rows, kept, *sent):
    block = kept.shape[1]
    groups, cap, _ = rows.shape
    for k in range(TPE):
        at = pl.multiple_of(lax.bitwise_xor(place[0], k) * block, block)
        total = jnp.zeros(kept.shape, F32)
        for part, pair in enumerate(((high_a, low_a), (high_b, low_b))):
            slots = slice(part * cap // 2, (part + 1) * cap // 2)
            piece = rows[:, slots, pl.ds(at, block)].astype(F32)
            piece = piece.reshape(groups * cap // 2, block).astype(BF16)
            for factor in pair:
                total = total + dot(factor[...], piece, ((0,), (0,)))
        if k == 0:
            kept[...] = total
        else:
            sent[k - 1][...] = total.astype(BF16)


def finish_kernel(kept, *refs):
    total = kept[...]
    for part in refs[:-1]:
        total = total + part[...].astype(F32)
    refs[-1][...] = total.astype(BF16)


def call(kernel, shapes, *args, flops=0, limit=None):
    specs = [pl.BlockSpec(memory_space=pltpu.VMEM)] * len(args)
    if args[0].ndim == 1:
        specs[0] = pl.BlockSpec(memory_space=pltpu.SMEM)
    outs = [jax.ShapeDtypeStruct(s, d) for s, d in shapes]
    moved = sum(a.size * a.dtype.itemsize for a in (*args, *outs))
    return pl.pallas_call(
        kernel,
        out_shape=outs,
        in_specs=specs,
        out_specs=[pl.BlockSpec(memory_space=pltpu.VMEM)] * len(outs),
        compiler_params=pltpu.CompilerParams(vmem_limit_bytes=limit),
        cost_estimate=pl.CostEstimate(flops=flops, bytes_accessed=moved, transcendentals=0),
    )(*args)


def on_device(tokens, routes, probs, w_gate, w_up, w_down):
    groups, shards = lax.axis_size("grp"), lax.axis_size("shard")
    per_group = shards // TPE
    tok, width = tokens.shape
    units = w_down.shape[1]
    block, quarter = width // shards, width // TPE
    cap = 2 * tok * routes.shape[1] // (groups * per_group)
    rows = groups * cap // 2
    room = 16 << 20
    z = lax.axis_index("shard")
    place = jnp.stack([z // TPE, lax.rem(z, TPE), lax.rem(z, 2)]).astype(jnp.int32)

    def over_y(x):
        return lax.all_to_all(x.reshape(groups, -1, x.shape[-1]), "grp", 0, 0, tiled=True)

    def swap(x, bits):
        return lax.ppermute(x, "shard", [(i, i ^ bits) for i in range(shards)])

    factor = ((rows, tok), BF16)
    sent_a, high_a, low_a, sent_b, high_b, low_b = call(
        functools.partial(dispatch_kernel, cap, per_group),
        [((rows, width // 2), BF16), factor, factor, ((rows, width), BF16), factor, factor],
        place, routes.T, probs.T, tokens, flops=3 * rows * tok * width,
    )
    mine = over_y(sent_a).reshape(rows, width // 2)
    parts = call(
        functools.partial(shuffle_kernel, block),
        [((units, quarter), BF16)] * TPE, place, w_down[0],
    )
    weights = [parts[0]] + [swap(parts[k], k) for k in range(1, TPE)]
    other = swap(mine, 1)
    arrived = over_y(sent_b).reshape(rows, width)
    (hidden_a,) = call(
        hidden_pair_kernel, [((rows, units), BF16)], place, mine, other, w_gate[0], w_up[0],
        flops=4 * rows * width * units,
    )
    hiddens_a = [hidden_a] + [swap(hidden_a, k) for k in range(1, TPE)]
    (hidden_b,) = call(
        hidden_kernel, [((rows, units), BF16)], arrived, w_gate[0], w_up[0],
        flops=4 * rows * width * units, limit=room,
    )
    hiddens_b = [hidden_b] + [swap(hidden_b, k) for k in range(1, TPE)]
    (result,) = call(
        down_kernel, [((groups, cap, quarter), BF16)], *hiddens_a, *hiddens_b, *weights,
        flops=4 * rows * width * units, limit=room,
    )
    returned = over_y(result)
    kept, *halves = call(
        combine_kernel,
        [((tok, block), F32)] + [((tok, block), BF16)] * (TPE - 1),
        place, high_a, low_a, high_b, low_b, returned, limit=room,
    )
    halves = [swap(h, TPE * (k + 1)) for k, h in enumerate(halves)]
    (mixed,) = call(finish_kernel, [((tok, block), BF16)], kept, *halves, limit=room)
    return mixed


def solution(mesh):
    return jax.shard_map(
        on_device,
        mesh=mesh,
        in_specs=(
            P(("grp", "side"), None),
            P(("grp", "side"), None),
            P(("grp", "side"), None),
            P(("grp", "shard"), None, None),
            P(("grp", "shard"), None, None),
            P(("grp", "shard"), None, None),
        ),
        out_specs=P(("grp", "side"), "shard"),
        check_vma=False,
    )
```

time: 145 us -> 170 us (1.17)
  waiting for transfers between devices: 49.8 us -> 12.2 us
  starting transfers between devices: 56.9 us -> 92.1 us
  blocking collectives: 20.3 us -> 46 us
  Pallas kernels: 7.94 us -> 14.5 us
  local copies, waits for them, and re-layouts: 8.51 us -> 2.52 us
    ppermute x9 -> x13, starting transfers between devices: 49.7 us -> 87.9 us  [swap(): return lax.ppermute(x, 'shard', [(i, i ^ bits) for i in range(shards)])]
    all_to_all x1, waiting for transfers between devices: 33.4 us -> 0.01 us  [over_y(): lax.all_to_all(x.reshape(groups, -1, x.shape[-1]), 'grp', 0, 0, tiled=True)]
    all_to_all x1 -> x2, blocking collectives: 20.3 us -> 46 us  [over_y(): lax.all_to_all(x.reshape(groups, -1, x.shape[-1]), 'grp', 0, 0, tiled=True)]
    pallas_call x6 -> x7, Pallas kernels: 7.94 us -> 14.5 us  [call(): pl.pallas_call(kernel, out_shape=outs, in_specs=specs, out_specs=[pl.Bloc...]
    unnamed x14 -> x22, local copies, waits for them, and re-layouts: 8.51 us -> 2.52 us
    ppermute x9 -> x13, waiting for transfers between devices: 16.4 us -> 12.2 us  [swap(): return lax.ppermute(x, 'shard', [(i, i ^ bits) for i in range(shards)])]
    all_to_all x1, starting transfers between devices: 7.2 us -> 4.24 us  [over_y(): lax.all_to_all(x.reshape(groups, -1, x.shape[-1]), 'grp', 0, 0, tiled=True)]
  transfers between devices with their start and end apart: 10 -> 14, of which waited for: 4 -> 4; matrix products, arithmetic and copies ran while one was open for 0% -> 0% of each run, Pallas kernels for 2% -> 5%
where the time goes in v3:
time: 170 us; the launch traced here: 168 us
  starting transfers between devices  92.1 us (54%)
  blocking collectives  46 us (27%)
  Pallas kernels  14.5 us (9%)
  waiting for transfers between devices  12.2 us (7%)
  local copies, waits for them, and re-layouts  2.52 us (1%)
    ppermute x13, starting transfers between devices, swap(): return lax.ppermute(x, 'shard', [(i, i ^ bits) for i in range(shards)])  87.9 us
    all_to_all x2, blocking collectives, over_y(): lax.all_to_all(x.reshape(groups, -1, x.shape[-1]), 'grp', 0, 0, tiled=True)  46 us
    pallas_call x7, Pallas kernels, call(): pl.pallas_call(kernel, out_shape=outs, in_specs=specs, out_specs=[pl.Bloc...  14.5 us
    ppermute x13, waiting for transfers between devices, swap(): return lax.ppermute(x, 'shard', [(i, i ^ bits) for i in range(shards)])  12.2 us
    all_to_all x1, starting transfers between devices, over_y(): lax.all_to_all(x.reshape(groups, -1, x.shape[-1]), 'grp', 0, 0, tiled=True)  4.24 us
  transfers between devices with their start and end apart: 14, of which 4 were waited for; matrix products, arithmetic and copies ran while one was open for 0% of the time, Pallas kernels for 5%

profile of v3, /device:TPU:6, one launch (start us, length us, event | category | flops | bytes accessed | tf_op | source)
XLA Modules:
  0.0 168.3 jit_solution(11256548199010390661)
XLA Ops:
  0.0 0.6 pad_add_fusion.place
  0.6 2.8 %shard_map.64 = (bf16[128,2048]{1,0:T(8,128)(2,1)}, bf16[128,64]{1,0:T(8,128)(2,1)}, bf16[128,64]{1,0:T(8,128)(2,1)}, bf16[128,4096]{1,0:T(8,128)(2,1)}, bf16[12...) custom-call(s32[3]{0:T(128)} %pad_add_fusion.place, s32[8,64]{1,0:T(8,128)} %bitcast.22, f32[8,64]{1,0:T(8,128)} %bitcast.23, ...), custom_call_target="tpu_custom_call" | custom-call | flops 100663296 | bytes 2166796 | tf_op jit(solution)/shard_map/pallas_call | solution.py:125
  3.4 23.1 %all_to_all.15 = bf16[16,8,2048]{2,1,0:T(8,128)(2,1)S(1)} all-to-all(bf16[16,8,2048]{2,1,0:T(8,128)(2,1)} %bitcast.21), channel_id=1, replica_groups=mesh['grp'=16,'shard'=16,'side'=4] {'grp'}, dimensions={0} | all-to-all | bytes 1048576 | tf_op jit(solution)/shard_map/all_to_all | solution.py:148
  26.6 4.2 %all-to-all-start.1 = ((bf16[16,8,4096]{2,1,0:T(8,128)(2,1)}), bf16[16,8,4096]{2,1,0:T(8,128)(2,1)S(1)}, u32[]{:S(2)}, u32[]{:S(2)}) async-start(bf16[16,8,4096]{2,1,0:T(8,128)(2,1)} %bitcast.20), calls=%async_computation.1 | async-start | bytes 2097152 | tf_op jit(solution)/shard_map/all_to_all | solution.py:148
  30.8 4.3 %collective-permute-start = (bf16[128,2048]{1,0:T(8,128)(2,1)S(1)}, bf16[128,2048]{1,0:T(8,128)(2,1)S(1)}, u32[]{:S(2)}, u32[]{:S(2)}) collective-permute-start(bf16[128,2048]{1,0:T(8,128)(2,1)S(1)} %bitcast.18), channel_id=1, source_target_pairs={{0,4},{4,0},{8,12},{12,8},{16,20},{20,16},{24,28},{28,24},{32,36},... | collective-permute-start | bytes 1572872 | tf_op jit(solution)/shard_map/ppermute | solution.py:151
  35.1 3.3 %shard_map.67 = (bf16[256,1024]{1,0:T(8,128)(2,1)}, bf16[256,1024]{1,0:T(8,128)(2,1)}, bf16[256,1024]{1,0:T(8,128)(2,1)}, bf16[256,1024]{1,0:T(8,128)(2,1)}) custom-call(s32[3]{0:T(128)} %pad_add_fusion.place, bf16[256,4096]{1,0:T(8,128)(2,1)} %bitcast.17), custom_call_target="tpu_custom_call" | custom-call | bytes 4194316 | tf_op jit(solution)/shard_map/pallas_call | solution.py:125
  38.4 1.9 %collective-permute-start.7 = (bf16[256,1024]{1,0:T(8,128)(2,1)}, bf16[256,1024]{1,0:T(8,128)(2,1)}, u32[]{:S(2)}, u32[]{:S(2)}) collective-permute-start(bf16[256,1024]{1,0:T(8,128)(2,1)} %get-tuple-element.26), channel_id=1, source_target_pairs={{0,4},{4,0},{8,12},{12,8},{16,20},{20,16},{24,28},{28,24},{32,36},... | collective-permute-start | bytes 1572872 | tf_op jit(solution)/shard_map/ppermute | solution.py:151
  40.3 6.1 %collective-permute-start.8 = (bf16[256,1024]{1,0:T(8,128)(2,1)}, bf16[256,1024]{1,0:T(8,128)(2,1)}, u32[]{:S(2)}, u32[]{:S(2)}) collective-permute-start(bf16[256,1024]{1,0:T(8,128)(2,1)} %get-tuple-element.27), channel_id=1, source_target_pairs={{0,8},{4,12},{8,0},{12,4},{16,24},{20,28},{24,16},{28,20},{32,40},... | collective-permute-start | bytes 1572872 | tf_op jit(solution)/shard_map/ppermute | solution.py:151
  46.4 3.4 %collective-permute-start.9 = (bf16[256,1024]{1,0:T(8,128)(2,1)}, bf16[256,1024]{1,0:T(8,128)(2,1)}, u32[]{:S(2)}, u32[]{:S(2)}) collective-permute-start(bf16[256,1024]{1,0:T(8,128)(2,1)} %get-tuple-element.28), channel_id=1, source_target_pairs={{0,12},{4,8},{8,4},{12,0},{16,28},{20,24},{24,20},{28,16},{32,44},... | collective-permute-start | bytes 1572872 | tf_op jit(solution)/shard_map/ppermute | solution.py:151
  49.8 0.8 copy-done.10
  50.6 4.1 %shard_map.65.refs_0_ = bf16[128,256]{1,0:T(8,128)(2,1)} custom-call(s32[3]{0:T(128)} %pad_add_fusion.place, bf16[128,2048]{1,0:T(8,128)(2,1)} %bitcast.19, bf16[128,2048]{1,0:T(8,128)(2,1)} %copy-done.10, bf16[4096,256]{1,0:T(8,128)(2,1)} %bitcast.12, bf16[4096,256]{1,0:T(8,128)(2,1)} %bitcast.14), custom_call_target="tpu_custom_call" | custom-call | flops 536870912 | bytes 5308428 | tf_op jit(solution)/shard_map/pallas_call | solution.py:125
  54.7 16.4 %collective-permute-start.3 = (bf16[128,256]{1,0:T(8,128)(2,1)}, bf16[128,256]{1,0:T(8,128)(2,1)S(1)}, u32[]{:S(2)}, u32[]{:S(2)}) collective-permute-start(bf16[128,256]{1,0:T(8,128)(2,1)} %shard_map.65.refs_0_), channel_id=1, source_target_pairs={{0,12},{4,8},{8,4},{12,0},{16,28},{20,24},{24,20},{28,16},{32,44},... | collective-permute-start | bytes 196616 | tf_op jit(solution)/shard_map/ppermute | solution.py:151
  71.1 1.9 %collective-permute-start.2 = (bf16[128,256]{1,0:T(8,128)(2,1)}, bf16[128,256]{1,0:T(8,128)(2,1)S(1)}, u32[]{:S(2)}, u32[]{:S(2)}) collective-permute-start(bf16[128,256]{1,0:T(8,128)(2,1)} %shard_map.65.refs_0_), channel_id=1, source_target_pairs={{0,8},{4,12},{8,0},{12,4},{16,24},{20,28},{24,16},{28,20},{32,40},... | collective-permute-start | bytes 196616 | tf_op jit(solution)/shard_map/ppermute | solution.py:151
  73.1 0.0 copy-start.1
  73.1 1.6 copy-done.1
  74.7 0.7 shard_map.66.refs_4_
  75.4 0.1 copy-done.3
  75.5 2.5 %collective-permute-start.1 = (bf16[128,256]{1,0:T(8,128)(2,1)S(1)}, bf16[128,256]{1,0:T(8,128)(2,1)S(1)}, u32[]{:S(2)}, u32[]{:S(2)}) collective-permute-start(bf16[128,256]{1,0:T(8,128)(2,1)S(1)} %copy-done.3), channel_id=1, source_target_pairs={{0,4},{4,0},{8,12},{12,8},{16,20},{20,16},{24,28},{28,24},{32,36},... | collective-permute-start | bytes 196616 | tf_op jit(solution)/shard_map/ppermute | solution.py:151
  78.0 14.2 %collective-permute-start.6 = (bf16[128,256]{1,0:T(8,128)(2,1)S(1)}, bf16[128,256]{1,0:T(8,128)(2,1)S(1)}, u32[]{:S(2)}, u32[]{:S(2)}) collective-permute-start(bf16[128,256]{1,0:T(8,128)(2,1)S(1)} %shard_map.66.refs_4_), channel_id=1, source_target_pairs={{0,12},{4,8},{8,4},{12,0},{16,28},{20,24},{24,20},{28,16},{32,44},... | collective-permute-start | bytes 196616 | tf_op jit(solution)/shard_map/ppermute | solution.py:151
  92.2 10.7 %collective-permute-start.5 = (bf16[128,256]{1,0:T(8,128)(2,1)S(1)}, bf16[128,256]{1,0:T(8,128)(2,1)S(1)}, u32[]{:S(2)}, u32[]{:S(2)}) collective-permute-start(bf16[128,256]{1,0:T(8,128)(2,1)S(1)} %shard_map.66.refs_4_), channel_id=1, source_target_pairs={{0,8},{4,12},{8,0},{12,4},{16,24},{20,28},{24,16},{28,20},{32,40},... | collective-permute-start | bytes 196616 | tf_op jit(solution)/shard_map/ppermute | solution.py:151
  102.8 1.9 %collective-permute-start.4 = (bf16[128,256]{1,0:T(8,128)(2,1)S(1)}, bf16[128,256]{1,0:T(8,128)(2,1)S(1)}, u32[]{:S(2)}, u32[]{:S(2)}) collective-permute-start(bf16[128,256]{1,0:T(8,128)(2,1)S(1)} %shard_map.66.refs_4_), channel_id=1, source_target_pairs={{0,4},{4,0},{8,12},{12,8},{16,20},{20,16},{24,28},{28,24},{32,36},... | collective-permute-start | bytes 196616 | tf_op jit(solution)/shard_map/ppermute | solution.py:151
  104.8 1.0 collective-permute-done.5.refs_6_
  105.8 3.2 %collective-permute-done.4.refs_5_ = bf16[128,256]{1,0:T(8,128)(2,1)S(1)} collective-permute-done((bf16[128,256]{1,0:T(8,128)(2,1)S(1)}, bf16[128,256]{1,0:T(8,128)(2,1)S(1)}, u32[]{:S(2)}, u32[]{:S(2)}) %collective-permute-start.4) | collective-permute-done | bytes 65568 | tf_op jit(solution)/shard_map/ppermute | solution.py:151
  109.0 2.1 %shard_map.68 = bf16[16,16,1024]{2,1,0:T(8,128)(2,1)S(1)} custom-call(bf16[128,256]{1,0:T(8,128)(2,1)S(1)} %copy-done.3, bf16[128,256]{1,0:T(8,128)(2,1)S(1)} %collective-permute-done.1.refs_1_, bf16[128,256]{1,0:T(8,128)(2,1)S(1)} %collective-permute-done.2.refs_2_, bf16[128,256]{1,0:T(8,128)(2,1)S(1)} %collective-permute-done.3.refs_3_, ...), custom_call_target="tpu_custom_call" | custom-call | flops 536870912 | bytes 3145728 | tf_op jit(solution)/shard_map/pallas_call | solution.py:125
  111.2 22.9 %all_to_all.16.rows = bf16[16,16,1024]{2,1,0:T(8,128)(2,1)S(1)} all-to-all(bf16[16,16,1024]{2,1,0:T(8,128)(2,1)S(1)} %shard_map.68), channel_id=1, replica_groups=mesh['grp'=16,'shard'=16,'side'=4] {'grp'}, dimensions={0} | all-to-all | bytes 1048576 | tf_op jit(solution)/shard_map/all_to_all | solution.py:148
  134.1 0.9 shard_map.69
  135.0 10.9 %collective-permute-start.10 = (bf16[64,256]{1,0:T(8,128)(2,1)S(1)}, bf16[64,256]{1,0:T(8,128)(2,1)S(1)}, u32[]{:S(2)}, u32[]{:S(2)}) collective-permute-start(bf16[64,256]{1,0:T(8,128)(2,1)S(1)} %get-tuple-element.30), channel_id=1, source_target_pairs={{0,16},{4,20},{8,24},{12,28},{16,0},{20,4},{24,8},{28,12},{32,48},... | collective-permute-start | bytes 98312 | tf_op jit(solution)/shard_map/ppermute | solution.py:151
  145.9 11.8 %collective-permute-start.11 = (bf16[64,256]{1,0:T(8,128)(2,1)S(1)}, bf16[64,256]{1,0:T(8,128)(2,1)S(1)}, u32[]{:S(2)}, u32[]{:S(2)}) collective-permute-start(bf16[64,256]{1,0:T(8,128)(2,1)S(1)} %get-tuple-element.31), channel_id=1, source_target_pairs={{0,32},{4,36},{8,40},{12,44},{16,48},{20,52},{24,56},{28,60},{32,0... | collective-permute-start | bytes 98312 | tf_op jit(solution)/shard_map/ppermute | solution.py:151
  157.7 1.9 %collective-permute-start.12 = (bf16[64,256]{1,0:T(8,128)(2,1)S(1)}, bf16[64,256]{1,0:T(8,128)(2,1)S(1)}, u32[]{:S(2)}, u32[]{:S(2)}) collective-permute-start(bf16[64,256]{1,0:T(8,128)(2,1)S(1)} %get-tuple-element.32), channel_id=1, source_target_pairs={{0,48},{4,52},{8,56},{12,60},{16,32},{20,36},{24,40},{28,44},{32,1... | collective-permute-start | bytes 98312 | tf_op jit(solution)/shard_map/ppermute | solution.py:151
  159.6 0.8 collective-permute-done.11.refs_1_
  160.4 7.2 %collective-permute-done.12.refs_2_ = bf16[64,256]{1,0:T(8,128)(2,1)S(1)} collective-permute-done((bf16[64,256]{1,0:T(8,128)(2,1)S(1)}, bf16[64,256]{1,0:T(8,128)(2,1)S(1)}, u32[]{:S(2)}, u32[]{:S(2)}) %collective-permute-start.12) | collective-permute-done | bytes 32800 | tf_op jit(solution)/shard_map/ppermute | solution.py:151
  167.6 0.6 shard_map.70
  (28 shorter events, 0.1 us)
Async XLA Ops:
  26.6 11.8 %copy-start.9 = (bf16[16,8,2048]{2,1,0:T(8,128)(2,1)}, bf16[16,8,2048]{2,1,0:T(8,128)(2,1)S(1)}, u32[]{:S(2)}) copy-start(bf16[16,8,2048]{2,1,0:T(8,128)(2,1)S(1)} %all_to_all.15) | copy-start | bytes 1572868
  26.6 46.5 %all-to-all-start.1 = ((bf16[16,8,4096]{2,1,0:T(8,128)(2,1)}), bf16[16,8,4096]{2,1,0:T(8,128)(2,1)S(1)}, u32[]{:S(2)}, u32[]{:S(2)}) async-start(bf16[16,8,4096]{2,1,0:T(8,128)(2,1)} %bitcast.20), calls=%async_computation.1 | async-start | bytes 2097152 | tf_op jit(solution)/shard_map/all_to_all | solution.py:148
  30.8 19.0 %collective-permute-start = (bf16[128,2048]{1,0:T(8,128)(2,1)S(1)}, bf16[128,2048]{1,0:T(8,128)(2,1)S(1)}, u32[]{:S(2)}, u32[]{:S(2)}) collective-permute-start(bf16[128,2048]{1,0:T(8,128)(2,1)S(1)} %bitcast.18), channel_id=1, source_target_pairs={{0,4},{4,0},{8,12},{12,8},{16,20},{20,16},{24,28},{28,24},{32,36},... | collective-permute-start | bytes 1572872 | tf_op jit(solution)/shard_map/ppermute | solution.py:151
  38.4 37.0 %collective-permute-start.7 = (bf16[256,1024]{1,0:T(8,128)(2,1)}, bf16[256,1024]{1,0:T(8,128)(2,1)}, u32[]{:S(2)}, u32[]{:S(2)}) collective-permute-start(bf16[256,1024]{1,0:T(8,128)(2,1)} %get-tuple-element.26), channel_id=1, source_target_pairs={{0,4},{4,0},{8,12},{12,8},{16,20},{20,16},{24,28},{28,24},{32,36},... | collective-permute-start | bytes 1572872 | tf_op jit(solution)/shard_map/ppermute | solution.py:151
  40.3 37.7 %collective-permute-start.8 = (bf16[256,1024]{1,0:T(8,128)(2,1)}, bf16[256,1024]{1,0:T(8,128)(2,1)}, u32[]{:S(2)}, u32[]{:S(2)}) collective-permute-start(bf16[256,1024]{1,0:T(8,128)(2,1)} %get-tuple-element.27), channel_id=1, source_target_pairs={{0,8},{4,12},{8,0},{12,4},{16,24},{20,28},{24,16},{28,20},{32,40},... | collective-permute-start | bytes 1572872 | tf_op jit(solution)/shard_map/ppermute | solution.py:151
  46.4 45.8 %collective-permute-start.9 = (bf16[256,1024]{1,0:T(8,128)(2,1)}, bf16[256,1024]{1,0:T(8,128)(2,1)}, u32[]{:S(2)}, u32[]{:S(2)}) collective-permute-start(bf16[256,1024]{1,0:T(8,128)(2,1)} %get-tuple-element.28), channel_id=1, source_target_pairs={{0,12},{4,8},{8,4},{12,0},{16,28},{20,24},{24,20},{28,16},{32,44},... | collective-permute-start | bytes 1572872 | tf_op jit(solution)/shard_map/ppermute | solution.py:151
  49.8 0.8 copy-start.10
  50.6 22.5 %copy-start = (bf16[1,4096,256]{2,1,0:T(8,128)(2,1)S(1)}, bf16[1,4096,256]{2,1,0:T(8,128)(2,1)}, u32[]{:S(2)}) copy-start(bf16[1,4096,256]{2,1,0:T(8,128)(2,1)} %param.9) | copy-start | bytes 6291460
  54.7 48.2 %collective-permute-start.3 = (bf16[128,256]{1,0:T(8,128)(2,1)}, bf16[128,256]{1,0:T(8,128)(2,1)S(1)}, u32[]{:S(2)}, u32[]{:S(2)}) collective-permute-start(bf16[128,256]{1,0:T(8,128)(2,1)} %shard_map.65.refs_0_), channel_id=1, source_target_pairs={{0,12},{4,8},{8,4},{12,0},{16,28},{20,24},{24,20},{28,16},{32,44},... | collective-permute-start | bytes 196616 | tf_op jit(solution)/shard_map/ppermute | solution.py:151
  71.1 33.6 %collective-permute-start.2 = (bf16[128,256]{1,0:T(8,128)(2,1)}, bf16[128,256]{1,0:T(8,128)(2,1)S(1)}, u32[]{:S(2)}, u32[]{:S(2)}) collective-permute-start(bf16[128,256]{1,0:T(8,128)(2,1)} %shard_map.65.refs_0_), channel_id=1, source_target_pairs={{0,8},{4,12},{8,0},{12,4},{16,24},{20,28},{24,16},{28,20},{32,40},... | collective-permute-start | bytes 196616 | tf_op jit(solution)/shard_map/ppermute | solution.py:151
  73.1 1.6 copy-start.1
  74.7 0.8 copy-start.3
  74.7 34.3 %copy-start.2 = (bf16[256,1024]{1,0:T(8,128)(2,1)S(1)}, bf16[256,1024]{1,0:T(8,128)(2,1)}, u32[]{:S(2)}) copy-start(bf16[256,1024]{1,0:T(8,128)(2,1)} %get-tuple-element.25.refs_8_) | copy-start | bytes 1572868
  75.5 29.3 %collective-permute-start.1 = (bf16[128,256]{1,0:T(8,128)(2,1)S(1)}, bf16[128,256]{1,0:T(8,128)(2,1)S(1)}, u32[]{:S(2)}, u32[]{:S(2)}) collective-permute-start(bf16[128,256]{1,0:T(8,128)(2,1)S(1)} %copy-done.3), channel_id=1, source_target_pairs={{0,4},{4,0},{8,12},{12,8},{16,20},{20,16},{24,28},{28,24},{32,36},... | collective-permute-start | bytes 196616 | tf_op jit(solution)/shard_map/ppermute | solution.py:151
  78.0 26.8 %collective-permute-start.6 = (bf16[128,256]{1,0:T(8,128)(2,1)S(1)}, bf16[128,256]{1,0:T(8,128)(2,1)S(1)}, u32[]{:S(2)}, u32[]{:S(2)}) collective-permute-start(bf16[128,256]{1,0:T(8,128)(2,1)S(1)} %shard_map.66.refs_4_), channel_id=1, source_target_pairs={{0,12},{4,8},{8,4},{12,0},{16,28},{20,24},{24,20},{28,16},{32,44},... | collective-permute-start | bytes 196616 | tf_op jit(solution)/shard_map/ppermute | solution.py:151
  92.2 13.6 %collective-permute-start.5 = (bf16[128,256]{1,0:T(8,128)(2,1)S(1)}, bf16[128,256]{1,0:T(8,128)(2,1)S(1)}, u32[]{:S(2)}, u32[]{:S(2)}) collective-permute-start(bf16[128,256]{1,0:T(8,128)(2,1)S(1)} %shard_map.66.refs_4_), channel_id=1, source_target_pairs={{0,8},{4,12},{8,0},{12,4},{16,24},{20,28},{24,16},{28,20},{32,40},... | collective-permute-start | bytes 196616 | tf_op jit(solution)/shard_map/ppermute | solution.py:151
  102.8 6.2 %collective-permute-start.4 = (bf16[128,256]{1,0:T(8,128)(2,1)S(1)}, bf16[128,256]{1,0:T(8,128)(2,1)S(1)}, u32[]{:S(2)}, u32[]{:S(2)}) collective-permute-start(bf16[128,256]{1,0:T(8,128)(2,1)S(1)} %shard_map.66.refs_4_), channel_id=1, source_target_pairs={{0,4},{4,0},{8,12},{12,8},{16,20},{20,16},{24,28},{28,24},{32,36},... | collective-permute-start | bytes 196616 | tf_op jit(solution)/shard_map/ppermute | solution.py:151
  109.0 25.1 %copy-start.4 = (bf16[128,64]{1,0:T(8,128)(2,1)S(1)}, bf16[128,64]{1,0:T(8,128)(2,1)}, u32[]{:S(2)}) copy-start(bf16[128,64]{1,0:T(8,128)(2,1)} %get-tuple-element.19.high_a) | copy-start | bytes 49156
  109.0 25.1 %copy-start.5 = (bf16[128,64]{1,0:T(8,128)(2,1)S(1)}, bf16[128,64]{1,0:T(8,128)(2,1)}, u32[]{:S(2)}) copy-start(bf16[128,64]{1,0:T(8,128)(2,1)} %get-tuple-element.20.low_a) | copy-start | bytes 49156
  109.0 25.1 %copy-start.6 = (bf16[128,64]{1,0:T(8,128)(2,1)S(1)}, bf16[128,64]{1,0:T(8,128)(2,1)}, u32[]{:S(2)}) copy-start(bf16[128,64]{1,0:T(8,128)(2,1)} %get-tuple-element.21.high_b) | copy-start | bytes 49156
  109.0 25.1 %copy-start.7 = (bf16[128,64]{1,0:T(8,128)(2,1)S(1)}, bf16[128,64]{1,0:T(8,128)(2,1)}, u32[]{:S(2)}) copy-start(bf16[128,64]{1,0:T(8,128)(2,1)} %get-tuple-element.22.low_b) | copy-start | bytes 49156
  109.0 25.1 %copy-start.8 = (s32[3]{0:T(128)S(1)}, s32[3]{0:T(128)}, u32[]{:S(2)}) copy-start(s32[3]{0:T(128)} %pad_add_fusion.place) | copy-start | bytes 40
  135.0 24.7 %collective-permute-start.10 = (bf16[64,256]{1,0:T(8,128)(2,1)S(1)}, bf16[64,256]{1,0:T(8,128)(2,1)S(1)}, u32[]{:S(2)}, u32[]{:S(2)}) collective-permute-start(bf16[64,256]{1,0:T(8,128)(2,1)S(1)} %get-tuple-element.30), channel_id=1, source_target_pairs={{0,16},{4,20},{8,24},{12,28},{16,0},{20,4},{24,8},{28,12},{32,48},... | collective-permute-start | bytes 98312 | tf_op jit(solution)/shard_map/ppermute | solution.py:151
  145.9 14.5 %collective-permute-start.11 = (bf16[64,256]{1,0:T(8,128)(2,1)S(1)}, bf16[64,256]{1,0:T(8,128)(2,1)S(1)}, u32[]{:S(2)}, u32[]{:S(2)}) collective-permute-start(bf16[64,256]{1,0:T(8,128)(2,1)S(1)} %get-tuple-element.31), channel_id=1, source_target_pairs={{0,32},{4,36},{8,40},{12,44},{16,48},{20,52},{24,56},{28,60},{32,0... | collective-permute-start | bytes 98312 | tf_op jit(solution)/shard_map/ppermute | solution.py:151
  157.7 9.9 %collective-permute-start.12 = (bf16[64,256]{1,0:T(8,128)(2,1)S(1)}, bf16[64,256]{1,0:T(8,128)(2,1)S(1)}, u32[]{:S(2)}, u32[]{:S(2)}) collective-permute-start(bf16[64,256]{1,0:T(8,128)(2,1)S(1)} %get-tuple-element.32), channel_id=1, source_target_pairs={{0,48},{4,52},{8,56},{12,60},{16,32},{20,36},{24,40},{28,44},{32,1... | collective-permute-start | bytes 98312 | tf_op jit(solution)/shard_map/ppermute | solution.py:151

commit v4 on v3

--- a/solution.py
+++ b/solution.py
@@ -53,10 +53,14 @@
 
 def shuffle_kernel(block, place, weights, *outs):
     for k, out in enumerate(outs):
-        owner = lax.bitwise_xor(place[1], k)
-        for m in range(out.shape[1] // block):
-            at = pl.multiple_of((m * TPE + owner) * block, block)
-            out[:, m * block : (m + 1) * block] = weights[:, pl.ds(at, block)]
+        at = place[3] * TPE + lax.bitwise_xor(place[1], k)
+        out[...] = weights[:, pl.ds(pl.multiple_of(at * block, block), block)]
+
+
+def stack_kernel(*refs):
+    size = refs[0].shape[0]
+    for k, ref in enumerate(refs[:-1]):
+        refs[-1][k * size : (k + 1) * size, :] = ref[...]
 
 
 def activate(gate, upper):
@@ -76,19 +80,21 @@
     out[...] = activate(dot(rows[...], w_gate[...]), dot(rows[...], w_up[...]))
 
 
-def down_kernel(*refs):
-    weights, out = refs[2 * TPE : 3 * TPE], refs[-1]
-    groups, cap, width = out.shape
-    step = min(256, width)
+def down_kernel(place, *refs):
+    weights, out = refs[2 * TPE : -1], refs[-1]
+    groups, cap, _ = out.shape
+    block = weights[0].shape[1]
+    units = refs[0].shape[1]
     for part in range(2):
         hidden = refs[part * TPE : (part + 1) * TPE]
         slots = slice(part * cap // 2, (part + 1) * cap // 2)
-        for at in range(0, width, step):
-            total = dot(hidden[0][...], weights[0][:, at : at + step])
+        for side, weight in enumerate(weights):
+            total = dot(hidden[0][...], weight[:units, :])
             for k in range(1, TPE):
-                total = total + dot(hidden[k][...], weights[k][:, at : at + step])
-            total = total.reshape(groups, cap // 2, step)
-            out[:, slots, at : at + step] = total.astype(BF16)
+                total = total + dot(hidden[k][...], weight[k * units : (k + 1) * units, :])
+            total = total.reshape(groups, cap // 2, block).astype(BF16)
+            at = pl.multiple_of(lax.bitwise_xor(place[3], side) * block, block)
+            out[:, slots, pl.ds(at, block)] = total
 
 
 def combine_kernel(place, high_a, low_a, high_b, low_b, rows, kept, *sent):
@@ -142,13 +148,15 @@
     rows = groups * cap // 2
     room = 16 << 20
     z = lax.axis_index("shard")
-    place = jnp.stack([z // TPE, lax.rem(z, TPE), lax.rem(z, 2)]).astype(jnp.int32)
+    sides = lax.axis_size("side")
+    place = [z // TPE, lax.rem(z, TPE), lax.rem(z, 2), lax.axis_index("side")]
+    place = jnp.stack(place).astype(jnp.int32)
 
     def over_y(x):
         return lax.all_to_all(x.reshape(groups, -1, x.shape[-1]), "grp", 0, 0, tiled=True)
 
-    def swap(x, bits):
-        return lax.ppermute(x, "shard", [(i, i ^ bits) for i in range(shards)])
+    def swap(x, bits, axis="shard"):
+        return lax.ppermute(x, axis, [(i, i ^ bits) for i in range(lax.axis_size(axis))])
 
     factor = ((rows, tok), BF16)
     sent_a, high_a, low_a, sent_b, high_b, low_b = call(
@@ -159,9 +167,11 @@
     mine = over_y(sent_a).reshape(rows, width // 2)
     parts = call(
         functools.partial(shuffle_kernel, block),
-        [((units, quarter), BF16)] * TPE, place, w_down[0],
-    )
-    weights = [parts[0]] + [swap(parts[k], k) for k in range(1, TPE)]
+        [((units, block), BF16)] * TPE, place, w_down[0],
+    )
+    parts = [parts[0]] + [swap(parts[k], k) for k in range(1, TPE)]
+    (weight,) = call(stack_kernel, [((units * TPE, block), BF16)], *parts)
+    weights = [weight] + [swap(weight, k, "side") for k in range(1, sides)]
     other = swap(mine, 1)
     arrived = over_y(sent_b).reshape(rows, width)
     (hidden_a,) = call(
@@ -175,7 +185,8 @@
     )
     hiddens_b = [hidden_b] + [swap(hidden_b, k) for k in range(1, TPE)]
     (result,) = call(
-        down_kernel, [((groups, cap, quarter), BF16)], *hiddens_a, *hiddens_b, *weights,
+        down_kernel, [((groups, cap, quarter), BF16)],
+        place, *hiddens_a, *hiddens_b, *weights,
         flops=4 * rows * width * units, limit=room,
     )
     returned = over_y(result)

time: 170 us -> 166 us (0.976)
  the two profiles are of different devices: /device:TPU:6 before, /device:TPU:1 now
where the time goes in v4:
time: 166 us
  starting transfers between devices  68.1 us (41%)
  blocking collectives  60.4 us (36%)
  waiting for transfers between devices  17.2 us (10%)
  Pallas kernels  15.6 us (9%)
  local copies, waits for them, and re-layouts  3.14 us (2%)
    ppermute x16, starting transfers between devices, swap(): lax.ppermute(x, axis, [(i, i ^ bits) for i in range(lax.axis_size(axis))])  64.6 us
    all_to_all x2, blocking collectives, over_y(): lax.all_to_all(x.reshape(groups, -1, x.shape[-1]), 'grp', 0, 0, tiled=True)  60.4 us
    ppermute x16, waiting for transfers between devices, swap(): lax.ppermute(x, axis, [(i, i ^ bits) for i in range(lax.axis_size(axis))])  17.2 us
    pallas_call x8, Pallas kernels, call(): pl.pallas_call(kernel, out_shape=outs, in_specs=specs, out_specs=[pl.Bloc...  15.6 us
    all_to_all x1, starting transfers between devices, over_y(): lax.all_to_all(x.reshape(groups, -1, x.shape[-1]), 'grp', 0, 0, tiled=True)  3.55 us
  transfers between devices with their start and end apart: 17, of which 4 were waited for; matrix products, arithmetic and copies ran while one was open for 0% of the time, Pallas kernels for 6%

profile of v4, /device:TPU:1, one launch (start us, length us, event | category | flops | bytes accessed | tf_op | source)
XLA Modules:
  0.0 165.5 jit_solution(4589614938775953141)
XLA Ops:
  0.7 2.8 %shard_map.64 = (bf16[128,2048]{1,0:T(8,128)(2,1)}, bf16[128,64]{1,0:T(8,128)(2,1)}, bf16[128,64]{1,0:T(8,128)(2,1)}, bf16[128,4096]{1,0:T(8,128)(2,1)}, bf16[12...) custom-call(s32[4]{0:T(128)} %pad_add_fusion.place, s32[8,64]{1,0:T(8,128)} %bitcast.23, f32[8,64]{1,0:T(8,128)} %bitcast.24, ...), custom_call_target="tpu_custom_call" | custom-call | flops 100663296 | bytes 2166800 | tf_op jit(solution)/shard_map/pallas_call | solution.py:131
  3.4 34.8 %all_to_all.15 = bf16[16,8,2048]{2,1,0:T(8,128)(2,1)S(1)} all-to-all(bf16[16,8,2048]{2,1,0:T(8,128)(2,1)} %bitcast.22), channel_id=1, replica_groups=mesh['grp'=16,'shard'=16,'side'=4] {'grp'}, dimensions={0} | all-to-all | bytes 1048576 | tf_op jit(solution)/shard_map/all_to_all | solution.py:156
  38.2 3.6 %all-to-all-start.1 = ((bf16[16,8,4096]{2,1,0:T(8,128)(2,1)}), bf16[16,8,4096]{2,1,0:T(8,128)(2,1)S(1)}, u32[]{:S(2)}, u32[]{:S(2)}) async-start(bf16[16,8,4096]{2,1,0:T(8,128)(2,1)} %bitcast.21), calls=%async_computation.1 | async-start | bytes 2097152 | tf_op jit(solution)/shard_map/all_to_all | solution.py:156
  41.8 2.5 %shard_map.67 = (bf16[256,256]{1,0:T(8,128)(2,1)}, bf16[256,256]{1,0:T(8,128)(2,1)}, bf16[256,256]{1,0:T(8,128)(2,1)}, bf16[256,256]{1,0:T(8,128)(2,1)}) custom-call(s32[4]{0:T(128)} %pad_add_fusion.place, bf16[256,4096]{1,0:T(8,128)(2,1)} %bitcast.18), custom_call_target="tpu_custom_call" | custom-call | bytes 2621456 | tf_op jit(solution)/shard_map/pallas_call | solution.py:131
  44.3 1.9 %collective-permute-start.7 = (bf16[256,256]{1,0:T(8,128)(2,1)}, bf16[256,256]{1,0:T(8,128)(2,1)S(1)}, u32[]{:S(2)}, u32[]{:S(2)}) collective-permute-start(bf16[256,256]{1,0:T(8,128)(2,1)} %get-tuple-element.26), channel_id=1, source_target_pairs={{0,4},{4,0},{8,12},{12,8},{16,20},{20,16},{24,28},{28,24},{32,36},... | collective-permute-start | bytes 393224 | tf_op jit(solution)/shard_map/ppermute | solution.py:159
  46.2 1.9 %collective-permute-start.8 = (bf16[256,256]{1,0:T(8,128)(2,1)}, bf16[256,256]{1,0:T(8,128)(2,1)S(1)}, u32[]{:S(2)}, u32[]{:S(2)}) collective-permute-start(bf16[256,256]{1,0:T(8,128)(2,1)} %get-tuple-element.27), channel_id=1, source_target_pairs={{0,8},{4,12},{8,0},{12,4},{16,24},{20,28},{24,16},{28,20},{32,40},... | collective-permute-start | bytes 393224 | tf_op jit(solution)/shard_map/ppermute | solution.py:159
  48.1 5.4 %collective-permute-start.9 = (bf16[256,256]{1,0:T(8,128)(2,1)}, bf16[256,256]{1,0:T(8,128)(2,1)S(1)}, u32[]{:S(2)}, u32[]{:S(2)}) collective-permute-start(bf16[256,256]{1,0:T(8,128)(2,1)} %get-tuple-element.28), channel_id=1, source_target_pairs={{0,12},{4,8},{8,4},{12,0},{16,28},{20,24},{24,20},{28,16},{32,44},... | collective-permute-start | bytes 393224 | tf_op jit(solution)/shard_map/ppermute | solution.py:159
  53.5 1.9 %collective-permute-start = (bf16[128,2048]{1,0:T(8,128)(2,1)S(1)}, bf16[128,2048]{1,0:T(8,128)(2,1)S(1)}, u32[]{:S(2)}, u32[]{:S(2)}) collective-permute-start(bf16[128,2048]{1,0:T(8,128)(2,1)S(1)} %bitcast.19), channel_id=1, source_target_pairs={{0,4},{4,0},{8,12},{12,8},{16,20},{20,16},{24,28},{28,24},{32,36},... | collective-permute-start | bytes 1572872 | tf_op jit(solution)/shard_map/ppermute | solution.py:159
  55.5 4.9 %collective-permute-done.8.refs_2_ = bf16[256,256]{1,0:T(8,128)(2,1)S(1)} collective-permute-done((bf16[256,256]{1,0:T(8,128)(2,1)}, bf16[256,256]{1,0:T(8,128)(2,1)S(1)}, u32[]{:S(2)}, u32[]{:S(2)}) %collective-permute-start.8) | collective-permute-done | bytes 131104 | tf_op jit(solution)/shard_map/ppermute | solution.py:159
  61.1 1.9 %shard_map.68.refs_8_ = bf16[1024,256]{1,0:T(8,128)(2,1)} custom-call(bf16[256,256]{1,0:T(8,128)(2,1)} %get-tuple-element.25.refs_0_, bf16[256,256]{1,0:T(8,128)(2,1)} %copy-done.11, bf16[256,256]{1,0:T(8,128)(2,1)} %copy-done.12, bf16[256,256]{1,0:T(8,128)(2,1)} %copy-done.13), custom_call_target="tpu_custom_call" | custom-call | bytes 1048576 | tf_op jit(solution)/shard_map/pallas_call | solution.py:131
  63.0 1.9 %collective-permute-start.10 = (bf16[1024,256]{1,0:T(8,128)(2,1)}, bf16[1024,256]{1,0:T(8,128)(2,1)}, u32[]{:S(2)}, u32[]{:S(2)}) collective-permute-start(bf16[1024,256]{1,0:T(8,128)(2,1)} %shard_map.68.refs_8_), channel_id=1, source_target_pairs={{0,1},{1,0},{2,3},{3,2},{4,5},{5,4},{6,7},{7,6},{8,9},{9,8},{10,11... | collective-permute-start | bytes 1572872 | tf_op jit(solution)/shard_map/ppermute | solution.py:159
  64.9 1.9 %collective-permute-start.11 = (bf16[1024,256]{1,0:T(8,128)(2,1)}, bf16[1024,256]{1,0:T(8,128)(2,1)}, u32[]{:S(2)}, u32[]{:S(2)}) collective-permute-start(bf16[1024,256]{1,0:T(8,128)(2,1)} %shard_map.68.refs_8_), channel_id=1, source_target_pairs={{0,2},{1,3},{2,0},{3,1},{4,6},{5,7},{6,4},{7,5},{8,10},{9,11},{10,... | collective-permute-start | bytes 1572872 | tf_op jit(solution)/shard_map/ppermute | solution.py:159
  66.8 5.7 %collective-permute-start.12 = (bf16[1024,256]{1,0:T(8,128)(2,1)}, bf16[1024,256]{1,0:T(8,128)(2,1)}, u32[]{:S(2)}, u32[]{:S(2)}) collective-permute-start(bf16[1024,256]{1,0:T(8,128)(2,1)} %shard_map.68.refs_8_), channel_id=1, source_target_pairs={{0,3},{1,2},{2,1},{3,0},{4,7},{5,6},{6,5},{7,4},{8,11},{9,10},{10,... | collective-permute-start | bytes 1572872 | tf_op jit(solution)/shard_map/ppermute | solution.py:159
  72.6 0.8 copy-done.10
  73.4 4.1 %shard_map.65.refs_0_ = bf16[128,256]{1,0:T(8,128)(2,1)} custom-call(s32[4]{0:T(128)} %pad_add_fusion.place, bf16[128,2048]{1,0:T(8,128)(2,1)} %bitcast.20, bf16[128,2048]{1,0:T(8,128)(2,1)} %copy-done.10, bf16[4096,256]{1,0:T(8,128)(2,1)} %bitcast.13, bf16[4096,256]{1,0:T(8,128)(2,1)} %bitcast.15), custom_call_target="tpu_custom_call" | custom-call | flops 536870912 | bytes 5308432 | tf_op jit(solution)/shard_map/pallas_call | solution.py:131
  77.4 4.9 %collective-permute-start.1 = (bf16[128,256]{1,0:T(8,128)(2,1)}, bf16[128,256]{1,0:T(8,128)(2,1)S(1)}, u32[]{:S(2)}, u32[]{:S(2)}) collective-permute-start(bf16[128,256]{1,0:T(8,128)(2,1)} %shard_map.65.refs_0_), channel_id=1, source_target_pairs={{0,4},{4,0},{8,12},{12,8},{16,20},{20,16},{24,28},{28,24},{32,36},... | collective-permute-start | bytes 196616 | tf_op jit(solution)/shard_map/ppermute | solution.py:159
  82.3 1.9 %collective-permute-start.2 = (bf16[128,256]{1,0:T(8,128)(2,1)}, bf16[128,256]{1,0:T(8,128)(2,1)S(1)}, u32[]{:S(2)}, u32[]{:S(2)}) collective-permute-start(bf16[128,256]{1,0:T(8,128)(2,1)} %shard_map.65.refs_0_), channel_id=1, source_target_pairs={{0,8},{4,12},{8,0},{12,4},{16,24},{20,28},{24,16},{28,20},{32,40},... | collective-permute-start | bytes 196616 | tf_op jit(solution)/shard_map/ppermute | solution.py:159
  84.3 1.6 copy-done.1
  85.9 0.8 shard_map.66.refs_4_
  86.7 4.0 %collective-permute-start.3 = (bf16[128,256]{1,0:T(8,128)(2,1)S(1)}, bf16[128,256]{1,0:T(8,128)(2,1)S(1)}, u32[]{:S(2)}, u32[]{:S(2)}) collective-permute-start(bf16[128,256]{1,0:T(8,128)(2,1)S(1)} %copy-done.3), channel_id=1, source_target_pairs={{0,12},{4,8},{8,4},{12,0},{16,28},{20,24},{24,20},{28,16},{32,44},... | collective-permute-start | bytes 196616 | tf_op jit(solution)/shard_map/ppermute | solution.py:159
  90.7 2.5 %collective-permute-start.4 = (bf16[128,256]{1,0:T(8,128)(2,1)S(1)}, bf16[128,256]{1,0:T(8,128)(2,1)S(1)}, u32[]{:S(2)}, u32[]{:S(2)}) collective-permute-start(bf16[128,256]{1,0:T(8,128)(2,1)S(1)} %shard_map.66.refs_4_), channel_id=1, source_target_pairs={{0,4},{4,0},{8,12},{12,8},{16,20},{20,16},{24,28},{28,24},{32,36},... | collective-permute-start | bytes 196616 | tf_op jit(solution)/shard_map/ppermute | solution.py:159
  93.2 2.5 %collective-permute-done.12.refs_11_ = bf16[1024,256]{1,0:T(8,128)(2,1)} collective-permute-done((bf16[1024,256]{1,0:T(8,128)(2,1)}, bf16[1024,256]{1,0:T(8,128)(2,1)}, u32[]{:S(2)}, u32[]{:S(2)}) %collective-permute-start.12) | collective-permute-done | bytes 524320 | tf_op jit(solution)/shard_map/ppermute | solution.py:159
  95.7 4.7 %collective-permute-start.5 = (bf16[128,256]{1,0:T(8,128)(2,1)S(1)}, bf16[128,256]{1,0:T(8,128)(2,1)S(1)}, u32[]{:S(2)}, u32[]{:S(2)}) collective-permute-start(bf16[128,256]{1,0:T(8,128)(2,1)S(1)} %shard_map.66.refs_4_), channel_id=1, source_target_pairs={{0,8},{4,12},{8,0},{12,4},{16,24},{20,28},{24,16},{28,20},{32,40},... | collective-permute-start | bytes 196616 | tf_op jit(solution)/shard_map/ppermute | solution.py:159
  100.4 4.0 %collective-permute-start.6 = (bf16[128,256]{1,0:T(8,128)(2,1)S(1)}, bf16[128,256]{1,0:T(8,128)(2,1)S(1)}, u32[]{:S(2)}, u32[]{:S(2)}) collective-permute-start(bf16[128,256]{1,0:T(8,128)(2,1)S(1)} %shard_map.66.refs_4_), channel_id=1, source_target_pairs={{0,12},{4,8},{8,4},{12,0},{16,28},{20,24},{24,20},{28,16},{32,44},... | collective-permute-start | bytes 196616 | tf_op jit(solution)/shard_map/ppermute | solution.py:159
  104.5 2.8 %collective-permute-done.6.refs_7_ = bf16[128,256]{1,0:T(8,128)(2,1)S(1)} collective-permute-done((bf16[128,256]{1,0:T(8,128)(2,1)S(1)}, bf16[128,256]{1,0:T(8,128)(2,1)S(1)}, u32[]{:S(2)}, u32[]{:S(2)}) %collective-permute-start.6) | collective-permute-done | bytes 65568 | tf_op jit(solution)/shard_map/ppermute | solution.py:159
  107.3 2.1 %shard_map.69 = bf16[16,16,1024]{2,1,0:T(8,128)(2,1)S(1)} custom-call(s32[4]{0:T(128)S(1)} %copy-done.8, bf16[128,256]{1,0:T(8,128)(2,1)S(1)} %copy-done.3, bf16[128,256]{1,0:T(8,128)(2,1)S(1)} %collective-permute-done.1.refs_1_, bf16[128,256]{1,0:T(8,128)(2,1)S(1)} %collective-permute-done.2.refs_2_, bf16[128,256]{1,0:T(8,128)(2,1)S(1)} %collective-permute-done.3.refs_3_, ...), custom_call_target="tpu_custom_call" | custom-call | flops 536870912 | bytes 3145744 | tf_op jit(solution)/shard_map/pallas_call | solution.py:131
  109.4 25.6 %all_to_all.16.rows = bf16[16,16,1024]{2,1,0:T(8,128)(2,1)S(1)} all-to-all(bf16[16,16,1024]{2,1,0:T(8,128)(2,1)S(1)} %shard_map.69), channel_id=1, replica_groups=mesh['grp'=16,'shard'=16,'side'=4] {'grp'}, dimensions={0} | all-to-all | bytes 1048576 | tf_op jit(solution)/shard_map/all_to_all | solution.py:156
  135.1 0.9 shard_map.70
  135.9 8.3 %collective-permute-start.13 = (bf16[64,256]{1,0:T(8,128)(2,1)S(1)}, bf16[64,256]{1,0:T(8,128)(2,1)S(1)}, u32[]{:S(2)}, u32[]{:S(2)}) collective-permute-start(bf16[64,256]{1,0:T(8,128)(2,1)S(1)} %get-tuple-element.30), channel_id=1, source_target_pairs={{0,16},{4,20},{8,24},{12,28},{16,0},{20,4},{24,8},{28,12},{32,48},... | collective-permute-start | bytes 98312 | tf_op jit(solution)/shard_map/ppermute | solution.py:159
  144.3 11.7 %collective-permute-start.14 = (bf16[64,256]{1,0:T(8,128)(2,1)S(1)}, bf16[64,256]{1,0:T(8,128)(2,1)S(1)}, u32[]{:S(2)}, u32[]{:S(2)}) collective-permute-start(bf16[64,256]{1,0:T(8,128)(2,1)S(1)} %get-tuple-element.31), channel_id=1, source_target_pairs={{0,32},{4,36},{8,40},{12,44},{16,48},{20,52},{24,56},{28,60},{32,0... | collective-permute-start | bytes 98312 | tf_op jit(solution)/shard_map/ppermute | solution.py:159
  155.9 1.9 %collective-permute-start.15 = (bf16[64,256]{1,0:T(8,128)(2,1)S(1)}, bf16[64,256]{1,0:T(8,128)(2,1)S(1)}, u32[]{:S(2)}, u32[]{:S(2)}) collective-permute-start(bf16[64,256]{1,0:T(8,128)(2,1)S(1)} %get-tuple-element.32), channel_id=1, source_target_pairs={{0,48},{4,52},{8,56},{12,60},{16,32},{20,36},{24,40},{28,44},{32,1... | collective-permute-start | bytes 98312 | tf_op jit(solution)/shard_map/ppermute | solution.py:159
  157.9 7.0 %collective-permute-done.15.refs_2_ = bf16[64,256]{1,0:T(8,128)(2,1)S(1)} collective-permute-done((bf16[64,256]{1,0:T(8,128)(2,1)S(1)}, bf16[64,256]{1,0:T(8,128)(2,1)S(1)}, u32[]{:S(2)}, u32[]{:S(2)}) %collective-permute-start.15) | collective-permute-done | bytes 32800 | tf_op jit(solution)/shard_map/ppermute | solution.py:159
  (41 shorter events, 2.1 us)
Async XLA Ops:
  38.2 15.3 %copy-start.9 = (bf16[16,8,2048]{2,1,0:T(8,128)(2,1)}, bf16[16,8,2048]{2,1,0:T(8,128)(2,1)S(1)}, u32[]{:S(2)}) copy-start(bf16[16,8,2048]{2,1,0:T(8,128)(2,1)S(1)} %all_to_all.15) | copy-start | bytes 1572868
  38.2 46.0 %all-to-all-start.1 = ((bf16[16,8,4096]{2,1,0:T(8,128)(2,1)}), bf16[16,8,4096]{2,1,0:T(8,128)(2,1)S(1)}, u32[]{:S(2)}, u32[]{:S(2)}) async-start(bf16[16,8,4096]{2,1,0:T(8,128)(2,1)} %bitcast.21), calls=%async_computation.1 | async-start | bytes 2097152 | tf_op jit(solution)/shard_map/all_to_all | solution.py:156
  44.3 11.2 %collective-permute-start.7 = (bf16[256,256]{1,0:T(8,128)(2,1)}, bf16[256,256]{1,0:T(8,128)(2,1)S(1)}, u32[]{:S(2)}, u32[]{:S(2)}) collective-permute-start(bf16[256,256]{1,0:T(8,128)(2,1)} %get-tuple-element.26), channel_id=1, source_target_pairs={{0,4},{4,0},{8,12},{12,8},{16,20},{20,16},{24,28},{28,24},{32,36},... | collective-permute-start | bytes 393224 | tf_op jit(solution)/shard_map/ppermute | solution.py:159
  46.2 14.2 %collective-permute-start.8 = (bf16[256,256]{1,0:T(8,128)(2,1)}, bf16[256,256]{1,0:T(8,128)(2,1)S(1)}, u32[]{:S(2)}, u32[]{:S(2)}) collective-permute-start(bf16[256,256]{1,0:T(8,128)(2,1)} %get-tuple-element.27), channel_id=1, source_target_pairs={{0,8},{4,12},{8,0},{12,4},{16,24},{20,28},{24,16},{28,20},{32,40},... | collective-permute-start | bytes 393224 | tf_op jit(solution)/shard_map/ppermute | solution.py:159
  48.1 12.3 %collective-permute-start.9 = (bf16[256,256]{1,0:T(8,128)(2,1)}, bf16[256,256]{1,0:T(8,128)(2,1)S(1)}, u32[]{:S(2)}, u32[]{:S(2)}) collective-permute-start(bf16[256,256]{1,0:T(8,128)(2,1)} %get-tuple-element.28), channel_id=1, source_target_pairs={{0,12},{4,8},{8,4},{12,0},{16,28},{20,24},{24,20},{28,16},{32,44},... | collective-permute-start | bytes 393224 | tf_op jit(solution)/shard_map/ppermute | solution.py:159
  53.5 19.0 %collective-permute-start = (bf16[128,2048]{1,0:T(8,128)(2,1)S(1)}, bf16[128,2048]{1,0:T(8,128)(2,1)S(1)}, u32[]{:S(2)}, u32[]{:S(2)}) collective-permute-start(bf16[128,2048]{1,0:T(8,128)(2,1)S(1)} %bitcast.19), channel_id=1, source_target_pairs={{0,4},{4,0},{8,12},{12,8},{16,20},{20,16},{24,28},{28,24},{32,36},... | collective-permute-start | bytes 1572872 | tf_op jit(solution)/shard_map/ppermute | solution.py:159
  55.5 4.9 %copy-start.11 = (bf16[256,256]{1,0:T(8,128)(2,1)}, bf16[256,256]{1,0:T(8,128)(2,1)S(1)}, u32[]{:S(2)}) copy-start(bf16[256,256]{1,0:T(8,128)(2,1)S(1)} %collective-permute-done.7.refs_1_) | copy-start | bytes 393220
  60.3 0.7 copy-start.12
  60.4 0.7 copy-start.13
  63.0 23.7 %collective-permute-start.10 = (bf16[1024,256]{1,0:T(8,128)(2,1)}, bf16[1024,256]{1,0:T(8,128)(2,1)}, u32[]{:S(2)}, u32[]{:S(2)}) collective-permute-start(bf16[1024,256]{1,0:T(8,128)(2,1)} %shard_map.68.refs_8_), channel_id=1, source_target_pairs={{0,1},{1,0},{2,3},{3,2},{4,5},{5,4},{6,7},{7,6},{8,9},{9,8},{10,11... | collective-permute-start | bytes 1572872 | tf_op jit(solution)/shard_map/ppermute | solution.py:159
  64.9 25.8 %collective-permute-start.11 = (bf16[1024,256]{1,0:T(8,128)(2,1)}, bf16[1024,256]{1,0:T(8,128)(2,1)}, u32[]{:S(2)}, u32[]{:S(2)}) collective-permute-start(bf16[1024,256]{1,0:T(8,128)(2,1)} %shard_map.68.refs_8_), channel_id=1, source_target_pairs={{0,2},{1,3},{2,0},{3,1},{4,6},{5,7},{6,4},{7,5},{8,10},{9,11},{10,... | collective-permute-start | bytes 1572872 | tf_op jit(solution)/shard_map/ppermute | solution.py:159
  66.8 28.9 %collective-permute-start.12 = (bf16[1024,256]{1,0:T(8,128)(2,1)}, bf16[1024,256]{1,0:T(8,128)(2,1)}, u32[]{:S(2)}, u32[]{:S(2)}) collective-permute-start(bf16[1024,256]{1,0:T(8,128)(2,1)} %shard_map.68.refs_8_), channel_id=1, source_target_pairs={{0,3},{1,2},{2,1},{3,0},{4,7},{5,6},{6,5},{7,4},{8,11},{9,10},{10,... | collective-permute-start | bytes 1572872 | tf_op jit(solution)/shard_map/ppermute | solution.py:159
  72.6 0.8 copy-start.10
  73.4 10.9 %copy-start = (bf16[1,4096,256]{2,1,0:T(8,128)(2,1)S(1)}, bf16[1,4096,256]{2,1,0:T(8,128)(2,1)}, u32[]{:S(2)}) copy-start(bf16[1,4096,256]{2,1,0:T(8,128)(2,1)} %param.9) | copy-start | bytes 6291460
  77.4 22.9 %collective-permute-start.1 = (bf16[128,256]{1,0:T(8,128)(2,1)}, bf16[128,256]{1,0:T(8,128)(2,1)S(1)}, u32[]{:S(2)}, u32[]{:S(2)}) collective-permute-start(bf16[128,256]{1,0:T(8,128)(2,1)} %shard_map.65.refs_0_), channel_id=1, source_target_pairs={{0,4},{4,0},{8,12},{12,8},{16,20},{20,16},{24,28},{28,24},{32,36},... | collective-permute-start | bytes 196616 | tf_op jit(solution)/shard_map/ppermute | solution.py:159
  82.3 22.1 %collective-permute-start.2 = (bf16[128,256]{1,0:T(8,128)(2,1)}, bf16[128,256]{1,0:T(8,128)(2,1)S(1)}, u32[]{:S(2)}, u32[]{:S(2)}) collective-permute-start(bf16[128,256]{1,0:T(8,128)(2,1)} %shard_map.65.refs_0_), channel_id=1, source_target_pairs={{0,8},{4,12},{8,0},{12,4},{16,24},{20,28},{24,16},{28,20},{32,40},... | collective-permute-start | bytes 196616 | tf_op jit(solution)/shard_map/ppermute | solution.py:159
  84.3 1.6 copy-start.1
  85.9 0.8 copy-start.3
  85.9 21.4 %copy-start.2 = (bf16[1024,256]{1,0:T(8,128)(2,1)S(1)}, bf16[1024,256]{1,0:T(8,128)(2,1)}, u32[]{:S(2)}) copy-start(bf16[1024,256]{1,0:T(8,128)(2,1)} %shard_map.68.refs_8_) | copy-start | bytes 1572868
  85.9 21.4 %copy-start.8 = (s32[4]{0:T(128)S(1)}, s32[4]{0:T(128)}, u32[]{:S(2)}) copy-start(s32[4]{0:T(128)} %pad_add_fusion.place) | copy-start | bytes 52
  86.6 48.4 %copy-start.4 = (bf16[128,64]{1,0:T(8,128)(2,1)S(1)}, bf16[128,64]{1,0:T(8,128)(2,1)}, u32[]{:S(2)}) copy-start(bf16[128,64]{1,0:T(8,128)(2,1)} %get-tuple-element.19.high_a) | copy-start | bytes 49156
  86.6 48.4 %copy-start.5 = (bf16[128,64]{1,0:T(8,128)(2,1)S(1)}, bf16[128,64]{1,0:T(8,128)(2,1)}, u32[]{:S(2)}) copy-start(bf16[128,64]{1,0:T(8,128)(2,1)} %get-tuple-element.20.low_a) | copy-start | bytes 49156
  86.6 48.4 %copy-start.6 = (bf16[128,64]{1,0:T(8,128)(2,1)S(1)}, bf16[128,64]{1,0:T(8,128)(2,1)}, u32[]{:S(2)}) copy-start(bf16[128,64]{1,0:T(8,128)(2,1)} %get-tuple-element.21.high_b) | copy-start | bytes 49156
  86.6 48.4 %copy-start.7 = (bf16[128,64]{1,0:T(8,128)(2,1)S(1)}, bf16[128,64]{1,0:T(8,128)(2,1)}, u32[]{:S(2)}) copy-start(bf16[128,64]{1,0:T(8,128)(2,1)} %get-tuple-element.22.low_b) | copy-start | bytes 49156
  86.7 17.7 %collective-permute-start.3 = (bf16[128,256]{1,0:T(8,128)(2,1)S(1)}, bf16[128,256]{1,0:T(8,128)(2,1)S(1)}, u32[]{:S(2)}, u32[]{:S(2)}) collective-permute-start(bf16[128,256]{1,0:T(8,128)(2,1)S(1)} %copy-done.3), channel_id=1, source_target_pairs={{0,12},{4,8},{8,4},{12,0},{16,28},{20,24},{24,20},{28,16},{32,44},... | collective-permute-start | bytes 196616 | tf_op jit(solution)/shard_map/ppermute | solution.py:159
  90.7 13.8 %collective-permute-start.4 = (bf16[128,256]{1,0:T(8,128)(2,1)S(1)}, bf16[128,256]{1,0:T(8,128)(2,1)S(1)}, u32[]{:S(2)}, u32[]{:S(2)}) collective-permute-start(bf16[128,256]{1,0:T(8,128)(2,1)S(1)} %shard_map.66.refs_4_), channel_id=1, source_target_pairs={{0,4},{4,0},{8,12},{12,8},{16,20},{20,16},{24,28},{28,24},{32,36},... | collective-permute-start | bytes 196616 | tf_op jit(solution)/shard_map/ppermute | solution.py:159
  95.7 8.8 %collective-permute-start.5 = (bf16[128,256]{1,0:T(8,128)(2,1)S(1)}, bf16[128,256]{1,0:T(8,128)(2,1)S(1)}, u32[]{:S(2)}, u32[]{:S(2)}) collective-permute-start(bf16[128,256]{1,0:T(8,128)(2,1)S(1)} %shard_map.66.refs_4_), channel_id=1, source_target_pairs={{0,8},{4,12},{8,0},{12,4},{16,24},{20,28},{24,16},{28,20},{32,40},... | collective-permute-start | bytes 196616 | tf_op jit(solution)/shard_map/ppermute | solution.py:159
  100.4 6.9 %collective-permute-start.6 = (bf16[128,256]{1,0:T(8,128)(2,1)S(1)}, bf16[128,256]{1,0:T(8,128)(2,1)S(1)}, u32[]{:S(2)}, u32[]{:S(2)}) collective-permute-start(bf16[128,256]{1,0:T(8,128)(2,1)S(1)} %shard_map.66.refs_4_), channel_id=1, source_target_pairs={{0,12},{4,8},{8,4},{12,0},{16,28},{20,24},{24,20},{28,16},{32,44},... | collective-permute-start | bytes 196616 | tf_op jit(solution)/shard_map/ppermute | solution.py:159
  135.9 21.9 %collective-permute-start.13 = (bf16[64,256]{1,0:T(8,128)(2,1)S(1)}, bf16[64,256]{1,0:T(8,128)(2,1)S(1)}, u32[]{:S(2)}, u32[]{:S(2)}) collective-permute-start(bf16[64,256]{1,0:T(8,128)(2,1)S(1)} %get-tuple-element.30), channel_id=1, source_target_pairs={{0,16},{4,20},{8,24},{12,28},{16,0},{20,4},{24,8},{28,12},{32,48},... | collective-permute-start | bytes 98312 | tf_op jit(solution)/shard_map/ppermute | solution.py:159
  144.3 13.6 %collective-permute-start.14 = (bf16[64,256]{1,0:T(8,128)(2,1)S(1)}, bf16[64,256]{1,0:T(8,128)(2,1)S(1)}, u32[]{:S(2)}, u32[]{:S(2)}) collective-permute-start(bf16[64,256]{1,0:T(8,128)(2,1)S(1)} %get-tuple-element.31), channel_id=1, source_target_pairs={{0,32},{4,36},{8,40},{12,44},{16,48},{20,52},{24,56},{28,60},{32,0... | collective-permute-start | bytes 98312 | tf_op jit(solution)/shard_map/ppermute | solution.py:159
  155.9 8.9 %collective-permute-start.15 = (bf16[64,256]{1,0:T(8,128)(2,1)S(1)}, bf16[64,256]{1,0:T(8,128)(2,1)S(1)}, u32[]{:S(2)}, u32[]{:S(2)}) collective-permute-start(bf16[64,256]{1,0:T(8,128)(2,1)S(1)} %get-tuple-element.32), channel_id=1, source_target_pairs={{0,48},{4,52},{8,56},{12,60},{16,32},{20,36},{24,40},{28,44},{32,1... | collective-permute-start | bytes 98312 | tf_op jit(solution)/shard_map/ppermute | solution.py:159

commit v5 on v4

v5 whole, which is shorter than its diff:
```python
import functools

import jax
import jax.numpy as jnp
from jax import lax
from jax.experimental import pallas as pl
from jax.experimental.pallas import tpu as pltpu
from jax.sharding import PartitionSpec as P


TPE = 4
BF16 = jnp.bfloat16
F32 = jnp.float32


def dot(a, b, dims=((1,), (0,))):
    return lax.dot_general(a, b, (dims, ((), ())), preferred_element_type=F32)


def unpack(place):
    z = lax.shift_right_logical(place[0], 2)
    quartet, tile = lax.shift_right_logical(z, 2), lax.bitwise_and(z, 3)
    return quartet, tile, lax.bitwise_and(z, 1), lax.bitwise_and(place[0], 3)


def dispatch_kernel(cap, per_group, part, place, routes, probs, tokens, sent, high, low):
    tok = tokens.shape[0]
    rows, width = sent.shape
    half = cap // 2
    gates = probs[...] / jnp.sum(probs[...], axis=0, keepdims=True)
    before = lax.broadcasted_iota(jnp.int32, (tok, tok), 0)
    before = before < lax.broadcasted_iota(jnp.int32, (tok, tok), 1)
    before = jnp.where(before, F32(1.0), F32(0.0)).astype(BF16)
    row = lax.broadcasted_iota(jnp.int32, (rows, tok), 0)
    target = lax.shift_right_logical(row, half.bit_length() - 1) * per_group + unpack(place)[0]
    slot = (lax.bitwise_and(row, half - 1) + part * half).astype(F32)
    hits = jnp.zeros((rows, tok), F32)
    weight = jnp.zeros((rows, tok), F32)
    for k in range(routes.shape[0]):
        match = routes[k : k + 1, :] == target
        hits = jnp.where(match, F32(1.0), hits)
        weight = jnp.where(match, gates[k : k + 1, :], weight)
    ranks = dot(hits.astype(BF16), before)
    chosen = (hits > 0.5) & (ranks == slot)
    select = jnp.where(chosen, F32(1.0), F32(0.0)).astype(BF16)
    mine = jnp.where(chosen, weight, F32(0.0))
    top = mine.astype(BF16)
    high[...] = top
    low[...] = (mine - top.astype(F32)).astype(BF16)
    step = min(512, width)
    for at in range(0, width, step):
        start = unpack(place)[2] * width + at if part == 0 else at
        piece = tokens[:, pl.ds(pl.multiple_of(start, step), step)]
        sent[:, at : at + step] = dot(select, piece).astype(BF16)


def shuffle_kernel(block, place, weights, *outs):
    for k, out in enumerate(outs):
        at = unpack(place)[3] * TPE + lax.bitwise_xor(unpack(place)[1], k)
        out[...] = weights[:, pl.ds(pl.multiple_of(at * block, block), block)]


def stack_kernel(*refs):
    size = refs[0].shape[0]
    for k, ref in enumerate(refs[:-1]):
        refs[-1][k * size : (k + 1) * size, :] = ref[...]


def activate(gate, upper):
    return (gate / (1.0 + jnp.exp(-gate)) * upper).astype(BF16)


def hidden_kernel(count, place, *refs):
    rows, w_gate, w_up = refs[:count], refs[count : 2 * count], refs[2 * count : 3 * count]
    out, gate, upper = refs[3 * count :]
    step = pl.program_id(0)
    if count == 1:
        size = w_gate[0].shape[0]
        piece = rows[0][:, pl.ds(pl.multiple_of(step * size, size), size)]
        gates, uppers = dot(piece, w_gate[0][...]), dot(piece, w_up[0][...])
    else:
        gates = dot(rows[0][...], w_gate[0][...]) + dot(rows[1][...], w_gate[1][...])
        uppers = dot(rows[0][...], w_up[0][...]) + dot(rows[1][...], w_up[1][...])

    @pl.when(step == 0)
    def _():
        gate[...] = gates
        upper[...] = uppers

    @pl.when(step > 0)
    def _():
        gate[...] += gates
        upper[...] += uppers

    @pl.when(step == pl.num_programs(0) - 1)
    def _():
        out[...] = activate(gate[...], upper[...])


def gate_up(place, rows, w_gate, w_up, steps=4):
    count, (height, width) = len(rows), rows[0].shape
    units, step = w_gate.shape[1], width // steps

    def near(i, place):
        return (i + steps * unpack(place)[2] if count == 2 else i, 0)

    def far(i, place):
        return (i + steps * (1 - unpack(place)[2]), 0)

    maps = [near, far][:count]
    row_spec = pl.BlockSpec((height, step), lambda i, place: (0, i))
    if count == 1:
        row_spec = pl.BlockSpec(memory_space=pltpu.VMEM)
        rows = [pltpu.with_memory_space_constraint(rows[0], pltpu.VMEM)]
    return pl.pallas_call(
        functools.partial(hidden_kernel, count),
        out_shape=jax.ShapeDtypeStruct((height, units), BF16),
        grid_spec=pltpu.PrefetchScalarGridSpec(
            num_scalar_prefetch=1,
            grid=(steps,),
            in_specs=[row_spec] * count
            + [pl.BlockSpec((step, units), m) for m in maps] * 2,
            out_specs=pl.BlockSpec(memory_space=pltpu.VMEM),
            scratch_shapes=[pltpu.VMEM((height, units), F32)] * 2,
        ),
        cost_estimate=pl.CostEstimate(
            flops=4 * height * units * w_gate.shape[0],
            bytes_accessed=4 * w_gate.size,
            transcendentals=height * units,
        ),
    )(place, *rows, *[w_gate] * count, *[w_up] * count)


def down_kernel(place, hidden, *refs):
    weights, out = refs[:-1], refs[-1]
    groups, cap, _ = out.shape
    block = weights[0].shape[1]
    count, height, units = hidden.shape
    _, tile, _, own_side = unpack(place)
    for side, weight in enumerate(weights):
        total = jnp.zeros((height, block), F32)
        for k in range(count):
            rows = hidden[lax.bitwise_xor(tile, k)]
            total = total + dot(rows, weight[k * units : (k + 1) * units, :])
        at = pl.multiple_of(lax.bitwise_xor(own_side, side) * block, block)
        total = total.reshape(2, groups, cap // 2, block).astype(BF16)
        for part in range(2):
            slots = slice(part * cap // 2, (part + 1) * cap // 2)
            out[:, slots, pl.ds(at, block)] = total[part]


def combine_kernel(high_a, low_a, high_b, low_b, rows, out):
    count, tok, block = out.shape
    groups, cap, _ = rows.shape
    for k in range(count):
        total = jnp.zeros((tok, block), F32)
        for part, pair in enumerate(((high_a, low_a), (high_b, low_b))):
            slots = slice(part * cap // 2, (part + 1) * cap // 2)
            piece = rows[:, slots, k * block : (k + 1) * block].astype(F32)
            piece = piece.reshape(groups * cap // 2, block).astype(BF16)
            for factor in pair:
                total = total + dot(factor[...], piece, ((0,), (0,)))
        out[k] = total.astype(BF16)


def finish_kernel(parts, out):
    total = parts[0].astype(F32)
    for k in range(1, parts.shape[0]):
        total = total + parts[k].astype(F32)
    out[...] = total.astype(BF16)


def call(kernel, shapes, *args, flops=0, limit=None):
    specs = [pl.BlockSpec(memory_space=pltpu.VMEM)] * len(args)
    if args[0].ndim == 1:
        specs[0] = pl.BlockSpec(memory_space=pltpu.SMEM)
    outs = [jax.ShapeDtypeStruct(s, d) for s, d in shapes]
    moved = sum(a.size * a.dtype.itemsize for a in (*args, *outs))
    return pl.pallas_call(
        kernel,
        out_shape=outs,
        in_specs=specs,
        out_specs=[pl.BlockSpec(memory_space=pltpu.VMEM)] * len(outs),
        compiler_params=pltpu.CompilerParams(vmem_limit_bytes=limit),
        cost_estimate=pl.CostEstimate(flops=flops, bytes_accessed=moved, transcendentals=0),
    )(*args)


def on_device(tokens, routes, probs, w_gate, w_up, w_down):
    groups, shards = lax.axis_size("grp"), lax.axis_size("shard")
    per_group = shards // TPE
    tok, width = tokens.shape
    units = w_down.shape[1]
    block, quarter = width // shards, width // TPE
    cap = 2 * tok * routes.shape[1] // (groups * per_group)
    rows = groups * cap // 2
    room = 16 << 20
    z = lax.axis_index("shard")
    sides = lax.axis_size("side")
    place = (z * TPE + lax.axis_index("side")).astype(jnp.int32).reshape(1)

    def over_y(x):
        return lax.all_to_all(x.reshape(groups, -1, x.shape[-1]), "grp", 0, 0, tiled=True)

    def swap(x, bits, axis="shard"):
        return lax.ppermute(x, axis, [(i, i ^ bits) for i in range(lax.axis_size(axis))])

    factor = ((rows, tok), BF16)

    def dispatch(part, size):
        return call(
            functools.partial(dispatch_kernel, cap, per_group, part),
            [((rows, size), BF16), factor, factor],
            place, routes.T, probs.T, tokens, flops=2 * rows * tok * size,
        )

    sent_a, high_a, low_a = dispatch(0, width // 2)
    mine = over_y(sent_a).reshape(rows, width // 2)
    sent_b, high_b, low_b = dispatch(1, width)
    parts = call(
        functools.partial(shuffle_kernel, block),
        [((units, block), BF16)] * TPE, place, w_down[0],
    )
    parts = [parts[0]] + [swap(parts[k], k) for k in range(1, TPE)]
    (weight,) = call(stack_kernel, [((units * TPE, block), BF16)], *parts)
    weights = [weight] + [swap(weight, k, "side") for k in range(1, sides)]
    other = swap(mine, 1)
    arrived = over_y(sent_b).reshape(rows, width)
    hidden_a = gate_up(place, [mine, other], w_gate[0], w_up[0])
    hidden_b = gate_up(place, [arrived], w_gate[0], w_up[0])
    quartets = [[i * TPE + k for k in range(TPE)] for i in range(per_group)]
    strided = [[i * TPE + k for i in range(per_group)] for k in range(TPE)]
    hidden = jnp.concatenate([hidden_a, hidden_b], axis=0)
    hidden = lax.all_gather(hidden, "shard", axis_index_groups=quartets)
    (result,) = call(
        down_kernel, [((groups, cap, quarter), BF16)], place, hidden, *weights,
        flops=4 * rows * width * units, limit=room,
    )
    returned = over_y(result)
    (parts,) = call(
        combine_kernel, [((per_group, tok, block), BF16)],
        high_a, low_a, high_b, low_b, returned, limit=room,
    )
    parts = lax.all_to_all(parts, "shard", 0, 0, tiled=True, axis_index_groups=strided)
    (mixed,) = call(finish_kernel, [((tok, block), BF16)], parts, limit=room)
    return mixed


def solution(mesh):
    return jax.shard_map(
        on_device,
        mesh=mesh,
        in_specs=(
            P(("grp", "side"), None),
            P(("grp", "side"), None),
            P(("grp", "side"), None),
            P(("grp", "shard"), None, None),
            P(("grp", "shard"), None, None),
            P(("grp", "shard"), None, None),
        ),
        out_specs=P(("grp", "side"), "shard"),
        check_vma=False,
    )
```

time: 166 us -> 155 us (0.934)
  starting transfers between devices: 68.1 us -> 41.8 us
  waiting for transfers between devices: 17.2 us -> 25.9 us
  blocking collectives: 60.4 us -> 65.3 us
  Pallas kernels: 15.6 us -> 19.7 us
  local copies, waits for them, and re-layouts: 3.14 us -> 0.75 us
    ppermute x16 -> x7, starting transfers between devices: 64.6 us -> 20.8 us  [swap(): lax.ppermute(x, axis, [(i, i ^ bits) for i in range(lax.axis_size(axis))])]
    all_to_all x2 -> x1, blocking collectives: 60.4 us -> 27.2 us  [over_y(): lax.all_to_all(x.reshape(groups, -1, x.shape[-1]), 'grp', 0, 0, tiled=True)]
    all_to_all x0 -> x1, blocking collectives: none -> 25.6 us  [on_device(): lax.all_to_all(parts, 'shard', 0, 0, tiled=True, axis_index_groups=strided)]
    all_to_all x1 -> x2, starting transfers between devices: 3.55 us -> 21 us  [over_y(): lax.all_to_all(x.reshape(groups, -1, x.shape[-1]), 'grp', 0, 0, tiled=True)]
    all_to_all x1 -> x2, waiting for transfers between devices: 0.01 us -> 14.7 us  [over_y(): lax.all_to_all(x.reshape(groups, -1, x.shape[-1]), 'grp', 0, 0, tiled=True)]
    all_gather x0 -> x1, blocking collectives: none -> 12.6 us  [on_device(): hidden = lax.all_gather(hidden, 'shard', axis_index_groups=quartets)]
    pallas_call x0 -> x2, Pallas kernels: none -> 8.71 us  [gate_up(): pl.pallas_call(functools.partial(hidden_kernel, count), out_shape=jax.Sha...]
    ppermute x16 -> x7, waiting for transfers between devices: 17.2 us -> 11.2 us  [swap(): lax.ppermute(x, axis, [(i, i ^ bits) for i in range(lax.axis_size(axis))])]
  transfers between devices with their start and end apart: 17 -> 9, of which waited for: 4 -> 3; matrix products, arithmetic and copies ran while one was open for 0% -> 1% of each run, Pallas kernels for 6% -> 10%
where the time goes in v5:
time: 155 us; the launch traced here: 154 us
  blocking collectives  65.3 us (42%)
  starting transfers between devices  41.8 us (27%)
  waiting for transfers between devices  25.9 us (17%)
  Pallas kernels  19.7 us (13%)
    all_to_all x1, blocking collectives, over_y(): lax.all_to_all(x.reshape(groups, -1, x.shape[-1]), 'grp', 0, 0, tiled=True)  27.2 us
    all_to_all x1, blocking collectives, on_device(): lax.all_to_all(parts, 'shard', 0, 0, tiled=True, axis_index_groups=strided)  25.6 us
    all_to_all x2, starting transfers between devices, over_y(): lax.all_to_all(x.reshape(groups, -1, x.shape[-1]), 'grp', 0, 0, tiled=True)  21 us
    ppermute x7, starting transfers between devices, swap(): lax.ppermute(x, axis, [(i, i ^ bits) for i in range(lax.axis_size(axis))])  20.8 us
    all_to_all x2, waiting for transfers between devices, over_y(): lax.all_to_all(x.reshape(groups, -1, x.shape[-1]), 'grp', 0, 0, tiled=True)  14.7 us
    all_gather x1, blocking collectives, on_device(): hidden = lax.all_gather(hidden, 'shard', axis_index_groups=quartets)  12.6 us
    ppermute x7, waiting for transfers between devices, swap(): lax.ppermute(x, axis, [(i, i ^ bits) for i in range(lax.axis_size(axis))])  11.2 us
    pallas_call x7, Pallas kernels, call(): pl.pallas_call(kernel, out_shape=outs, in_specs=specs, out_specs=[pl.Bloc...  11 us
  transfers between devices with their start and end apart: 9, of which 3 were waited for; matrix products, arithmetic and copies ran while one was open for 1% of the time, Pallas kernels for 10%

profile of v5, /device:TPU:1, one launch (start us, length us, event | category | flops | bytes accessed | tf_op | source)
XLA Modules:
  0.0 154.5 jit_solution(12942405901661998467)
XLA Ops:
  0.0 2.3 %shard_map.64 = (bf16[128,2048]{1,0:T(8,128)(2,1)}, bf16[128,64]{1,0:T(8,128)(2,1)}, bf16[128,64]{1,0:T(8,128)(2,1)}) custom-call(s32[1]{0:T(128)} %bitcast.place, s32[8,64]{1,0:T(8,128)} %bitcast.24, f32[8,64]{1,0:T(8,128)} %bitcast.26, bf16[64,4096]{1,0:T(8,128)(2,1)} %tokens.3), custom_call_target="tpu_custom_call" | custom-call | flops 33554432 | bytes 1085444 | tf_op jit(solution)/shard_map/pallas_call | solution.py:179
  2.3 17.5 %all-to-all-start = ((bf16[16,8,2048]{2,1,0:T(8,128)(2,1)}), bf16[16,8,2048]{2,1,0:T(8,128)(2,1)S(1)}, u32[]{:S(2)}, u32[]{:S(2)}) async-start(bf16[16,8,2048]{2,1,0:T(8,128)(2,1)} %bitcast.23), calls=%async_computation | async-start | bytes 1048576 | tf_op jit(solution)/shard_map/all_to_all | solution.py:203
  19.8 2.6 %shard_map.65 = (bf16[128,4096]{1,0:T(8,128)(2,1)}, bf16[128,64]{1,0:T(8,128)(2,1)}, bf16[128,64]{1,0:T(8,128)(2,1)}) custom-call(s32[1]{0:T(128)} %bitcast.place, s32[8,64]{1,0:T(8,128)} %bitcast.25, f32[8,64]{1,0:T(8,128)} %bitcast.27, bf16[64,4096]{1,0:T(8,128)(2,1)} %tokens.3), custom_call_target="tpu_custom_call" | custom-call | flops 67108864 | bytes 1609732 | tf_op jit(solution)/shard_map/pallas_call | solution.py:179
  22.4 14.7 %all-to-all-done = bf16[16,8,2048]{2,1,0:T(8,128)(2,1)S(1)} async-done(((bf16[16,8,2048]{2,1,0:T(8,128)(2,1)}), bf16[16,8,2048]{2,1,0:T(8,128)(2,1)S(1)}, u32[]{:S(2)}, u32[]{:S(2)}) %all-to-all-start) | async-done | bytes 524320 | tf_op jit(solution)/shard_map/all_to_all | solution.py:203
  37.1 3.6 %all-to-all-start.1 = ((bf16[16,8,4096]{2,1,0:T(8,128)(2,1)}), bf16[16,8,4096]{2,1,0:T(8,128)(2,1)S(1)}, u32[]{:S(2)}, u32[]{:S(2)}) async-start(bf16[16,8,4096]{2,1,0:T(8,128)(2,1)} %bitcast.22), calls=%async_computation.1 | async-start | bytes 2097152 | tf_op jit(solution)/shard_map/all_to_all | solution.py:203
  40.6 1.9 %collective-permute-start = (bf16[128,2048]{1,0:T(8,128)(2,1)S(1)}, bf16[128,2048]{1,0:T(8,128)(2,1)}, u32[]{:S(2)}, u32[]{:S(2)}) collective-permute-start(bf16[128,2048]{1,0:T(8,128)(2,1)S(1)} %bitcast.19), channel_id=1, source_target_pairs={{0,4},{4,0},{8,12},{12,8},{16,20},{20,16},{24,28},{28,24},{32,36},... | collective-permute-start | bytes 1572872 | tf_op jit(solution)/shard_map/ppermute | solution.py:206
  42.6 2.5 %shard_map.68 = (bf16[256,256]{1,0:T(8,128)(2,1)}, bf16[256,256]{1,0:T(8,128)(2,1)}, bf16[256,256]{1,0:T(8,128)(2,1)}, bf16[256,256]{1,0:T(8,128)(2,1)}) custom-call(s32[1]{0:T(128)} %bitcast.place, bf16[256,4096]{1,0:T(8,128)(2,1)} %bitcast.21), custom_call_target="tpu_custom_call" | custom-call | bytes 2621444 | tf_op jit(solution)/shard_map/pallas_call | solution.py:179
  45.0 3.4 %collective-permute-start.1 = (bf16[256,256]{1,0:T(8,128)(2,1)}, bf16[256,256]{1,0:T(8,128)(2,1)S(1)}, u32[]{:S(2)}, u32[]{:S(2)}) collective-permute-start(bf16[256,256]{1,0:T(8,128)(2,1)} %get-tuple-element.22), channel_id=1, source_target_pairs={{0,4},{4,0},{8,12},{12,8},{16,20},{20,16},{24,28},{28,24},{32,36},... | collective-permute-start | bytes 393224 | tf_op jit(solution)/shard_map/ppermute | solution.py:206
  48.4 1.9 %collective-permute-start.2 = (bf16[256,256]{1,0:T(8,128)(2,1)}, bf16[256,256]{1,0:T(8,128)(2,1)S(1)}, u32[]{:S(2)}, u32[]{:S(2)}) collective-permute-start(bf16[256,256]{1,0:T(8,128)(2,1)} %get-tuple-element.23), channel_id=1, source_target_pairs={{0,8},{4,12},{8,0},{12,4},{16,24},{20,28},{24,16},{28,20},{32,40},... | collective-permute-start | bytes 393224 | tf_op jit(solution)/shard_map/ppermute | solution.py:206
  50.3 4.0 %collective-permute-start.3 = (bf16[256,256]{1,0:T(8,128)(2,1)}, bf16[256,256]{1,0:T(8,128)(2,1)S(1)}, u32[]{:S(2)}, u32[]{:S(2)}) collective-permute-start(bf16[256,256]{1,0:T(8,128)(2,1)} %get-tuple-element.24), channel_id=1, source_target_pairs={{0,12},{4,8},{8,4},{12,0},{16,28},{20,24},{24,20},{28,16},{32,44},... | collective-permute-start | bytes 393224 | tf_op jit(solution)/shard_map/ppermute | solution.py:206
  54.3 10.5 %collective-permute-done.1.refs_1_ = bf16[256,256]{1,0:T(8,128)(2,1)S(1)} collective-permute-done((bf16[256,256]{1,0:T(8,128)(2,1)}, bf16[256,256]{1,0:T(8,128)(2,1)S(1)}, u32[]{:S(2)}, u32[]{:S(2)}) %collective-permute-start.1) | collective-permute-done | bytes 131104 | tf_op jit(solution)/shard_map/ppermute | solution.py:206
  64.8 0.0 collective-permute-done.2.refs_2_
  64.8 0.0 collective-permute-done.3.refs_3_
  64.9 0.6 copy-done.7
  65.5 0.1 copy-done.8
  65.6 0.0 copy-done.9
  65.6 1.9 %shard_map.69.refs_0_ = bf16[1024,256]{1,0:T(8,128)(2,1)} custom-call(bf16[256,256]{1,0:T(8,128)(2,1)} %get-tuple-element.21.refs_0_, bf16[256,256]{1,0:T(8,128)(2,1)} %copy-done.7, bf16[256,256]{1,0:T(8,128)(2,1)} %copy-done.8, bf16[256,256]{1,0:T(8,128)(2,1)} %copy-done.9), custom_call_target="tpu_custom_call" | custom-call | bytes 1048576 | tf_op jit(solution)/shard_map/pallas_call | solution.py:179
  67.5 1.9 %collective-permute-start.4 = (bf16[1024,256]{1,0:T(8,128)(2,1)}, bf16[1024,256]{1,0:T(8,128)(2,1)S(1)}, u32[]{:S(2)}, u32[]{:S(2)}) collective-permute-start(bf16[1024,256]{1,0:T(8,128)(2,1)} %shard_map.69.refs_0_), channel_id=1, source_target_pairs={{0,1},{1,0},{2,3},{3,2},{4,5},{5,4},{6,7},{7,6},{8,9},{9,8},{10,11... | collective-permute-start | bytes 1572872 | tf_op jit(solution)/shard_map/ppermute | solution.py:206
  69.4 1.9 %collective-permute-start.5 = (bf16[1024,256]{1,0:T(8,128)(2,1)}, bf16[1024,256]{1,0:T(8,128)(2,1)S(1)}, u32[]{:S(2)}, u32[]{:S(2)}) collective-permute-start(bf16[1024,256]{1,0:T(8,128)(2,1)} %shard_map.69.refs_0_), channel_id=1, source_target_pairs={{0,2},{1,3},{2,0},{3,1},{4,6},{5,7},{6,4},{7,5},{8,10},{9,11},{10,... | collective-permute-start | bytes 1572872 | tf_op jit(solution)/shard_map/ppermute | solution.py:206
  71.3 5.7 %collective-permute-start.6 = (bf16[1024,256]{1,0:T(8,128)(2,1)}, bf16[1024,256]{1,0:T(8,128)(2,1)S(1)}, u32[]{:S(2)}, u32[]{:S(2)}) collective-permute-start(bf16[1024,256]{1,0:T(8,128)(2,1)} %shard_map.69.refs_0_), channel_id=1, source_target_pairs={{0,3},{1,2},{2,1},{3,0},{4,7},{5,6},{6,5},{7,4},{8,11},{9,10},{10,... | collective-permute-start | bytes 1572872 | tf_op jit(solution)/shard_map/ppermute | solution.py:206
  77.1 0.0 collective-permute-done.refs_1_
  77.1 4.5 %shard_map.66 = bf16[128,256]{1,0:T(8,128)(2,1)} custom-call(s32[1]{0:T(128)} %bitcast.place, bf16[128,2048]{1,0:T(8,128)(2,1)} %bitcast.20, bf16[128,2048]{1,0:T(8,128)(2,1)} %collective-permute-done.refs_1_, bf16[4096,256]{1,0:T(8,128)(2,1)} %bitcast.13, bf16[4096,256]{1,0:T(8,128)(2,1)} %bitcast.14, bf16[4096,256]{1,0:T(8,128)(2,1)} %bitcast.16, ...), custom_call_target="tpu_custom_call" | custom-call | flops 536870912 | bytes 4194304 | tf_op jit(solution)/shard_map/pallas_call | solution.py:115
  81.6 4.2 %shard_map.67 = bf16[128,256]{1,0:T(8,128)(2,1)} custom-call(s32[1]{0:T(128)} %bitcast.place, bf16[128,4096]{1,0:T(8,128)(2,1)S(1)} %bitcast.11, bf16[4096,256]{1,0:T(8,128)(2,1)} %bitcast.15, bf16[4096,256]{1,0:T(8,128)(2,1)} %bitcast.18), custom_call_target="tpu_custom_call" | custom-call | flops 536870912 | bytes 4194304 | tf_op jit(solution)/shard_map/pallas_call | solution.py:115
  85.8 0.8 pad_maximum_fusion
  86.7 12.6 %all-gather = bf16[1024,256]{1,0:T(8,128)(2,1)S(1)} all-gather(bf16[256,256]{1,0:T(8,128)(2,1)S(1)} %pad_maximum_fusion), channel_id=2, replica_groups={{0,4,8,12},{16,20,24,28},{32,36,40,44},{48,52,56,60},{1,5,9,13},{17,21,..., dimensions={0}, use_global_device_ids=true | all-gather | bytes 655360 | tf_op jit(solution)/shard_map/all_gather | solution.py:234
  99.2 0.0 collective-permute-done.4.refs_1_
  99.2 0.7 collective-permute-done.6.refs_3_
  100.0 0.7 shard_map.70
  100.7 27.2 %all_to_all.20.rows = bf16[16,16,1024]{2,1,0:T(8,128)(2,1)S(1)} all-to-all(bf16[16,16,1024]{2,1,0:T(8,128)(2,1)S(1)} %shard_map.70), channel_id=1, replica_groups=mesh['grp'=16,'shard'=16,'side'=4] {'grp'}, dimensions={0} | all-to-all | bytes 1048576 | tf_op jit(solution)/shard_map/all_to_all | solution.py:203
  127.9 0.3 shard_map.71
  128.2 25.6 %all_to_all.21.parts = bf16[4,64,256]{2,1,0:T(8,128)(2,1)S(1)} all-to-all(bf16[4,64,256]{2,1,0:T(8,128)(2,1)S(1)} %shard_map.71), channel_id=1, replica_groups={{0,16,32,48},{4,20,36,52},{8,24,40,56},{12,28,44,60},{1,17,33,49},{5,21..., dimensions={0} | all-to-all | bytes 262144 | tf_op jit(solution)/shard_map/all_to_all | solution.py:244
  153.8 0.6 shard_map.72
  (19 shorter events, 0.0 us)
Async XLA Ops:
  2.3 34.8 %all-to-all-start = ((bf16[16,8,2048]{2,1,0:T(8,128)(2,1)}), bf16[16,8,2048]{2,1,0:T(8,128)(2,1)S(1)}, u32[]{:S(2)}, u32[]{:S(2)}) async-start(bf16[16,8,2048]{2,1,0:T(8,128)(2,1)} %bitcast.23), calls=%async_computation | async-start | bytes 1048576 | tf_op jit(solution)/shard_map/all_to_all | solution.py:203
  37.1 8.0 %copy-start.5 = (bf16[16,8,2048]{2,1,0:T(8,128)(2,1)}, bf16[16,8,2048]{2,1,0:T(8,128)(2,1)S(1)}, u32[]{:S(2)}) copy-start(bf16[16,8,2048]{2,1,0:T(8,128)(2,1)S(1)} %all-to-all-done) | copy-start | bytes 1572868
  37.1 44.5 %all-to-all-start.1 = ((bf16[16,8,4096]{2,1,0:T(8,128)(2,1)}), bf16[16,8,4096]{2,1,0:T(8,128)(2,1)S(1)}, u32[]{:S(2)}, u32[]{:S(2)}) async-start(bf16[16,8,4096]{2,1,0:T(8,128)(2,1)} %bitcast.22), calls=%async_computation.1 | async-start | bytes 2097152 | tf_op jit(solution)/shard_map/all_to_all | solution.py:203
  40.6 36.5 %collective-permute-start = (bf16[128,2048]{1,0:T(8,128)(2,1)S(1)}, bf16[128,2048]{1,0:T(8,128)(2,1)}, u32[]{:S(2)}, u32[]{:S(2)}) collective-permute-start(bf16[128,2048]{1,0:T(8,128)(2,1)S(1)} %bitcast.19), channel_id=1, source_target_pairs={{0,4},{4,0},{8,12},{12,8},{16,20},{20,16},{24,28},{28,24},{32,36},... | collective-permute-start | bytes 1572872 | tf_op jit(solution)/shard_map/ppermute | solution.py:206
  45.0 19.8 %collective-permute-start.1 = (bf16[256,256]{1,0:T(8,128)(2,1)}, bf16[256,256]{1,0:T(8,128)(2,1)S(1)}, u32[]{:S(2)}, u32[]{:S(2)}) collective-permute-start(bf16[256,256]{1,0:T(8,128)(2,1)} %get-tuple-element.22), channel_id=1, source_target_pairs={{0,4},{4,0},{8,12},{12,8},{16,20},{20,16},{24,28},{28,24},{32,36},... | collective-permute-start | bytes 393224 | tf_op jit(solution)/shard_map/ppermute | solution.py:206
  48.4 16.5 %collective-permute-start.2 = (bf16[256,256]{1,0:T(8,128)(2,1)}, bf16[256,256]{1,0:T(8,128)(2,1)S(1)}, u32[]{:S(2)}, u32[]{:S(2)}) collective-permute-start(bf16[256,256]{1,0:T(8,128)(2,1)} %get-tuple-element.23), channel_id=1, source_target_pairs={{0,8},{4,12},{8,0},{12,4},{16,24},{20,28},{24,16},{28,20},{32,40},... | collective-permute-start | bytes 393224 | tf_op jit(solution)/shard_map/ppermute | solution.py:206
  50.3 14.5 %collective-permute-start.3 = (bf16[256,256]{1,0:T(8,128)(2,1)}, bf16[256,256]{1,0:T(8,128)(2,1)S(1)}, u32[]{:S(2)}, u32[]{:S(2)}) collective-permute-start(bf16[256,256]{1,0:T(8,128)(2,1)} %get-tuple-element.24), channel_id=1, source_target_pairs={{0,12},{4,8},{8,4},{12,0},{16,28},{20,24},{24,20},{28,16},{32,44},... | collective-permute-start | bytes 393224 | tf_op jit(solution)/shard_map/ppermute | solution.py:206
  64.8 0.6 copy-start.7
  64.8 0.7 copy-start.8
  64.9 0.7 copy-start.9
  67.5 31.8 %collective-permute-start.4 = (bf16[1024,256]{1,0:T(8,128)(2,1)}, bf16[1024,256]{1,0:T(8,128)(2,1)S(1)}, u32[]{:S(2)}, u32[]{:S(2)}) collective-permute-start(bf16[1024,256]{1,0:T(8,128)(2,1)} %shard_map.69.refs_0_), channel_id=1, source_target_pairs={{0,1},{1,0},{2,3},{3,2},{4,5},{5,4},{6,7},{7,6},{8,9},{9,8},{10,11... | collective-permute-start | bytes 1572872 | tf_op jit(solution)/shard_map/ppermute | solution.py:206
  69.4 29.8 %collective-permute-start.5 = (bf16[1024,256]{1,0:T(8,128)(2,1)}, bf16[1024,256]{1,0:T(8,128)(2,1)S(1)}, u32[]{:S(2)}, u32[]{:S(2)}) collective-permute-start(bf16[1024,256]{1,0:T(8,128)(2,1)} %shard_map.69.refs_0_), channel_id=1, source_target_pairs={{0,2},{1,3},{2,0},{3,1},{4,6},{5,7},{6,4},{7,5},{8,10},{9,11},{10,... | collective-permute-start | bytes 1572872 | tf_op jit(solution)/shard_map/ppermute | solution.py:206
  71.3 28.6 %collective-permute-start.6 = (bf16[1024,256]{1,0:T(8,128)(2,1)}, bf16[1024,256]{1,0:T(8,128)(2,1)S(1)}, u32[]{:S(2)}, u32[]{:S(2)}) collective-permute-start(bf16[1024,256]{1,0:T(8,128)(2,1)} %shard_map.69.refs_0_), channel_id=1, source_target_pairs={{0,3},{1,2},{2,1},{3,0},{4,7},{5,6},{6,5},{7,4},{8,11},{9,10},{10,... | collective-permute-start | bytes 1572872 | tf_op jit(solution)/shard_map/ppermute | solution.py:206
  81.6 4.2 %copy-start.6 = (bf16[128,256]{1,0:T(8,128)(2,1)S(1)}, bf16[128,256]{1,0:T(8,128)(2,1)}, u32[]{:S(2)}) copy-start(bf16[128,256]{1,0:T(8,128)(2,1)} %shard_map.66) | copy-start | bytes 196612
  81.6 18.3 %copy-start = (bf16[1024,256]{1,0:T(8,128)(2,1)S(1)}, bf16[1024,256]{1,0:T(8,128)(2,1)}, u32[]{:S(2)}) copy-start(bf16[1024,256]{1,0:T(8,128)(2,1)} %shard_map.69.refs_0_) | copy-start | bytes 1572868
  99.9 27.9 %copy-start.1 = (bf16[128,64]{1,0:T(8,128)(2,1)S(1)}, bf16[128,64]{1,0:T(8,128)(2,1)}, u32[]{:S(2)}) copy-start(bf16[128,64]{1,0:T(8,128)(2,1)} %get-tuple-element.15.high_a) | copy-start | bytes 49156
  99.9 27.9 %copy-start.2 = (bf16[128,64]{1,0:T(8,128)(2,1)S(1)}, bf16[128,64]{1,0:T(8,128)(2,1)}, u32[]{:S(2)}) copy-start(bf16[128,64]{1,0:T(8,128)(2,1)} %get-tuple-element.16.low_a) | copy-start | bytes 49156
  99.9 27.9 %copy-start.3 = (bf16[128,64]{1,0:T(8,128)(2,1)S(1)}, bf16[128,64]{1,0:T(8,128)(2,1)}, u32[]{:S(2)}) copy-start(bf16[128,64]{1,0:T(8,128)(2,1)} %get-tuple-element.17.high_b) | copy-start | bytes 49156
  100.0 27.9 %copy-start.4 = (bf16[128,64]{1,0:T(8,128)(2,1)S(1)}, bf16[128,64]{1,0:T(8,128)(2,1)}, u32[]{:S(2)}) copy-start(bf16[128,64]{1,0:T(8,128)(2,1)} %get-tuple-element.18.low_b) | copy-start | bytes 49156

commit v6 on v5

--- a/solution.py
+++ b/solution.py
@@ -70,65 +70,44 @@
     return (gate / (1.0 + jnp.exp(-gate)) * upper).astype(BF16)
 
 
-def hidden_kernel(count, place, *refs):
-    rows, w_gate, w_up = refs[:count], refs[count : 2 * count], refs[2 * count : 3 * count]
-    out, gate, upper = refs[3 * count :]
-    step = pl.program_id(0)
-    if count == 1:
-        size = w_gate[0].shape[0]
-        piece = rows[0][:, pl.ds(pl.multiple_of(step * size, size), size)]
-        gates, uppers = dot(piece, w_gate[0][...]), dot(piece, w_up[0][...])
-    else:
-        gates = dot(rows[0][...], w_gate[0][...]) + dot(rows[1][...], w_gate[1][...])
-        uppers = dot(rows[0][...], w_up[0][...]) + dot(rows[1][...], w_up[1][...])
-
-    @pl.when(step == 0)
-    def _():
-        gate[...] = gates
-        upper[...] = uppers
-
-    @pl.when(step > 0)
-    def _():
-        gate[...] += gates
-        upper[...] += uppers
-
-    @pl.when(step == pl.num_programs(0) - 1)
-    def _():
-        out[...] = activate(gate[...], upper[...])
-
-
-def gate_up(place, rows, w_gate, w_up, steps=4):
-    count, (height, width) = len(rows), rows[0].shape
-    units, step = w_gate.shape[1], width // steps
-
-    def near(i, place):
-        return (i + steps * unpack(place)[2] if count == 2 else i, 0)
-
-    def far(i, place):
-        return (i + steps * (1 - unpack(place)[2]), 0)
-
-    maps = [near, far][:count]
-    row_spec = pl.BlockSpec((height, step), lambda i, place: (0, i))
-    if count == 1:
-        row_spec = pl.BlockSpec(memory_space=pltpu.VMEM)
-        rows = [pltpu.with_memory_space_constraint(rows[0], pltpu.VMEM)]
+def hidden_a_kernel(place, mine, other, w_gate, w_up, out):
+    width = mine.shape[1]
+    parity = unpack(place)[2]
+    own = pl.ds(pl.multiple_of(parity * width, width), width)
+    far = pl.ds(pl.multiple_of((1 - parity) * width, width), width)
+    gate = dot(mine[...], w_gate[own, :]) + dot(other[...], w_gate[far, :])
+    upper = dot(mine[...], w_up[own, :]) + dot(other[...], w_up[far, :])
+    out[...] = activate(gate, upper)
+
+
+def hidden_b_kernel(before, rows, w_gate, w_up_far, out, w_up, sems):
+    height = before.shape[0]
+    load = pltpu.make_async_copy(w_up_far, w_up, sems.at[0])
+    load.start()
+    keep = pltpu.make_async_copy(before, out.at[pl.ds(0, height), :], sems.at[1])
+    keep.start()
+    gate = dot(rows[...], w_gate[...])
+    keep.wait()
+    load.wait()
+    out[height:, :] = activate(gate, dot(rows[...], w_up[...]))
+
+
+def hidden_b(before, rows, w_gate, w_up):
+    height, units = before.shape
+    inside = pl.BlockSpec(memory_space=pltpu.VMEM)
+    outside = pl.BlockSpec(memory_space=pltpu.HBM)
+    before = pltpu.with_memory_space_constraint(before, pltpu.HBM)
     return pl.pallas_call(
-        functools.partial(hidden_kernel, count),
-        out_shape=jax.ShapeDtypeStruct((height, units), BF16),
-        grid_spec=pltpu.PrefetchScalarGridSpec(
-            num_scalar_prefetch=1,
-            grid=(steps,),
-            in_specs=[row_spec] * count
-            + [pl.BlockSpec((step, units), m) for m in maps] * 2,
-            out_specs=pl.BlockSpec(memory_space=pltpu.VMEM),
-            scratch_shapes=[pltpu.VMEM((height, units), F32)] * 2,
+        hidden_b_kernel,
+        out_shape=jax.ShapeDtypeStruct((2 * height, units), BF16),
+        in_specs=[outside, inside, inside, outside],
+        out_specs=inside,
+        scratch_shapes=[pltpu.VMEM(w_up.shape, BF16), pltpu.SemaphoreType.DMA((2,))],
+        compiler_params=pltpu.CompilerParams(vmem_limit_bytes=16 << 20),
+        cost_estimate=pl.CostEstimate(
+            flops=4 * height * w_up.size, bytes_accessed=4 * w_up.size, transcendentals=0
         ),
-        cost_estimate=pl.CostEstimate(
-            flops=4 * height * units * w_gate.shape[0],
-            bytes_accessed=4 * w_gate.size,
-            transcendentals=height * units,
-        ),
-    )(place, *rows, *[w_gate] * count, *[w_up] * count)
+    )(before, rows, w_gate, pltpu.with_memory_space_constraint(w_up, pltpu.HBM))
 
 
 def down_kernel(place, hidden, *refs):
@@ -226,11 +205,13 @@
     weights = [weight] + [swap(weight, k, "side") for k in range(1, sides)]
     other = swap(mine, 1)
     arrived = over_y(sent_b).reshape(rows, width)
-    hidden_a = gate_up(place, [mine, other], w_gate[0], w_up[0])
-    hidden_b = gate_up(place, [arrived], w_gate[0], w_up[0])
+    (hidden,) = call(
+        hidden_a_kernel, [((rows, units), BF16)], place, mine, other, w_gate[0], w_up[0],
+        flops=4 * rows * width * units,
+    )
+    hidden = hidden_b(hidden, arrived, w_gate[0], w_up[0])
     quartets = [[i * TPE + k for k in range(TPE)] for i in range(per_group)]
     strided = [[i * TPE + k for i in range(per_group)] for k in range(TPE)]
-    hidden = jnp.concatenate([hidden_a, hidden_b], axis=0)
     hidden = lax.all_gather(hidden, "shard", axis_index_groups=quartets)
     (result,) = call(
         down_kernel, [((groups, cap, quarter), BF16)], place, hidden, *weights,

time: 155 us -> 155 us (level)
  waiting for transfers between devices: 25.9 us -> 28.3 us
  blocking collectives: 65.3 us -> 63.3 us
    pallas_call x2 -> x1, Pallas kernels: 8.71 us -> 2.36 us  [hidden_b(): pl.pallas_call(hidden_b_kernel, out_shape=jax.ShapeDtypeStruct((2 * heigh...]
    pallas_call x7 -> x8, Pallas kernels: 11 us -> 16.4 us  [call(): pl.pallas_call(kernel, out_shape=outs, in_specs=specs, out_specs=[pl.Bloc...]
    all_to_all x1, blocking collectives: 27.2 us -> 24.4 us  [over_y(): lax.all_to_all(x.reshape(groups, -1, x.shape[-1]), 'grp', 0, 0, tiled=True)]
    ppermute x7, waiting for transfers between devices: 11.2 us -> 13.6 us  [swap(): lax.ppermute(x, axis, [(i, i ^ bits) for i in range(lax.axis_size(axis))])]
  transfers between devices with their start and end apart: 9 -> 9, of which waited for: 3 -> 3; matrix products, arithmetic and copies ran while one was open for 1% -> 0% of each run, Pallas kernels for 10% -> 9%
where the time goes in v6:
time: 155 us; the launch traced here: 154 us
  blocking collectives  63.3 us (41%)
  starting transfers between devices  41.8 us (27%)
  waiting for transfers between devices  28.3 us (18%)
  Pallas kernels  18.8 us (12%)
    all_to_all x1, blocking collectives, on_device(): lax.all_to_all(parts, 'shard', 0, 0, tiled=True, axis_index_groups=strided)  26.2 us
    all_to_all x1, blocking collectives, over_y(): lax.all_to_all(x.reshape(groups, -1, x.shape[-1]), 'grp', 0, 0, tiled=True)  24.4 us
    all_to_all x2, starting transfers between devices, over_y(): lax.all_to_all(x.reshape(groups, -1, x.shape[-1]), 'grp', 0, 0, tiled=True)  21 us
    ppermute x7, starting transfers between devices, swap(): lax.ppermute(x, axis, [(i, i ^ bits) for i in range(lax.axis_size(axis))])  20.8 us
    pallas_call x8, Pallas kernels, call(): pl.pallas_call(kernel, out_shape=outs, in_specs=specs, out_specs=[pl.Bloc...  16.4 us
    all_to_all x2, waiting for transfers between devices, over_y(): lax.all_to_all(x.reshape(groups, -1, x.shape[-1]), 'grp', 0, 0, tiled=True)  14.7 us
    ppermute x7, waiting for transfers between devices, swap(): lax.ppermute(x, axis, [(i, i ^ bits) for i in range(lax.axis_size(axis))])  13.6 us
    all_gather x1, blocking collectives, on_device(): hidden = lax.all_gather(hidden, 'shard', axis_index_groups=quartets)  12.6 us
  transfers between devices with their start and end apart: 9, of which 3 were waited for; matrix products, arithmetic and copies ran while one was open for 0% of the time, Pallas kernels for 9%

profile of v6, /device:TPU:1, one launch (start us, length us, event | category | flops | bytes accessed | tf_op | source)
XLA Modules:
  0.0 153.9 jit_solution(14538884065552740502)
XLA Ops:
  0.0 2.3 %shard_map.64 = (bf16[128,2048]{1,0:T(8,128)(2,1)}, bf16[128,64]{1,0:T(8,128)(2,1)}, bf16[128,64]{1,0:T(8,128)(2,1)}) custom-call(s32[1]{0:T(128)} %bitcast.place, s32[8,64]{1,0:T(8,128)} %bitcast.22, f32[8,64]{1,0:T(8,128)} %bitcast.24, bf16[64,4096]{1,0:T(8,128)(2,1)} %tokens.3), custom_call_target="tpu_custom_call" | custom-call | flops 33554432 | bytes 1085444 | tf_op jit(solution)/shard_map/pallas_call | solution.py:158
  2.3 17.5 %all-to-all-start = ((bf16[16,8,2048]{2,1,0:T(8,128)(2,1)}), bf16[16,8,2048]{2,1,0:T(8,128)(2,1)S(1)}, u32[]{:S(2)}, u32[]{:S(2)}) async-start(bf16[16,8,2048]{2,1,0:T(8,128)(2,1)} %bitcast.21), calls=%async_computation | async-start | bytes 1048576 | tf_op jit(solution)/shard_map/all_to_all | solution.py:182
  19.8 2.6 %shard_map.65 = (bf16[128,4096]{1,0:T(8,128)(2,1)}, bf16[128,64]{1,0:T(8,128)(2,1)}, bf16[128,64]{1,0:T(8,128)(2,1)}) custom-call(s32[1]{0:T(128)} %bitcast.place, s32[8,64]{1,0:T(8,128)} %bitcast.23, f32[8,64]{1,0:T(8,128)} %bitcast.25, bf16[64,4096]{1,0:T(8,128)(2,1)} %tokens.3), custom_call_target="tpu_custom_call" | custom-call | flops 67108864 | bytes 1609732 | tf_op jit(solution)/shard_map/pallas_call | solution.py:158
  22.4 14.7 %all-to-all-done = bf16[16,8,2048]{2,1,0:T(8,128)(2,1)S(1)} async-done(((bf16[16,8,2048]{2,1,0:T(8,128)(2,1)}), bf16[16,8,2048]{2,1,0:T(8,128)(2,1)S(1)}, u32[]{:S(2)}, u32[]{:S(2)}) %all-to-all-start) | async-done | bytes 524320 | tf_op jit(solution)/shard_map/all_to_all | solution.py:182
  37.1 3.6 %all-to-all-start.1 = ((bf16[16,8,4096]{2,1,0:T(8,128)(2,1)}), bf16[16,8,4096]{2,1,0:T(8,128)(2,1)S(1)}, u32[]{:S(2)}, u32[]{:S(2)}) async-start(bf16[16,8,4096]{2,1,0:T(8,128)(2,1)} %bitcast.20), calls=%async_computation.1 | async-start | bytes 2097152 | tf_op jit(solution)/shard_map/all_to_all | solution.py:182
  40.6 1.9 %collective-permute-start = (bf16[128,2048]{1,0:T(8,128)(2,1)S(1)}, bf16[128,2048]{1,0:T(8,128)(2,1)S(1)}, u32[]{:S(2)}, u32[]{:S(2)}) collective-permute-start(bf16[128,2048]{1,0:T(8,128)(2,1)S(1)} %bitcast.18), channel_id=1, source_target_pairs={{0,4},{4,0},{8,12},{12,8},{16,20},{20,16},{24,28},{28,24},{32,36},... | collective-permute-start | bytes 1572872 | tf_op jit(solution)/shard_map/ppermute | solution.py:185
  42.6 2.5 %shard_map.68 = (bf16[256,256]{1,0:T(8,128)(2,1)}, bf16[256,256]{1,0:T(8,128)(2,1)}, bf16[256,256]{1,0:T(8,128)(2,1)}, bf16[256,256]{1,0:T(8,128)(2,1)}) custom-call(s32[1]{0:T(128)} %bitcast.place, bf16[256,4096]{1,0:T(8,128)(2,1)} %bitcast.17), custom_call_target="tpu_custom_call" | custom-call | bytes 2621444 | tf_op jit(solution)/shard_map/pallas_call | solution.py:158
  45.0 3.4 %collective-permute-start.1 = (bf16[256,256]{1,0:T(8,128)(2,1)}, bf16[256,256]{1,0:T(8,128)(2,1)S(1)}, u32[]{:S(2)}, u32[]{:S(2)}) collective-permute-start(bf16[256,256]{1,0:T(8,128)(2,1)} %get-tuple-element.22), channel_id=1, source_target_pairs={{0,4},{4,0},{8,12},{12,8},{16,20},{20,16},{24,28},{28,24},{32,36},... | collective-permute-start | bytes 393224 | tf_op jit(solution)/shard_map/ppermute | solution.py:185
  48.4 1.9 %collective-permute-start.2 = (bf16[256,256]{1,0:T(8,128)(2,1)}, bf16[256,256]{1,0:T(8,128)(2,1)S(1)}, u32[]{:S(2)}, u32[]{:S(2)}) collective-permute-start(bf16[256,256]{1,0:T(8,128)(2,1)} %get-tuple-element.23), channel_id=1, source_target_pairs={{0,8},{4,12},{8,0},{12,4},{16,24},{20,28},{24,16},{28,20},{32,40},... | collective-permute-start | bytes 393224 | tf_op jit(solution)/shard_map/ppermute | solution.py:185
  50.3 4.0 %collective-permute-start.3 = (bf16[256,256]{1,0:T(8,128)(2,1)}, bf16[256,256]{1,0:T(8,128)(2,1)S(1)}, u32[]{:S(2)}, u32[]{:S(2)}) collective-permute-start(bf16[256,256]{1,0:T(8,128)(2,1)} %get-tuple-element.24), channel_id=1, source_target_pairs={{0,12},{4,8},{8,4},{12,0},{16,28},{20,24},{24,20},{28,16},{32,44},... | collective-permute-start | bytes 393224 | tf_op jit(solution)/shard_map/ppermute | solution.py:185
  54.3 10.5 %collective-permute-done.1.refs_1_ = bf16[256,256]{1,0:T(8,128)(2,1)S(1)} collective-permute-done((bf16[256,256]{1,0:T(8,128)(2,1)}, bf16[256,256]{1,0:T(8,128)(2,1)S(1)}, u32[]{:S(2)}, u32[]{:S(2)}) %collective-permute-start.1) | collective-permute-done | bytes 131104 | tf_op jit(solution)/shard_map/ppermute | solution.py:185
  64.8 0.6 copy-done.8
  65.5 0.1 copy-done.9
  65.5 0.0 copy-done.10
  65.6 1.9 %shard_map.69.refs_0_ = bf16[1024,256]{1,0:T(8,128)(2,1)} custom-call(bf16[256,256]{1,0:T(8,128)(2,1)} %get-tuple-element.21.refs_0_, bf16[256,256]{1,0:T(8,128)(2,1)} %copy-done.8, bf16[256,256]{1,0:T(8,128)(2,1)} %copy-done.9, bf16[256,256]{1,0:T(8,128)(2,1)} %copy-done.10), custom_call_target="tpu_custom_call" | custom-call | bytes 1048576 | tf_op jit(solution)/shard_map/pallas_call | solution.py:158
  67.5 1.9 %collective-permute-start.4 = (bf16[1024,256]{1,0:T(8,128)(2,1)}, bf16[1024,256]{1,0:T(8,128)(2,1)}, u32[]{:S(2)}, u32[]{:S(2)}) collective-permute-start(bf16[1024,256]{1,0:T(8,128)(2,1)} %shard_map.69.refs_0_), channel_id=1, source_target_pairs={{0,1},{1,0},{2,3},{3,2},{4,5},{5,4},{6,7},{7,6},{8,9},{9,8},{10,11... | collective-permute-start | bytes 1572872 | tf_op jit(solution)/shard_map/ppermute | solution.py:185
  69.4 1.9 %collective-permute-start.5 = (bf16[1024,256]{1,0:T(8,128)(2,1)}, bf16[1024,256]{1,0:T(8,128)(2,1)}, u32[]{:S(2)}, u32[]{:S(2)}) collective-permute-start(bf16[1024,256]{1,0:T(8,128)(2,1)} %shard_map.69.refs_0_), channel_id=1, source_target_pairs={{0,2},{1,3},{2,0},{3,1},{4,6},{5,7},{6,4},{7,5},{8,10},{9,11},{10,... | collective-permute-start | bytes 1572872 | tf_op jit(solution)/shard_map/ppermute | solution.py:185
  71.4 5.7 %collective-permute-start.6 = (bf16[1024,256]{1,0:T(8,128)(2,1)}, bf16[1024,256]{1,0:T(8,128)(2,1)}, u32[]{:S(2)}, u32[]{:S(2)}) collective-permute-start(bf16[1024,256]{1,0:T(8,128)(2,1)} %shard_map.69.refs_0_), channel_id=1, source_target_pairs={{0,3},{1,2},{2,1},{3,0},{4,7},{5,6},{6,5},{7,4},{8,11},{9,10},{10,... | collective-permute-start | bytes 1572872 | tf_op jit(solution)/shard_map/ppermute | solution.py:185
  77.1 0.0 collective-permute-done.other
  77.1 0.8 copy-done.7
  77.9 4.0 %shard_map.66.before = bf16[128,256]{1,0:T(8,128)(2,1)} custom-call(s32[1]{0:T(128)} %bitcast.place, bf16[128,2048]{1,0:T(8,128)(2,1)} %bitcast.19, bf16[128,2048]{1,0:T(8,128)(2,1)} %copy-done.7, bf16[4096,256]{1,0:T(8,128)(2,1)} %bitcast.11, bf16[4096,256]{1,0:T(8,128)(2,1)} %bitcast.15), custom_call_target="tpu_custom_call" | custom-call | flops 536870912 | bytes 5308420 | tf_op jit(solution)/shard_map/pallas_call | solution.py:158
  82.0 0.0 all-to-all-done.1
  82.0 2.4 %shard_map.67 = bf16[256,256]{1,0:T(8,128)(2,1)S(1)} custom-call(bf16[128,256]{1,0:T(8,128)(2,1)} %shard_map.66.before, bf16[128,4096]{1,0:T(8,128)(2,1)S(1)} %bitcast.13, bf16[4096,256]{1,0:T(8,128)(2,1)S(1)} %bitcast.12, bf16[4096,256]{1,0:T(8,128)(2,1)} %bitcast.16), custom_call_target="tpu_custom_call" | custom-call | flops 536870912 | bytes 4194304 | tf_op jit(solution)/shard_map/pallas_call | solution.py:100
  84.3 12.6 %all-gather = bf16[1024,256]{1,0:T(8,128)(2,1)S(1)} all-gather(bf16[256,256]{1,0:T(8,128)(2,1)S(1)} %shard_map.67), channel_id=2, replica_groups={{0,4,8,12},{16,20,24,28},{32,36,40,44},{48,52,56,60},{1,5,9,13},{17,21,..., dimensions={0}, use_global_device_ids=true | all-gather | bytes 655360 | tf_op jit(solution)/shard_map/all_gather | solution.py:215
  97.0 0.0 collective-permute-done.4.refs_1_
  97.0 0.0 collective-permute-done.5.refs_2_
  97.0 3.1 %collective-permute-done.6.refs_3_ = bf16[1024,256]{1,0:T(8,128)(2,1)} collective-permute-done((bf16[1024,256]{1,0:T(8,128)(2,1)}, bf16[1024,256]{1,0:T(8,128)(2,1)}, u32[]{:S(2)}, u32[]{:S(2)}) %collective-permute-start.6) | collective-permute-done | bytes 524320 | tf_op jit(solution)/shard_map/ppermute | solution.py:185
  100.1 2.1 %shard_map.70 = bf16[16,16,1024]{2,1,0:T(8,128)(2,1)S(1)} custom-call(s32[1]{0:T(128)} %bitcast.place, bf16[4,256,256]{2,1,0:T(8,128)(2,1)S(1)} %bitcast.14, bf16[1024,256]{1,0:T(8,128)(2,1)S(1)} %copy-done.1, bf16[1024,256]{1,0:T(8,128)(2,1)} %collective-permute-done.4.refs_1_, bf16[1024,256]{1,0:T(8,128)(2,1)} %collective-permute-done.5.refs_2_, ...), custom_call_target="tpu_custom_call" | custom-call | flops 536870912 | bytes 3145732 | tf_op jit(solution)/shard_map/pallas_call | solution.py:158
  102.2 24.4 %all_to_all.20.rows = bf16[16,16,1024]{2,1,0:T(8,128)(2,1)S(1)} all-to-all(bf16[16,16,1024]{2,1,0:T(8,128)(2,1)S(1)} %shard_map.70), channel_id=1, replica_groups=mesh['grp'=16,'shard'=16,'side'=4] {'grp'}, dimensions={0} | all-to-all | bytes 1048576 | tf_op jit(solution)/shard_map/all_to_all | solution.py:182
  126.7 0.3 shard_map.71
  127.0 26.2 %all_to_all.21.parts = bf16[4,64,256]{2,1,0:T(8,128)(2,1)S(1)} all-to-all(bf16[4,64,256]{2,1,0:T(8,128)(2,1)S(1)} %shard_map.71), channel_id=1, replica_groups={{0,16,32,48},{4,20,36,52},{8,24,40,56},{12,28,44,60},{1,17,33,49},{5,21..., dimensions={0} | all-to-all | bytes 262144 | tf_op jit(solution)/shard_map/all_to_all | solution.py:225
  153.2 0.6 shard_map.72
  (20 shorter events, 0.0 us)
Async XLA Ops:
  2.3 34.8 %all-to-all-start = ((bf16[16,8,2048]{2,1,0:T(8,128)(2,1)}), bf16[16,8,2048]{2,1,0:T(8,128)(2,1)S(1)}, u32[]{:S(2)}, u32[]{:S(2)}) async-start(bf16[16,8,2048]{2,1,0:T(8,128)(2,1)} %bitcast.21), calls=%async_computation | async-start | bytes 1048576 | tf_op jit(solution)/shard_map/all_to_all | solution.py:182
  37.1 8.0 %copy-start.6 = (bf16[16,8,2048]{2,1,0:T(8,128)(2,1)}, bf16[16,8,2048]{2,1,0:T(8,128)(2,1)S(1)}, u32[]{:S(2)}) copy-start(bf16[16,8,2048]{2,1,0:T(8,128)(2,1)S(1)} %all-to-all-done) | copy-start | bytes 1572868
  37.1 44.9 %all-to-all-start.1 = ((bf16[16,8,4096]{2,1,0:T(8,128)(2,1)}), bf16[16,8,4096]{2,1,0:T(8,128)(2,1)S(1)}, u32[]{:S(2)}, u32[]{:S(2)}) async-start(bf16[16,8,4096]{2,1,0:T(8,128)(2,1)} %bitcast.20), calls=%async_computation.1 | async-start | bytes 2097152 | tf_op jit(solution)/shard_map/all_to_all | solution.py:182
  40.6 36.5 %collective-permute-start = (bf16[128,2048]{1,0:T(8,128)(2,1)S(1)}, bf16[128,2048]{1,0:T(8,128)(2,1)S(1)}, u32[]{:S(2)}, u32[]{:S(2)}) collective-permute-start(bf16[128,2048]{1,0:T(8,128)(2,1)S(1)} %bitcast.18), channel_id=1, source_target_pairs={{0,4},{4,0},{8,12},{12,8},{16,20},{20,16},{24,28},{28,24},{32,36},... | collective-permute-start | bytes 1572872 | tf_op jit(solution)/shard_map/ppermute | solution.py:185
  45.0 19.8 %collective-permute-start.1 = (bf16[256,256]{1,0:T(8,128)(2,1)}, bf16[256,256]{1,0:T(8,128)(2,1)S(1)}, u32[]{:S(2)}, u32[]{:S(2)}) collective-permute-start(bf16[256,256]{1,0:T(8,128)(2,1)} %get-tuple-element.22), channel_id=1, source_target_pairs={{0,4},{4,0},{8,12},{12,8},{16,20},{20,16},{24,28},{28,24},{32,36},... | collective-permute-start | bytes 393224 | tf_op jit(solution)/shard_map/ppermute | solution.py:185
  48.4 16.4 %collective-permute-start.2 = (bf16[256,256]{1,0:T(8,128)(2,1)}, bf16[256,256]{1,0:T(8,128)(2,1)S(1)}, u32[]{:S(2)}, u32[]{:S(2)}) collective-permute-start(bf16[256,256]{1,0:T(8,128)(2,1)} %get-tuple-element.23), channel_id=1, source_target_pairs={{0,8},{4,12},{8,0},{12,4},{16,24},{20,28},{24,16},{28,20},{32,40},... | collective-permute-start | bytes 393224 | tf_op jit(solution)/shard_map/ppermute | solution.py:185
  50.3 14.5 %collective-permute-start.3 = (bf16[256,256]{1,0:T(8,128)(2,1)}, bf16[256,256]{1,0:T(8,128)(2,1)S(1)}, u32[]{:S(2)}, u32[]{:S(2)}) collective-permute-start(bf16[256,256]{1,0:T(8,128)(2,1)} %get-tuple-element.24), channel_id=1, source_target_pairs={{0,12},{4,8},{8,4},{12,0},{16,28},{20,24},{24,20},{28,16},{32,44},... | collective-permute-start | bytes 393224 | tf_op jit(solution)/shard_map/ppermute | solution.py:185
  64.8 0.6 copy-start.8
  64.8 0.7 copy-start.9
  64.8 0.7 copy-start.10
  67.5 29.5 %collective-permute-start.4 = (bf16[1024,256]{1,0:T(8,128)(2,1)}, bf16[1024,256]{1,0:T(8,128)(2,1)}, u32[]{:S(2)}, u32[]{:S(2)}) collective-permute-start(bf16[1024,256]{1,0:T(8,128)(2,1)} %shard_map.69.refs_0_), channel_id=1, source_target_pairs={{0,1},{1,0},{2,3},{3,2},{4,5},{5,4},{6,7},{7,6},{8,9},{9,8},{10,11... | collective-permute-start | bytes 1572872 | tf_op jit(solution)/shard_map/ppermute | solution.py:185
  69.4 27.6 %collective-permute-start.5 = (bf16[1024,256]{1,0:T(8,128)(2,1)}, bf16[1024,256]{1,0:T(8,128)(2,1)}, u32[]{:S(2)}, u32[]{:S(2)}) collective-permute-start(bf16[1024,256]{1,0:T(8,128)(2,1)} %shard_map.69.refs_0_), channel_id=1, source_target_pairs={{0,2},{1,3},{2,0},{3,1},{4,6},{5,7},{6,4},{7,5},{8,10},{9,11},{10,... | collective-permute-start | bytes 1572872 | tf_op jit(solution)/shard_map/ppermute | solution.py:185
  71.4 28.7 %collective-permute-start.6 = (bf16[1024,256]{1,0:T(8,128)(2,1)}, bf16[1024,256]{1,0:T(8,128)(2,1)}, u32[]{:S(2)}, u32[]{:S(2)}) collective-permute-start(bf16[1024,256]{1,0:T(8,128)(2,1)} %shard_map.69.refs_0_), channel_id=1, source_target_pairs={{0,3},{1,2},{2,1},{3,0},{4,7},{5,6},{6,5},{7,4},{8,11},{9,10},{10,... | collective-permute-start | bytes 1572872 | tf_op jit(solution)/shard_map/ppermute | solution.py:185
  77.1 0.8 copy-start.7
  77.9 4.1 %copy-start = (bf16[1,4096,256]{2,1,0:T(8,128)(2,1)S(1)}, bf16[1,4096,256]{2,1,0:T(8,128)(2,1)}, u32[]{:S(2)}) copy-start(bf16[1,4096,256]{2,1,0:T(8,128)(2,1)} %param.9) | copy-start | bytes 6291460
  82.0 18.1 %copy-start.1 = (bf16[1024,256]{1,0:T(8,128)(2,1)S(1)}, bf16[1024,256]{1,0:T(8,128)(2,1)}, u32[]{:S(2)}) copy-start(bf16[1024,256]{1,0:T(8,128)(2,1)} %shard_map.69.refs_0_) | copy-start | bytes 1572868
  100.1 26.6 %copy-start.2 = (bf16[128,64]{1,0:T(8,128)(2,1)S(1)}, bf16[128,64]{1,0:T(8,128)(2,1)}, u32[]{:S(2)}) copy-start(bf16[128,64]{1,0:T(8,128)(2,1)} %get-tuple-element.15.high_a) | copy-start | bytes 49156
  100.1 26.6 %copy-start.3 = (bf16[128,64]{1,0:T(8,128)(2,1)S(1)}, bf16[128,64]{1,0:T(8,128)(2,1)}, u32[]{:S(2)}) copy-start(bf16[128,64]{1,0:T(8,128)(2,1)} %get-tuple-element.16.low_a) | copy-start | bytes 49156
  100.1 26.6 %copy-start.4 = (bf16[128,64]{1,0:T(8,128)(2,1)S(1)}, bf16[128,64]{1,0:T(8,128)(2,1)}, u32[]{:S(2)}) copy-start(bf16[128,64]{1,0:T(8,128)(2,1)} %get-tuple-element.17.high_b) | copy-start | bytes 49156
  100.1 26.6 %copy-start.5 = (bf16[128,64]{1,0:T(8,128)(2,1)S(1)}, bf16[128,64]{1,0:T(8,128)(2,1)}, u32[]{:S(2)}) copy-start(bf16[128,64]{1,0:T(8,128)(2,1)} %get-tuple-element.18.low_b) | copy-start | bytes 49156

commit v7 on v6

--- a/solution.py
+++ b/solution.py
@@ -54,10 +54,32 @@
         sent[:, at : at + step] = dot(select, piece).astype(BF16)
 
 
-def shuffle_kernel(block, place, weights, *outs):
+def shuffle_kernel(place, weights, *refs):
+    outs, sems = refs[:-1], refs[-1]
+    _, tile, _, side = unpack(place)
+    block = outs[0].shape[1]
+    loads = []
     for k, out in enumerate(outs):
-        at = unpack(place)[3] * TPE + lax.bitwise_xor(unpack(place)[1], k)
-        out[...] = weights[:, pl.ds(pl.multiple_of(at * block, block), block)]
+        at = pl.multiple_of((side * TPE + lax.bitwise_xor(tile, k)) * block, block)
+        loads.append(pltpu.make_async_copy(weights.at[:, pl.ds(at, block)], out, sems.at[k]))
+    for load in loads:
+        load.start()
+    for load in loads:
+        load.wait()
+
+
+def shuffle(place, weights, block):
+    return pl.pallas_call(
+        shuffle_kernel,
+        out_shape=[jax.ShapeDtypeStruct((weights.shape[0], block), BF16)] * TPE,
+        in_specs=[pl.BlockSpec(memory_space=pltpu.SMEM), pl.BlockSpec(memory_space=pltpu.HBM)],
+        out_specs=[pl.BlockSpec(memory_space=pltpu.VMEM)] * TPE,
+        scratch_shapes=[pltpu.SemaphoreType.DMA((TPE,))],
+        compiler_params=pltpu.CompilerParams(vmem_limit_bytes=16 << 20),
+        cost_estimate=pl.CostEstimate(
+            flops=0, bytes_accessed=4 * TPE * weights.shape[0] * block, transcendentals=0
+        ),
+    )(place, pltpu.with_memory_space_constraint(weights, pltpu.HBM))
 
 
 def stack_kernel(*refs):
@@ -80,34 +102,52 @@
     out[...] = activate(gate, upper)
 
 
-def hidden_b_kernel(before, rows, w_gate, w_up_far, out, w_up, sems):
-    height = before.shape[0]
-    load = pltpu.make_async_copy(w_up_far, w_up, sems.at[0])
-    load.start()
-    keep = pltpu.make_async_copy(before, out.at[pl.ds(0, height), :], sems.at[1])
+def hidden_b_kernel(before, rows, w_gate_far, w_up_far, out, w_gate, w_up, sems):
+    height, pieces = before.shape[0], sems.shape[0] // 2
+    size = w_gate.shape[0] // pieces
+    keep = pltpu.make_async_copy(before, out.at[pl.ds(0, height), :], sems.at[2 * pieces])
+    loads = []
+    for c in range(pieces):
+        at = pl.ds(c * size, size)
+        for k, (far, here) in enumerate(((w_gate_far, w_gate), (w_up_far, w_up))):
+            loads.append(pltpu.make_async_copy(far.at[at, :], here.at[at, :], sems.at[2 * c + k]))
+    for load in loads:
+        load.start()
     keep.start()
-    gate = dot(rows[...], w_gate[...])
+    gate = jnp.zeros((height, w_gate.shape[1]), F32)
+    upper = jnp.zeros((height, w_up.shape[1]), F32)
+    for c in range(pieces):
+        at = slice(c * size, (c + 1) * size)
+        loads[2 * c].wait()
+        gate = gate + dot(rows[:, at], w_gate[at, :])
+        loads[2 * c + 1].wait()
+        upper = upper + dot(rows[:, at], w_up[at, :])
     keep.wait()
-    load.wait()
-    out[height:, :] = activate(gate, dot(rows[...], w_up[...]))
-
-
-def hidden_b(before, rows, w_gate, w_up):
+    out[height:, :] = activate(gate, upper)
+
+
+def hidden_b(before, rows, w_gate, w_up, pieces=4):
     height, units = before.shape
     inside = pl.BlockSpec(memory_space=pltpu.VMEM)
     outside = pl.BlockSpec(memory_space=pltpu.HBM)
-    before = pltpu.with_memory_space_constraint(before, pltpu.HBM)
+    before, w_gate, w_up = [
+        pltpu.with_memory_space_constraint(a, pltpu.HBM) for a in (before, w_gate, w_up)
+    ]
     return pl.pallas_call(
         hidden_b_kernel,
         out_shape=jax.ShapeDtypeStruct((2 * height, units), BF16),
-        in_specs=[outside, inside, inside, outside],
+        in_specs=[outside, inside, outside, outside],
         out_specs=inside,
-        scratch_shapes=[pltpu.VMEM(w_up.shape, BF16), pltpu.SemaphoreType.DMA((2,))],
+        scratch_shapes=[
+            pltpu.VMEM(w_gate.shape, BF16),
+            pltpu.VMEM(w_up.shape, BF16),
+            pltpu.SemaphoreType.DMA((2 * pieces + 1,)),
+        ],
         compiler_params=pltpu.CompilerParams(vmem_limit_bytes=16 << 20),
         cost_estimate=pl.CostEstimate(
             flops=4 * height * w_up.size, bytes_accessed=4 * w_up.size, transcendentals=0
         ),
-    )(before, rows, w_gate, pltpu.with_memory_space_constraint(w_up, pltpu.HBM))
+    )(before, rows, w_gate, w_up)
 
 
 def down_kernel(place, hidden, *refs):
@@ -196,10 +236,7 @@
     sent_a, high_a, low_a = dispatch(0, width // 2)
     mine = over_y(sent_a).reshape(rows, width // 2)
     sent_b, high_b, low_b = dispatch(1, width)
-    parts = call(
-        functools.partial(shuffle_kernel, block),
-        [((units, block), BF16)] * TPE, place, w_down[0],
-    )
+    parts = shuffle(place, w_down[0], block)
     parts = [parts[0]] + [swap(parts[k], k) for k in range(1, TPE)]
     (weight,) = call(stack_kernel, [((units * TPE, block), BF16)], *parts)
     weights = [weight] + [swap(weight, k, "side") for k in range(1, sides)]
@@ -213,6 +250,7 @@
     quartets = [[i * TPE + k for k in range(TPE)] for i in range(per_group)]
     strided = [[i * TPE + k for i in range(per_group)] for k in range(TPE)]
     hidden = lax.all_gather(hidden, "shard", axis_index_groups=quartets)
+    weights = [pltpu.with_memory_space_constraint(w, pltpu.VMEM) for w in weights]
     (result,) = call(
         down_kernel, [((groups, cap, quarter), BF16)], place, hidden, *weights,
         flops=4 * rows * width * units, limit=room,

time: 155 us -> 153 us (0.987)
  Pallas kernels: 18.8 us -> 16.7 us
    pallas_call x8 -> x7, Pallas kernels: 16.4 us -> 12.5 us  [call(): pl.pallas_call(kernel, out_shape=outs, in_specs=specs, out_specs=[pl.Bloc...]
  transfers between devices with their start and end apart: 9 -> 9, of which waited for: 3 -> 3; matrix products, arithmetic and copies ran while one was open for 0% -> 0% of each run, Pallas kernels for 9% -> 8%
where the time goes in v7:
time: 153 us
  blocking collectives  63.2 us (41%)
  starting transfers between devices  41.8 us (27%)
  waiting for transfers between devices  29.3 us (19%)
  Pallas kernels  16.7 us (11%)
    all_to_all x1, blocking collectives, on_device(): lax.all_to_all(parts, 'shard', 0, 0, tiled=True, axis_index_groups=strided)  26.7 us
    all_to_all x1, blocking collectives, over_y(): lax.all_to_all(x.reshape(groups, -1, x.shape[-1]), 'grp', 0, 0, tiled=True)  24.1 us
    all_to_all x2, starting transfers between devices, over_y(): lax.all_to_all(x.reshape(groups, -1, x.shape[-1]), 'grp', 0, 0, tiled=True)  21 us
    ppermute x7, starting transfers between devices, swap(): lax.ppermute(x, axis, [(i, i ^ bits) for i in range(lax.axis_size(axis))])  20.8 us
    all_to_all x2, waiting for transfers between devices, over_y(): lax.all_to_all(x.reshape(groups, -1, x.shape[-1]), 'grp', 0, 0, tiled=True)  14.7 us
    ppermute x7, waiting for transfers between devices, swap(): lax.ppermute(x, axis, [(i, i ^ bits) for i in range(lax.axis_size(axis))])  14.6 us
    pallas_call x7, Pallas kernels, call(): pl.pallas_call(kernel, out_shape=outs, in_specs=specs, out_specs=[pl.Bloc...  12.5 us
    all_gather x1, blocking collectives, on_device(): hidden = lax.all_gather(hidden, 'shard', axis_index_groups=quartets)  12.5 us
  transfers between devices with their start and end apart: 9, of which 3 were waited for; matrix products, arithmetic and copies ran while one was open for 0% of the time, Pallas kernels for 8%

profile of v7, /device:TPU:1, one launch (start us, length us, event | category | flops | bytes accessed | tf_op | source)
XLA Modules:
  0.0 152.5 jit_solution(17995103576698103692)
XLA Ops:
  0.0 2.3 %shard_map.64 = (bf16[128,2048]{1,0:T(8,128)(2,1)}, bf16[128,64]{1,0:T(8,128)(2,1)}, bf16[128,64]{1,0:T(8,128)(2,1)}) custom-call(s32[1]{0:T(128)} %bitcast.place, s32[8,64]{1,0:T(8,128)} %bitcast.22, f32[8,64]{1,0:T(8,128)} %bitcast.24, bf16[64,4096]{1,0:T(8,128)(2,1)} %tokens.3), custom_call_target="tpu_custom_call" | custom-call | flops 33554432 | bytes 1085444 | tf_op jit(solution)/shard_map/pallas_call | solution.py:198
  2.3 17.5 %all-to-all-start = ((bf16[16,8,2048]{2,1,0:T(8,128)(2,1)}), bf16[16,8,2048]{2,1,0:T(8,128)(2,1)S(1)}, u32[]{:S(2)}, u32[]{:S(2)}) async-start(bf16[16,8,2048]{2,1,0:T(8,128)(2,1)} %bitcast.21), calls=%async_computation | async-start | bytes 1048576 | tf_op jit(solution)/shard_map/all_to_all | solution.py:222
  19.8 2.6 %shard_map.65 = (bf16[128,4096]{1,0:T(8,128)(2,1)}, bf16[128,64]{1,0:T(8,128)(2,1)}, bf16[128,64]{1,0:T(8,128)(2,1)}) custom-call(s32[1]{0:T(128)} %bitcast.place, s32[8,64]{1,0:T(8,128)} %bitcast.23, f32[8,64]{1,0:T(8,128)} %bitcast.25, bf16[64,4096]{1,0:T(8,128)(2,1)} %tokens.3), custom_call_target="tpu_custom_call" | custom-call | flops 67108864 | bytes 1609732 | tf_op jit(solution)/shard_map/pallas_call | solution.py:198
  22.4 14.7 %all-to-all-done = bf16[16,8,2048]{2,1,0:T(8,128)(2,1)S(1)} async-done(((bf16[16,8,2048]{2,1,0:T(8,128)(2,1)}), bf16[16,8,2048]{2,1,0:T(8,128)(2,1)S(1)}, u32[]{:S(2)}, u32[]{:S(2)}) %all-to-all-start) | async-done | bytes 524320 | tf_op jit(solution)/shard_map/all_to_all | solution.py:222
  37.1 3.6 %all-to-all-start.1 = ((bf16[16,8,4096]{2,1,0:T(8,128)(2,1)}), bf16[16,8,4096]{2,1,0:T(8,128)(2,1)S(1)}, u32[]{:S(2)}, u32[]{:S(2)}) async-start(bf16[16,8,4096]{2,1,0:T(8,128)(2,1)} %bitcast.20), calls=%async_computation.1 | async-start | bytes 2097152 | tf_op jit(solution)/shard_map/all_to_all | solution.py:222
  40.6 1.9 %collective-permute-start = (bf16[128,2048]{1,0:T(8,128)(2,1)S(1)}, bf16[128,2048]{1,0:T(8,128)(2,1)}, u32[]{:S(2)}, u32[]{:S(2)}) collective-permute-start(bf16[128,2048]{1,0:T(8,128)(2,1)S(1)} %bitcast.18), channel_id=1, source_target_pairs={{0,4},{4,0},{8,12},{12,8},{16,20},{20,16},{24,28},{28,24},{32,36},... | collective-permute-start | bytes 1572872 | tf_op jit(solution)/shard_map/ppermute | solution.py:225
  42.6 1.1 shard_map.68
  43.7 0.6 copy-done.1
  44.4 3.4 %collective-permute-start.1 = (bf16[256,256]{1,0:T(8,128)(2,1)S(1)}, bf16[256,256]{1,0:T(8,128)(2,1)S(1)}, u32[]{:S(2)}, u32[]{:S(2)}) collective-permute-start(bf16[256,256]{1,0:T(8,128)(2,1)S(1)} %get-tuple-element.22), channel_id=1, source_target_pairs={{0,4},{4,0},{8,12},{12,8},{16,20},{20,16},{24,28},{28,24},{32,36},... | collective-permute-start | bytes 393224 | tf_op jit(solution)/shard_map/ppermute | solution.py:225
  47.7 1.9 %collective-permute-start.2 = (bf16[256,256]{1,0:T(8,128)(2,1)S(1)}, bf16[256,256]{1,0:T(8,128)(2,1)S(1)}, u32[]{:S(2)}, u32[]{:S(2)}) collective-permute-start(bf16[256,256]{1,0:T(8,128)(2,1)S(1)} %get-tuple-element.23), channel_id=1, source_target_pairs={{0,8},{4,12},{8,0},{12,4},{16,24},{20,28},{24,16},{28,20},{32,40},... | collective-permute-start | bytes 393224 | tf_op jit(solution)/shard_map/ppermute | solution.py:225
  49.7 4.0 %collective-permute-start.3 = (bf16[256,256]{1,0:T(8,128)(2,1)S(1)}, bf16[256,256]{1,0:T(8,128)(2,1)S(1)}, u32[]{:S(2)}, u32[]{:S(2)}) collective-permute-start(bf16[256,256]{1,0:T(8,128)(2,1)S(1)} %get-tuple-element.24), channel_id=1, source_target_pairs={{0,12},{4,8},{8,4},{12,0},{16,28},{20,24},{24,20},{28,16},{32,44},... | collective-permute-start | bytes 393224 | tf_op jit(solution)/shard_map/ppermute | solution.py:225
  53.7 11.2 %collective-permute-done.1.refs_1_ = bf16[256,256]{1,0:T(8,128)(2,1)S(1)} collective-permute-done((bf16[256,256]{1,0:T(8,128)(2,1)S(1)}, bf16[256,256]{1,0:T(8,128)(2,1)S(1)}, u32[]{:S(2)}, u32[]{:S(2)}) %collective-permute-start.1) | collective-permute-done | bytes 131104 | tf_op jit(solution)/shard_map/ppermute | solution.py:225
  64.8 0.0 collective-permute-done.2.refs_2_
  64.8 0.0 collective-permute-done.3.refs_3_
  64.9 0.6 copy-done.7
  65.5 0.1 copy-done.8
  65.6 0.0 copy-done.9
  65.6 1.9 %shard_map.69.refs_0_ = bf16[1024,256]{1,0:T(8,128)(2,1)} custom-call(bf16[256,256]{1,0:T(8,128)(2,1)} %copy-done.1, bf16[256,256]{1,0:T(8,128)(2,1)} %copy-done.7, bf16[256,256]{1,0:T(8,128)(2,1)} %copy-done.8, bf16[256,256]{1,0:T(8,128)(2,1)} %copy-done.9), custom_call_target="tpu_custom_call" | custom-call | bytes 1048576 | tf_op jit(solution)/shard_map/pallas_call | solution.py:198
  67.5 1.9 %collective-permute-start.4 = (bf16[1024,256]{1,0:T(8,128)(2,1)}, bf16[1024,256]{1,0:T(8,128)(2,1)S(1)}, u32[]{:S(2)}, u32[]{:S(2)}) collective-permute-start(bf16[1024,256]{1,0:T(8,128)(2,1)} %shard_map.69.refs_0_), channel_id=1, source_target_pairs={{0,1},{1,0},{2,3},{3,2},{4,5},{5,4},{6,7},{7,6},{8,9},{9,8},{10,11... | collective-permute-start | bytes 1572872 | tf_op jit(solution)/shard_map/ppermute | solution.py:225
  69.4 1.9 %collective-permute-start.5 = (bf16[1024,256]{1,0:T(8,128)(2,1)}, bf16[1024,256]{1,0:T(8,128)(2,1)S(1)}, u32[]{:S(2)}, u32[]{:S(2)}) collective-permute-start(bf16[1024,256]{1,0:T(8,128)(2,1)} %shard_map.69.refs_0_), channel_id=1, source_target_pairs={{0,2},{1,3},{2,0},{3,1},{4,6},{5,7},{6,4},{7,5},{8,10},{9,11},{10,... | collective-permute-start | bytes 1572872 | tf_op jit(solution)/shard_map/ppermute | solution.py:225
  71.3 5.7 %collective-permute-start.6 = (bf16[1024,256]{1,0:T(8,128)(2,1)}, bf16[1024,256]{1,0:T(8,128)(2,1)S(1)}, u32[]{:S(2)}, u32[]{:S(2)}) collective-permute-start(bf16[1024,256]{1,0:T(8,128)(2,1)} %shard_map.69.refs_0_), channel_id=1, source_target_pairs={{0,3},{1,2},{2,1},{3,0},{4,7},{5,6},{6,5},{7,4},{8,11},{9,10},{10,... | collective-permute-start | bytes 1572872 | tf_op jit(solution)/shard_map/ppermute | solution.py:225
  77.1 0.0 collective-permute-done.other
  77.1 3.9 %shard_map.66.before = bf16[128,256]{1,0:T(8,128)(2,1)} custom-call(s32[1]{0:T(128)} %bitcast.place, bf16[128,2048]{1,0:T(8,128)(2,1)} %bitcast.19, bf16[128,2048]{1,0:T(8,128)(2,1)} %collective-permute-done.other, bf16[4096,256]{1,0:T(8,128)(2,1)} %bitcast.13, bf16[4096,256]{1,0:T(8,128)(2,1)} %bitcast.15), custom_call_target="tpu_custom_call" | custom-call | flops 536870912 | bytes 5308420 | tf_op jit(solution)/shard_map/pallas_call | solution.py:198
  81.0 0.0 all-to-all-done.1
  81.0 3.1 %shard_map.67 = bf16[256,256]{1,0:T(8,128)(2,1)S(1)} custom-call(bf16[128,256]{1,0:T(8,128)(2,1)} %shard_map.66.before, bf16[128,4096]{1,0:T(8,128)(2,1)S(1)} %bitcast.11, bf16[4096,256]{1,0:T(8,128)(2,1)} %bitcast.14, bf16[4096,256]{1,0:T(8,128)(2,1)} %bitcast.16), custom_call_target="tpu_custom_call" | custom-call | flops 536870912 | bytes 4194304 | tf_op jit(solution)/shard_map/pallas_call | solution.py:136
  84.1 12.5 %all-gather = bf16[1024,256]{1,0:T(8,128)(2,1)S(1)} all-gather(bf16[256,256]{1,0:T(8,128)(2,1)S(1)} %shard_map.67), channel_id=2, replica_groups={{0,4,8,12},{16,20,24,28},{32,36,40,44},{48,52,56,60},{1,5,9,13},{17,21,..., dimensions={0}, use_global_device_ids=true | all-gather | bytes 655360 | tf_op jit(solution)/shard_map/all_gather | solution.py:252
  96.6 3.4 %collective-permute-done.6.refs_3_ = bf16[1024,256]{1,0:T(8,128)(2,1)S(1)} collective-permute-done((bf16[1024,256]{1,0:T(8,128)(2,1)}, bf16[1024,256]{1,0:T(8,128)(2,1)S(1)}, u32[]{:S(2)}, u32[]{:S(2)}) %collective-permute-start.6) | collective-permute-done | bytes 524320 | tf_op jit(solution)/shard_map/ppermute | solution.py:225
  100.0 0.7 shard_map.70
  100.7 24.1 %all_to_all.20.rows = bf16[16,16,1024]{2,1,0:T(8,128)(2,1)S(1)} all-to-all(bf16[16,16,1024]{2,1,0:T(8,128)(2,1)S(1)} %shard_map.70), channel_id=1, replica_groups=mesh['grp'=16,'shard'=16,'side'=4] {'grp'}, dimensions={0} | all-to-all | bytes 1048576 | tf_op jit(solution)/shard_map/all_to_all | solution.py:222
  124.9 0.3 shard_map.71
  125.2 26.7 %all_to_all.21.parts = bf16[4,64,256]{2,1,0:T(8,128)(2,1)S(1)} all-to-all(bf16[4,64,256]{2,1,0:T(8,128)(2,1)S(1)} %shard_map.71), channel_id=1, replica_groups={{0,16,32,48},{4,20,36,52},{8,24,40,56},{12,28,44,60},{1,17,33,49},{5,21..., dimensions={0} | all-to-all | bytes 262144 | tf_op jit(solution)/shard_map/all_to_all | solution.py:263
  151.9 0.6 shard_map.72
  (18 shorter events, 0.0 us)
Async XLA Ops:
  2.3 34.8 %all-to-all-start = ((bf16[16,8,2048]{2,1,0:T(8,128)(2,1)}), bf16[16,8,2048]{2,1,0:T(8,128)(2,1)S(1)}, u32[]{:S(2)}, u32[]{:S(2)}) async-start(bf16[16,8,2048]{2,1,0:T(8,128)(2,1)} %bitcast.21), calls=%async_computation | async-start | bytes 1048576 | tf_op jit(solution)/shard_map/all_to_all | solution.py:222
  37.1 6.6 %copy-start.6 = (bf16[16,8,2048]{2,1,0:T(8,128)(2,1)}, bf16[16,8,2048]{2,1,0:T(8,128)(2,1)S(1)}, u32[]{:S(2)}) copy-start(bf16[16,8,2048]{2,1,0:T(8,128)(2,1)S(1)} %all-to-all-done) | copy-start | bytes 1572868
  37.1 43.9 %all-to-all-start.1 = ((bf16[16,8,4096]{2,1,0:T(8,128)(2,1)}), bf16[16,8,4096]{2,1,0:T(8,128)(2,1)S(1)}, u32[]{:S(2)}, u32[]{:S(2)}) async-start(bf16[16,8,4096]{2,1,0:T(8,128)(2,1)} %bitcast.20), calls=%async_computation.1 | async-start | bytes 2097152 | tf_op jit(solution)/shard_map/all_to_all | solution.py:222
  40.6 36.5 %collective-permute-start = (bf16[128,2048]{1,0:T(8,128)(2,1)S(1)}, bf16[128,2048]{1,0:T(8,128)(2,1)}, u32[]{:S(2)}, u32[]{:S(2)}) collective-permute-start(bf16[128,2048]{1,0:T(8,128)(2,1)S(1)} %bitcast.18), channel_id=1, source_target_pairs={{0,4},{4,0},{8,12},{12,8},{16,20},{20,16},{24,28},{28,24},{32,36},... | collective-permute-start | bytes 1572872 | tf_op jit(solution)/shard_map/ppermute | solution.py:225
  43.7 0.7 copy-start.1
  44.4 20.5 %collective-permute-start.1 = (bf16[256,256]{1,0:T(8,128)(2,1)S(1)}, bf16[256,256]{1,0:T(8,128)(2,1)S(1)}, u32[]{:S(2)}, u32[]{:S(2)}) collective-permute-start(bf16[256,256]{1,0:T(8,128)(2,1)S(1)} %get-tuple-element.22), channel_id=1, source_target_pairs={{0,4},{4,0},{8,12},{12,8},{16,20},{20,16},{24,28},{28,24},{32,36},... | collective-permute-start | bytes 393224 | tf_op jit(solution)/shard_map/ppermute | solution.py:225
  47.7 17.1 %collective-permute-start.2 = (bf16[256,256]{1,0:T(8,128)(2,1)S(1)}, bf16[256,256]{1,0:T(8,128)(2,1)S(1)}, u32[]{:S(2)}, u32[]{:S(2)}) collective-permute-start(bf16[256,256]{1,0:T(8,128)(2,1)S(1)} %get-tuple-element.23), channel_id=1, source_target_pairs={{0,8},{4,12},{8,0},{12,4},{16,24},{20,28},{24,16},{28,20},{32,40},... | collective-permute-start | bytes 393224 | tf_op jit(solution)/shard_map/ppermute | solution.py:225
  49.7 15.2 %collective-permute-start.3 = (bf16[256,256]{1,0:T(8,128)(2,1)S(1)}, bf16[256,256]{1,0:T(8,128)(2,1)S(1)}, u32[]{:S(2)}, u32[]{:S(2)}) collective-permute-start(bf16[256,256]{1,0:T(8,128)(2,1)S(1)} %get-tuple-element.24), channel_id=1, source_target_pairs={{0,12},{4,8},{8,4},{12,0},{16,28},{20,24},{24,20},{28,16},{32,44},... | collective-permute-start | bytes 393224 | tf_op jit(solution)/shard_map/ppermute | solution.py:225
  64.8 0.6 copy-start.7
  64.8 0.7 copy-start.8
  64.9 0.7 copy-start.9
  67.5 29.1 %collective-permute-start.4 = (bf16[1024,256]{1,0:T(8,128)(2,1)}, bf16[1024,256]{1,0:T(8,128)(2,1)S(1)}, u32[]{:S(2)}, u32[]{:S(2)}) collective-permute-start(bf16[1024,256]{1,0:T(8,128)(2,1)} %shard_map.69.refs_0_), channel_id=1, source_target_pairs={{0,1},{1,0},{2,3},{3,2},{4,5},{5,4},{6,7},{7,6},{8,9},{9,8},{10,11... | collective-permute-start | bytes 1572872 | tf_op jit(solution)/shard_map/ppermute | solution.py:225
  69.4 27.1 %collective-permute-start.5 = (bf16[1024,256]{1,0:T(8,128)(2,1)}, bf16[1024,256]{1,0:T(8,128)(2,1)S(1)}, u32[]{:S(2)}, u32[]{:S(2)}) collective-permute-start(bf16[1024,256]{1,0:T(8,128)(2,1)} %shard_map.69.refs_0_), channel_id=1, source_target_pairs={{0,2},{1,3},{2,0},{3,1},{4,6},{5,7},{6,4},{7,5},{8,10},{9,11},{10,... | collective-permute-start | bytes 1572872 | tf_op jit(solution)/shard_map/ppermute | solution.py:225
  71.3 28.6 %collective-permute-start.6 = (bf16[1024,256]{1,0:T(8,128)(2,1)}, bf16[1024,256]{1,0:T(8,128)(2,1)S(1)}, u32[]{:S(2)}, u32[]{:S(2)}) collective-permute-start(bf16[1024,256]{1,0:T(8,128)(2,1)} %shard_map.69.refs_0_), channel_id=1, source_target_pairs={{0,3},{1,2},{2,1},{3,0},{4,7},{5,6},{6,5},{7,4},{8,11},{9,10},{10,... | collective-permute-start | bytes 1572872 | tf_op jit(solution)/shard_map/ppermute | solution.py:225
  81.0 18.9 %copy-start = (bf16[1024,256]{1,0:T(8,128)(2,1)S(1)}, bf16[1024,256]{1,0:T(8,128)(2,1)}, u32[]{:S(2)}) copy-start(bf16[1024,256]{1,0:T(8,128)(2,1)} %shard_map.69.refs_0_) | copy-start | bytes 1572868
  100.0 24.9 %copy-start.2 = (bf16[128,64]{1,0:T(8,128)(2,1)S(1)}, bf16[128,64]{1,0:T(8,128)(2,1)}, u32[]{:S(2)}) copy-start(bf16[128,64]{1,0:T(8,128)(2,1)} %get-tuple-element.15.high_a) | copy-start | bytes 49156
  100.0 24.9 %copy-start.3 = (bf16[128,64]{1,0:T(8,128)(2,1)S(1)}, bf16[128,64]{1,0:T(8,128)(2,1)}, u32[]{:S(2)}) copy-start(bf16[128,64]{1,0:T(8,128)(2,1)} %get-tuple-element.16.low_a) | copy-start | bytes 49156
  100.0 24.9 %copy-start.4 = (bf16[128,64]{1,0:T(8,128)(2,1)S(1)}, bf16[128,64]{1,0:T(8,128)(2,1)}, u32[]{:S(2)}) copy-start(bf16[128,64]{1,0:T(8,128)(2,1)} %get-tuple-element.17.high_b) | copy-start | bytes 49156
  100.0 24.9 %copy-start.5 = (bf16[128,64]{1,0:T(8,128)(2,1)S(1)}, bf16[128,64]{1,0:T(8,128)(2,1)}, u32[]{:S(2)}) copy-start(bf16[128,64]{1,0:T(8,128)(2,1)} %get-tuple-element.18.low_b) | copy-start | bytes 49156

commit v8 on v7

--- a/solution.py
+++ b/solution.py
@@ -23,11 +23,10 @@
     return quartet, tile, lax.bitwise_and(z, 1), lax.bitwise_and(place[0], 3)
 
 
-def dispatch_kernel(cap, per_group, part, place, routes, probs, tokens, sent, high, low):
+def dispatch_kernel(cap, per_group, part, place, routes, tokens, sent):
     tok = tokens.shape[0]
     rows, width = sent.shape
     half = cap // 2
-    gates = probs[...] / jnp.sum(probs[...], axis=0, keepdims=True)
     before = lax.broadcasted_iota(jnp.int32, (tok, tok), 0)
     before = before < lax.broadcasted_iota(jnp.int32, (tok, tok), 1)
     before = jnp.where(before, F32(1.0), F32(0.0)).astype(BF16)
@@ -35,23 +34,38 @@
     target = lax.shift_right_logical(row, half.bit_length() - 1) * per_group + unpack(place)[0]
     slot = (lax.bitwise_and(row, half - 1) + part * half).astype(F32)
     hits = jnp.zeros((rows, tok), F32)
+    for k in range(routes.shape[0]):
+        hits = jnp.where(routes[k : k + 1, :] == target, F32(1.0), hits)
+    ranks = dot(hits.astype(BF16), before)
+    chosen = (hits > 0.5) & (ranks == slot)
+    select = jnp.where(chosen, F32(1.0), F32(0.0)).astype(BF16)
+    step = min(512, width)
+    for at in range(0, width, step):
+        start = unpack(place)[2] * width + at if part == 0 else at
+        piece = tokens[:, pl.ds(pl.multiple_of(start, step), step)]
+        sent[:, at : at + step] = dot(select, piece).astype(BF16)
+
+
+def factor_kernel(cap, routes, probs, high, low):
+    rows, tok = high.shape
+    gates = probs[...] / jnp.sum(probs[...], axis=0, keepdims=True)
+    before = lax.broadcasted_iota(jnp.int32, (tok, tok), 0)
+    before = before < lax.broadcasted_iota(jnp.int32, (tok, tok), 1)
+    before = jnp.where(before, F32(1.0), F32(0.0)).astype(BF16)
+    row = lax.broadcasted_iota(jnp.int32, (rows, tok), 0)
+    target = lax.shift_right_logical(row, cap.bit_length() - 1)
+    slot = lax.bitwise_and(row, cap - 1).astype(F32)
+    hits = jnp.zeros((rows, tok), F32)
     weight = jnp.zeros((rows, tok), F32)
     for k in range(routes.shape[0]):
         match = routes[k : k + 1, :] == target
         hits = jnp.where(match, F32(1.0), hits)
         weight = jnp.where(match, gates[k : k + 1, :], weight)
-    ranks = dot(hits.astype(BF16), before)
-    chosen = (hits > 0.5) & (ranks == slot)
-    select = jnp.where(chosen, F32(1.0), F32(0.0)).astype(BF16)
-    mine = jnp.where(chosen, weight, F32(0.0))
-    top = mine.astype(BF16)
+    chosen = (hits > 0.5) & (dot(hits.astype(BF16), before) == slot)
+    weight = jnp.where(chosen, weight, F32(0.0))
+    top = weight.astype(BF16)
     high[...] = top
-    low[...] = (mine - top.astype(F32)).astype(BF16)
-    step = min(512, width)
-    for at in range(0, width, step):
-        start = unpack(place)[2] * width + at if part == 0 else at
-        piece = tokens[:, pl.ds(pl.multiple_of(start, step), step)]
-        sent[:, at : at + step] = dot(select, piece).astype(BF16)
+    low[...] = (weight - top.astype(F32)).astype(BF16)
 
 
 def shuffle_kernel(place, weights, *refs):
@@ -152,8 +166,7 @@
 
 def down_kernel(place, hidden, *refs):
     weights, out = refs[:-1], refs[-1]
-    groups, cap, _ = out.shape
-    block = weights[0].shape[1]
+    groups, _, cap, block = out.shape
     count, height, units = hidden.shape
     _, tile, _, own_side = unpack(place)
     for side, weight in enumerate(weights):
@@ -161,31 +174,15 @@
         for k in range(count):
             rows = hidden[lax.bitwise_xor(tile, k)]
             total = total + dot(rows, weight[k * units : (k + 1) * units, :])
-        at = pl.multiple_of(lax.bitwise_xor(own_side, side) * block, block)
+        at = lax.bitwise_xor(own_side, side)
         total = total.reshape(2, groups, cap // 2, block).astype(BF16)
         for part in range(2):
             slots = slice(part * cap // 2, (part + 1) * cap // 2)
-            out[:, slots, pl.ds(at, block)] = total[part]
-
-
-def combine_kernel(high_a, low_a, high_b, low_b, rows, out):
-    count, tok, block = out.shape
-    groups, cap, _ = rows.shape
-    for k in range(count):
-        total = jnp.zeros((tok, block), F32)
-        for part, pair in enumerate(((high_a, low_a), (high_b, low_b))):
-            slots = slice(part * cap // 2, (part + 1) * cap // 2)
-            piece = rows[:, slots, k * block : (k + 1) * block].astype(F32)
-            piece = piece.reshape(groups * cap // 2, block).astype(BF16)
-            for factor in pair:
-                total = total + dot(factor[...], piece, ((0,), (0,)))
-        out[k] = total.astype(BF16)
-
-
-def finish_kernel(parts, out):
-    total = parts[0].astype(F32)
-    for k in range(1, parts.shape[0]):
-        total = total + parts[k].astype(F32)
+            out[:, at, slots, :] = total[part]
+
+
+def combine_kernel(high, low, rows, out):
+    total = dot(high[...], rows[...], ((0,), (0,))) + dot(low[...], rows[...], ((0,), (0,)))
     out[...] = total.astype(BF16)
 
 
@@ -210,7 +207,7 @@
     per_group = shards // TPE
     tok, width = tokens.shape
     units = w_down.shape[1]
-    block, quarter = width // shards, width // TPE
+    block = width // shards
     cap = 2 * tok * routes.shape[1] // (groups * per_group)
     rows = groups * cap // 2
     room = 16 << 20
@@ -224,18 +221,22 @@
     def swap(x, bits, axis="shard"):
         return lax.ppermute(x, axis, [(i, i ^ bits) for i in range(lax.axis_size(axis))])
 
-    factor = ((rows, tok), BF16)
-
     def dispatch(part, size):
-        return call(
+        (sent,) = call(
             functools.partial(dispatch_kernel, cap, per_group, part),
-            [((rows, size), BF16), factor, factor],
-            place, routes.T, probs.T, tokens, flops=2 * rows * tok * size,
+            [((rows, size), BF16)],
+            place, routes.T, tokens, flops=2 * rows * tok * size,
         )
-
-    sent_a, high_a, low_a = dispatch(0, width // 2)
+        return sent
+
+    sent_a = dispatch(0, width // 2)
     mine = over_y(sent_a).reshape(rows, width // 2)
-    sent_b, high_b, low_b = dispatch(1, width)
+    sent_b = dispatch(1, width)
+    slots = groups * per_group * cap
+    high, low = call(
+        functools.partial(factor_kernel, cap), [((slots, tok), BF16)] * 2,
+        routes.T, probs.T, flops=2 * slots * tok * tok,
+    )
     parts = shuffle(place, w_down[0], block)
     parts = [parts[0]] + [swap(parts[k], k) for k in range(1, TPE)]
     (weight,) = call(stack_kernel, [((units * TPE, block), BF16)], *parts)
@@ -248,20 +249,24 @@
     )
     hidden = hidden_b(hidden, arrived, w_gate[0], w_up[0])
     quartets = [[i * TPE + k for k in range(TPE)] for i in range(per_group)]
-    strided = [[i * TPE + k for i in range(per_group)] for k in range(TPE)]
     hidden = lax.all_gather(hidden, "shard", axis_index_groups=quartets)
     weights = [pltpu.with_memory_space_constraint(w, pltpu.VMEM) for w in weights]
     (result,) = call(
-        down_kernel, [((groups, cap, quarter), BF16)], place, hidden, *weights,
+        down_kernel, [((groups, TPE, cap, block), BF16)], place, hidden, *weights,
         flops=4 * rows * width * units, limit=room,
     )
-    returned = over_y(result)
-    (parts,) = call(
-        combine_kernel, [((per_group, tok, block), BF16)],
-        high_a, low_a, high_b, low_b, returned, limit=room,
-    )
-    parts = lax.all_to_all(parts, "shard", 0, 0, tiled=True, axis_index_groups=strided)
-    (mixed,) = call(finish_kernel, [((tok, block), BF16)], parts, limit=room)
+    homes = [
+        [(g * per_group + q) * TPE + k for g in range(groups) for q in range(per_group)]
+        for k in range(TPE)
+    ]
+    result = result.reshape(groups * TPE, cap, block)
+    returned = lax.all_to_all(
+        result, ("grp", "shard"), 0, 0, tiled=True, axis_index_groups=homes
+    ).reshape(slots, block)
+    (mixed,) = call(
+        combine_kernel, [((tok, block), BF16)], high, low, returned,
+        flops=4 * slots * tok * block, limit=room,
+    )
     return mixed
 
 

time: 153 us -> 158 us (1.033)
  blocking collectives: 63.2 us -> 12.5 us
  waiting for transfers between devices: 29.3 us -> 60.7 us
  starting transfers between devices: 41.8 us -> 61.3 us
  Pallas kernels: 16.7 us -> 19.7 us
  local copies, waits for them, and re-layouts: 1.39 us -> 3.28 us
    all_to_all x2 -> x0, blocking collectives: 50.8 us -> none  [the longest x1 26.7 us: on_device(): lax.all_to_all(parts, 'shard', 0, 0, tiled=True, axis_index_groups=strided)]
    all_to_all x0 -> x1, waiting for transfers between devices: none -> 31.4 us  [on_device(): lax.all_to_all(result, ('grp', 'shard'), 0, 0, tiled=True, axis_index_gro...]
    all_to_all x0 -> x1, starting transfers between devices: none -> 19.5 us  [on_device(): lax.all_to_all(result, ('grp', 'shard'), 0, 0, tiled=True, axis_index_gro...]
    pallas_call x7, Pallas kernels: 12.5 us -> 15.5 us  [call(): pl.pallas_call(kernel, out_shape=outs, in_specs=specs, out_specs=[pl.Bloc...]
    unnamed x20 -> x16, local copies, waits for them, and re-layouts: 1.39 us -> 3.28 us
  transfers between devices with their start and end apart: 9 -> 10, of which waited for: 3 -> 4; matrix products, arithmetic and copies ran while one was open for 0% -> 0% of each run, Pallas kernels for 8% -> 9%
where the time goes in v8:
time: 158 us
  starting transfers between devices  61.3 us (39%)
  waiting for transfers between devices  60.7 us (38%)
  Pallas kernels  19.7 us (12%)
  blocking collectives  12.5 us (8%)
  local copies, waits for them, and re-layouts  3.28 us (2%)
    all_to_all x1, waiting for transfers between devices, on_device(): lax.all_to_all(result, ('grp', 'shard'), 0, 0, tiled=True, axis_index_gro...  31.4 us
    all_to_all x2, starting transfers between devices, over_y(): lax.all_to_all(x.reshape(groups, -1, x.shape[-1]), 'grp', 0, 0, tiled=True)  21 us
    ppermute x7, starting transfers between devices, swap(): lax.ppermute(x, axis, [(i, i ^ bits) for i in range(lax.axis_size(axis))])  20.8 us
    all_to_all x1, starting transfers between devices, on_device(): lax.all_to_all(result, ('grp', 'shard'), 0, 0, tiled=True, axis_index_gro...  19.5 us
    pallas_call x7, Pallas kernels, call(): pl.pallas_call(kernel, out_shape=outs, in_specs=specs, out_specs=[pl.Bloc...  15.5 us
    all_to_all x2, waiting for transfers between devices, over_y(): lax.all_to_all(x.reshape(groups, -1, x.shape[-1]), 'grp', 0, 0, tiled=True)  14.7 us
    ppermute x7, waiting for transfers between devices, swap(): lax.ppermute(x, axis, [(i, i ^ bits) for i in range(lax.axis_size(axis))])  14.6 us
    all_gather x1, blocking collectives, on_device(): hidden = lax.all_gather(hidden, 'shard', axis_index_groups=quartets)  12.5 us
  transfers between devices with their start and end apart: 10, of which 4 were waited for; matrix products, arithmetic and copies ran while one was open for 0% of the time, Pallas kernels for 9%

profile of v8, /device:TPU:1, one launch (start us, length us, event | category | flops | bytes accessed | tf_op | source)
XLA Modules:
  0.0 157.5 jit_solution(14143842827542695560)
XLA Ops:
  0.0 2.3 %shard_map.65 = bf16[128,2048]{1,0:T(8,128)(2,1)} custom-call(s32[1]{0:T(128)} %bitcast.2.place, s32[8,64]{1,0:T(8,128)} %bitcast.25, bf16[64,4096]{1,0:T(8,128)(2,1)} %tokens.3), custom_call_target="tpu_custom_call" | custom-call | flops 33554432 | bytes 1050628 | tf_op jit(solution)/shard_map/pallas_call | solution.py:195
  2.3 17.5 %all-to-all-start = ((bf16[16,8,2048]{2,1,0:T(8,128)(2,1)}), bf16[16,8,2048]{2,1,0:T(8,128)(2,1)S(1)}, u32[]{:S(2)}, u32[]{:S(2)}) async-start(bf16[16,8,2048]{2,1,0:T(8,128)(2,1)} %bitcast.22), calls=%async_computation | async-start | bytes 1048576 | tf_op jit(solution)/shard_map/all_to_all | solution.py:219
  19.7 2.6 %shard_map.67 = bf16[128,4096]{1,0:T(8,128)(2,1)} custom-call(s32[1]{0:T(128)} %bitcast.2.place, s32[8,64]{1,0:T(8,128)} %bitcast.26, bf16[64,4096]{1,0:T(8,128)(2,1)} %tokens.3), custom_call_target="tpu_custom_call" | custom-call | flops 67108864 | bytes 1574916 | tf_op jit(solution)/shard_map/pallas_call | solution.py:195
  22.3 14.7 %all-to-all-done = bf16[16,8,2048]{2,1,0:T(8,128)(2,1)S(1)} async-done(((bf16[16,8,2048]{2,1,0:T(8,128)(2,1)}), bf16[16,8,2048]{2,1,0:T(8,128)(2,1)S(1)}, u32[]{:S(2)}, u32[]{:S(2)}) %all-to-all-start) | async-done | bytes 524320 | tf_op jit(solution)/shard_map/all_to_all | solution.py:219
  37.0 3.6 %all-to-all-start.1 = ((bf16[16,8,4096]{2,1,0:T(8,128)(2,1)}), bf16[16,8,4096]{2,1,0:T(8,128)(2,1)S(1)}, u32[]{:S(2)}, u32[]{:S(2)}) async-start(bf16[16,8,4096]{2,1,0:T(8,128)(2,1)} %bitcast.20), calls=%async_computation.1 | async-start | bytes 2097152 | tf_op jit(solution)/shard_map/all_to_all | solution.py:219
  40.6 1.9 %collective-permute-start = (bf16[128,2048]{1,0:T(8,128)(2,1)S(1)}, bf16[128,2048]{1,0:T(8,128)(2,1)}, u32[]{:S(2)}, u32[]{:S(2)}) collective-permute-start(bf16[128,2048]{1,0:T(8,128)(2,1)S(1)} %bitcast.23), channel_id=1, source_target_pairs={{0,4},{4,0},{8,12},{12,8},{16,20},{20,16},{24,28},{28,24},{32,36},... | collective-permute-start | bytes 1572872 | tf_op jit(solution)/shard_map/ppermute | solution.py:222
  42.5 1.1 shard_map.69
  43.7 0.6 copy-done.3
  44.4 3.4 %collective-permute-start.1 = (bf16[256,256]{1,0:T(8,128)(2,1)S(1)}, bf16[256,256]{1,0:T(8,128)(2,1)S(1)}, u32[]{:S(2)}, u32[]{:S(2)}) collective-permute-start(bf16[256,256]{1,0:T(8,128)(2,1)S(1)} %get-tuple-element.14), channel_id=1, source_target_pairs={{0,4},{4,0},{8,12},{12,8},{16,20},{20,16},{24,28},{28,24},{32,36},... | collective-permute-start | bytes 393224 | tf_op jit(solution)/shard_map/ppermute | solution.py:222
  47.7 1.9 %collective-permute-start.2 = (bf16[256,256]{1,0:T(8,128)(2,1)S(1)}, bf16[256,256]{1,0:T(8,128)(2,1)S(1)}, u32[]{:S(2)}, u32[]{:S(2)}) collective-permute-start(bf16[256,256]{1,0:T(8,128)(2,1)S(1)} %get-tuple-element.15), channel_id=1, source_target_pairs={{0,8},{4,12},{8,0},{12,4},{16,24},{20,28},{24,16},{28,20},{32,40},... | collective-permute-start | bytes 393224 | tf_op jit(solution)/shard_map/ppermute | solution.py:222
  49.6 4.0 %collective-permute-start.3 = (bf16[256,256]{1,0:T(8,128)(2,1)S(1)}, bf16[256,256]{1,0:T(8,128)(2,1)S(1)}, u32[]{:S(2)}, u32[]{:S(2)}) collective-permute-start(bf16[256,256]{1,0:T(8,128)(2,1)S(1)} %get-tuple-element.16), channel_id=1, source_target_pairs={{0,12},{4,8},{8,4},{12,0},{16,28},{20,24},{24,20},{28,16},{32,44},... | collective-permute-start | bytes 393224 | tf_op jit(solution)/shard_map/ppermute | solution.py:222
  53.6 11.2 %collective-permute-done.1.refs_1_ = bf16[256,256]{1,0:T(8,128)(2,1)S(1)} collective-permute-done((bf16[256,256]{1,0:T(8,128)(2,1)S(1)}, bf16[256,256]{1,0:T(8,128)(2,1)S(1)}, u32[]{:S(2)}, u32[]{:S(2)}) %collective-permute-start.1) | collective-permute-done | bytes 131104 | tf_op jit(solution)/shard_map/ppermute | solution.py:222
  64.8 0.0 collective-permute-done.2.refs_2_
  64.8 0.0 collective-permute-done.3.refs_3_
  64.8 0.6 copy-done.5
  65.5 0.1 copy-done.6
  65.5 0.0 copy-done.7
  65.6 1.9 %shard_map.70.refs_0_ = bf16[1024,256]{1,0:T(8,128)(2,1)} custom-call(bf16[256,256]{1,0:T(8,128)(2,1)} %copy-done.3, bf16[256,256]{1,0:T(8,128)(2,1)} %copy-done.5, bf16[256,256]{1,0:T(8,128)(2,1)} %copy-done.6, bf16[256,256]{1,0:T(8,128)(2,1)} %copy-done.7), custom_call_target="tpu_custom_call" | custom-call | bytes 1048576 | tf_op jit(solution)/shard_map/pallas_call | solution.py:195
  67.5 1.9 %collective-permute-start.4 = (bf16[1024,256]{1,0:T(8,128)(2,1)}, bf16[1024,256]{1,0:T(8,128)(2,1)S(1)}, u32[]{:S(2)}, u32[]{:S(2)}) collective-permute-start(bf16[1024,256]{1,0:T(8,128)(2,1)} %shard_map.70.refs_0_), channel_id=1, source_target_pairs={{0,1},{1,0},{2,3},{3,2},{4,5},{5,4},{6,7},{7,6},{8,9},{9,8},{10,11... | collective-permute-start | bytes 1572872 | tf_op jit(solution)/shard_map/ppermute | solution.py:222
  69.4 1.9 %collective-permute-start.5 = (bf16[1024,256]{1,0:T(8,128)(2,1)}, bf16[1024,256]{1,0:T(8,128)(2,1)S(1)}, u32[]{:S(2)}, u32[]{:S(2)}) collective-permute-start(bf16[1024,256]{1,0:T(8,128)(2,1)} %shard_map.70.refs_0_), channel_id=1, source_target_pairs={{0,2},{1,3},{2,0},{3,1},{4,6},{5,7},{6,4},{7,5},{8,10},{9,11},{10,... | collective-permute-start | bytes 1572872 | tf_op jit(solution)/shard_map/ppermute | solution.py:222
  71.3 5.7 %collective-permute-start.6 = (bf16[1024,256]{1,0:T(8,128)(2,1)}, bf16[1024,256]{1,0:T(8,128)(2,1)S(1)}, u32[]{:S(2)}, u32[]{:S(2)}) collective-permute-start(bf16[1024,256]{1,0:T(8,128)(2,1)} %shard_map.70.refs_0_), channel_id=1, source_target_pairs={{0,3},{1,2},{2,1},{3,0},{4,7},{5,6},{6,5},{7,4},{8,11},{9,10},{10,... | collective-permute-start | bytes 1572872 | tf_op jit(solution)/shard_map/ppermute | solution.py:222
  77.1 3.9 %shard_map.66.before = bf16[128,256]{1,0:T(8,128)(2,1)} custom-call(s32[1]{0:T(128)} %bitcast.2.place, bf16[128,2048]{1,0:T(8,128)(2,1)} %bitcast.24, bf16[128,2048]{1,0:T(8,128)(2,1)} %collective-permute-done.other, bf16[4096,256]{1,0:T(8,128)(2,1)} %bitcast.16, bf16[4096,256]{1,0:T(8,128)(2,1)} %bitcast.18), custom_call_target="tpu_custom_call" | custom-call | flops 536870912 | bytes 5308420 | tf_op jit(solution)/shard_map/pallas_call | solution.py:195
  81.0 3.1 %shard_map.68 = bf16[256,256]{1,0:T(8,128)(2,1)S(1)} custom-call(bf16[128,256]{1,0:T(8,128)(2,1)} %shard_map.66.before, bf16[128,4096]{1,0:T(8,128)(2,1)S(1)} %bitcast.13, bf16[4096,256]{1,0:T(8,128)(2,1)} %bitcast.17, bf16[4096,256]{1,0:T(8,128)(2,1)} %bitcast.19), custom_call_target="tpu_custom_call" | custom-call | flops 536870912 | bytes 4194304 | tf_op jit(solution)/shard_map/pallas_call | solution.py:150
  84.1 12.5 %all-gather = bf16[1024,256]{1,0:T(8,128)(2,1)S(1)} all-gather(bf16[256,256]{1,0:T(8,128)(2,1)S(1)} %shard_map.68), channel_id=2, replica_groups={{0,4,8,12},{16,20,24,28},{32,36,40,44},{48,52,56,60},{1,5,9,13},{17,21,..., dimensions={0}, use_global_device_ids=true | all-gather | bytes 655360 | tf_op jit(solution)/shard_map/all_gather | solution.py:252
  96.5 3.4 %collective-permute-done.6.refs_3_ = bf16[1024,256]{1,0:T(8,128)(2,1)S(1)} collective-permute-done((bf16[1024,256]{1,0:T(8,128)(2,1)}, bf16[1024,256]{1,0:T(8,128)(2,1)S(1)}, u32[]{:S(2)}, u32[]{:S(2)}) %collective-permute-start.6) | collective-permute-done | bytes 524320 | tf_op jit(solution)/shard_map/ppermute | solution.py:222
  99.9 1.5 shard_map.71
  101.5 19.5 %all-to-all-start.2 = ((bf16[64,16,256]{2,1,0:T(8,128)(2,1)}), bf16[64,16,256]{2,1,0:T(8,128)(2,1)S(1)}, u32[]{:S(2)}, u32[]{:S(2)}) async-start(bf16[64,16,256]{2,1,0:T(8,128)(2,1)} %bitcast.11), calls=%async_computation.2 | async-start | bytes 1048576 | tf_op jit(solution)/shard_map/all_to_all | solution.py:263
  121.0 2.3 %shard_map.64 = (bf16[1024,64]{1,0:T(8,128)(2,1)}, bf16[1024,64]{1,0:T(8,128)(2,1)}) custom-call(s32[8,64]{1,0:T(8,128)} %bitcast.27, f32[8,64]{1,0:T(8,128)} %bitcast.28), custom_call_target="tpu_custom_call" | custom-call | flops 8388608 | bytes 266240 | tf_op jit(solution)/shard_map/pallas_call | solution.py:195
  123.3 31.4 %all-to-all-done.2 = bf16[64,16,256]{2,1,0:T(8,128)(2,1)S(1)} async-done(((bf16[64,16,256]{2,1,0:T(8,128)(2,1)}), bf16[64,16,256]{2,1,0:T(8,128)(2,1)S(1)}, u32[]{:S(2)}, u32[]{:S(2)}) %all-to-all-start.2) | async-done | bytes 524320 | tf_op jit(solution)/shard_map/all_to_all | solution.py:263
  154.7 0.9 copy-done.1
  155.6 0.9 copy-done.2
  156.6 1.0 shard_map.72
  (14 shorter events, 0.0 us)
Async XLA Ops:
  2.3 34.8 %all-to-all-start = ((bf16[16,8,2048]{2,1,0:T(8,128)(2,1)}), bf16[16,8,2048]{2,1,0:T(8,128)(2,1)S(1)}, u32[]{:S(2)}, u32[]{:S(2)}) async-start(bf16[16,8,2048]{2,1,0:T(8,128)(2,1)} %bitcast.22), calls=%async_computation | async-start | bytes 1048576 | tf_op jit(solution)/shard_map/all_to_all | solution.py:219
  37.0 6.6 %copy-start.4 = (bf16[16,8,2048]{2,1,0:T(8,128)(2,1)}, bf16[16,8,2048]{2,1,0:T(8,128)(2,1)S(1)}, u32[]{:S(2)}) copy-start(bf16[16,8,2048]{2,1,0:T(8,128)(2,1)S(1)} %all-to-all-done) | copy-start | bytes 1572868
  37.0 44.0 %all-to-all-start.1 = ((bf16[16,8,4096]{2,1,0:T(8,128)(2,1)}), bf16[16,8,4096]{2,1,0:T(8,128)(2,1)S(1)}, u32[]{:S(2)}, u32[]{:S(2)}) async-start(bf16[16,8,4096]{2,1,0:T(8,128)(2,1)} %bitcast.20), calls=%async_computation.1 | async-start | bytes 2097152 | tf_op jit(solution)/shard_map/all_to_all | solution.py:219
  40.6 36.5 %collective-permute-start = (bf16[128,2048]{1,0:T(8,128)(2,1)S(1)}, bf16[128,2048]{1,0:T(8,128)(2,1)}, u32[]{:S(2)}, u32[]{:S(2)}) collective-permute-start(bf16[128,2048]{1,0:T(8,128)(2,1)S(1)} %bitcast.23), channel_id=1, source_target_pairs={{0,4},{4,0},{8,12},{12,8},{16,20},{20,16},{24,28},{28,24},{32,36},... | collective-permute-start | bytes 1572872 | tf_op jit(solution)/shard_map/ppermute | solution.py:222
  43.7 0.7 copy-start.3
  44.4 20.5 %collective-permute-start.1 = (bf16[256,256]{1,0:T(8,128)(2,1)S(1)}, bf16[256,256]{1,0:T(8,128)(2,1)S(1)}, u32[]{:S(2)}, u32[]{:S(2)}) collective-permute-start(bf16[256,256]{1,0:T(8,128)(2,1)S(1)} %get-tuple-element.14), channel_id=1, source_target_pairs={{0,4},{4,0},{8,12},{12,8},{16,20},{20,16},{24,28},{28,24},{32,36},... | collective-permute-start | bytes 393224 | tf_op jit(solution)/shard_map/ppermute | solution.py:222
  47.7 17.1 %collective-permute-start.2 = (bf16[256,256]{1,0:T(8,128)(2,1)S(1)}, bf16[256,256]{1,0:T(8,128)(2,1)S(1)}, u32[]{:S(2)}, u32[]{:S(2)}) collective-permute-start(bf16[256,256]{1,0:T(8,128)(2,1)S(1)} %get-tuple-element.15), channel_id=1, source_target_pairs={{0,8},{4,12},{8,0},{12,4},{16,24},{20,28},{24,16},{28,20},{32,40},... | collective-permute-start | bytes 393224 | tf_op jit(solution)/shard_map/ppermute | solution.py:222
  49.6 15.2 %collective-permute-start.3 = (bf16[256,256]{1,0:T(8,128)(2,1)S(1)}, bf16[256,256]{1,0:T(8,128)(2,1)S(1)}, u32[]{:S(2)}, u32[]{:S(2)}) collective-permute-start(bf16[256,256]{1,0:T(8,128)(2,1)S(1)} %get-tuple-element.16), channel_id=1, source_target_pairs={{0,12},{4,8},{8,4},{12,0},{16,28},{20,24},{24,20},{28,16},{32,44},... | collective-permute-start | bytes 393224 | tf_op jit(solution)/shard_map/ppermute | solution.py:222
  64.8 0.7 copy-start.5
  64.8 0.7 copy-start.6
  64.8 0.7 copy-start.7
  67.5 29.1 %collective-permute-start.4 = (bf16[1024,256]{1,0:T(8,128)(2,1)}, bf16[1024,256]{1,0:T(8,128)(2,1)S(1)}, u32[]{:S(2)}, u32[]{:S(2)}) collective-permute-start(bf16[1024,256]{1,0:T(8,128)(2,1)} %shard_map.70.refs_0_), channel_id=1, source_target_pairs={{0,1},{1,0},{2,3},{3,2},{4,5},{5,4},{6,7},{7,6},{8,9},{9,8},{10,11... | collective-permute-start | bytes 1572872 | tf_op jit(solution)/shard_map/ppermute | solution.py:222
  69.4 27.1 %collective-permute-start.5 = (bf16[1024,256]{1,0:T(8,128)(2,1)}, bf16[1024,256]{1,0:T(8,128)(2,1)S(1)}, u32[]{:S(2)}, u32[]{:S(2)}) collective-permute-start(bf16[1024,256]{1,0:T(8,128)(2,1)} %shard_map.70.refs_0_), channel_id=1, source_target_pairs={{0,2},{1,3},{2,0},{3,1},{4,6},{5,7},{6,4},{7,5},{8,10},{9,11},{10,... | collective-permute-start | bytes 1572872 | tf_op jit(solution)/shard_map/ppermute | solution.py:222
  71.3 28.6 %collective-permute-start.6 = (bf16[1024,256]{1,0:T(8,128)(2,1)}, bf16[1024,256]{1,0:T(8,128)(2,1)S(1)}, u32[]{:S(2)}, u32[]{:S(2)}) collective-permute-start(bf16[1024,256]{1,0:T(8,128)(2,1)} %shard_map.70.refs_0_), channel_id=1, source_target_pairs={{0,3},{1,2},{2,1},{3,0},{4,7},{5,6},{6,5},{7,4},{8,11},{9,10},{10,... | collective-permute-start | bytes 1572872 | tf_op jit(solution)/shard_map/ppermute | solution.py:222
  81.0 18.9 %copy-start = (bf16[1024,256]{1,0:T(8,128)(2,1)S(1)}, bf16[1024,256]{1,0:T(8,128)(2,1)}, u32[]{:S(2)}) copy-start(bf16[1024,256]{1,0:T(8,128)(2,1)} %shard_map.70.refs_0_) | copy-start | bytes 1572868
  101.5 53.2 %all-to-all-start.2 = ((bf16[64,16,256]{2,1,0:T(8,128)(2,1)}), bf16[64,16,256]{2,1,0:T(8,128)(2,1)S(1)}, u32[]{:S(2)}, u32[]{:S(2)}) async-start(bf16[64,16,256]{2,1,0:T(8,128)(2,1)} %bitcast.11), calls=%async_computation.2 | async-start | bytes 1048576 | tf_op jit(solution)/shard_map/all_to_all | solution.py:263
  154.7 1.0 copy-start.1
  155.6 0.9 copy-start.2
